TPU v7x, 256 devices: a whole 4x4x8 slice. The times are simulated.
256 devices in a mesh: gx: 16 (over z, y_lo), gy: 16 (over y_hi, x, core).
Axes of the slice: x: 4, y: 4 (y_hi: 2, y_lo: 2; y = y_hi * 2 + y_lo), z: 8, core: 2. Of those that a mesh axis runs over, the one named last changes fastest.
Arguments:
- psi: float32 [64, 128, 4096], P(None, 'gx', 'gy'), may hold values from -500 to 500
- potential: float32 [128, 4096], P('gx', 'gy'), may hold values from -2 to 0
Outputs:
- orbitals: float32 [64, 128, 4096], P(None, 'gx', 'gy')
All inputs are finite; a program needn't handle non-finite values.
Results may differ from a plain program's by a relative error of at most 0.0003.
Values sent between devices are 32-bit elements; how exact they have to be, the bound alone decides.
No kernel may reach another device: no remote copies, remote signals or barrier semaphores. Data moves between devices by JAX's collectives and lax.ppermute only.
A program may use at most 64 MiB of HBM per device.

v0:
```python
import jax
import jax.numpy as jnp
from jax import lax
from jax.sharding import PartitionSpec as P

NZ = 64


COEFS = (-205.0 / 72.0, 8.0 / 5.0, -1.0 / 5.0, 8.0 / 315.0, -1.0 / 560.0)
CENTER = 6.5
HALF_WIDTH = 5.5


def padded(array, sides, width):
    for axis, dim in sides:
        size, length = (lax.axis_size(axis), array.shape[dim])
        up = [(i, (i + 1) % size) for i in range(size)]
        down = [(j, i) for i, j in up]
        last = lax.slice_in_dim(array, length - width, length, axis=dim)
        first = lax.slice_in_dim(array, 0, width, axis=dim)
        before = lax.ppermute(last, axis, up)
        after = lax.ppermute(first, axis, down)
        array = jnp.concatenate([before, array, after], axis=dim)
    return array


def along_third(field, depth_index):
    laplace = 3.0 * COEFS[0] * field
    for distance in range(1, 5):
        forward = jnp.where(
            depth_index < NZ - distance,
            jnp.roll(field, -distance, 2),
            jnp.roll(field, NZ - distance, 2),
        )
        behind = jnp.where(
            depth_index >= distance, jnp.roll(field, distance, 2), jnp.roll(field, distance - NZ, 2)
        )
        laplace = laplace + COEFS[distance] * (forward + behind)
    return laplace


def hamiltonian(field, field_pot, depth_index):
    row_count = field.shape[1]
    lane_count = field.shape[2]
    padded_x = padded(field, (("gx", 1),), 4)
    laplace = along_third(field, depth_index)
    padded_y = padded(field, (("gy", 2),), 4 * NZ)
    for distance in range(1, 5):
        laplace = laplace + COEFS[distance] * (
            padded_x[:, 4 + distance : 4 + distance + row_count]
            + padded_x[:, 4 - distance : 4 - distance + row_count]
        )
        ahead_start = (4 + distance) * NZ
        back_start = (4 - distance) * NZ
        laplace = laplace + COEFS[distance] * (
            padded_y[:, :, ahead_start : ahead_start + lane_count]
            + padded_y[:, :, back_start : back_start + lane_count]
        )
    return -0.5 * laplace + field_pot * field


def orthonormal(matrix, ncount):
    local_gram = jnp.dot(matrix, matrix.T, precision=lax.Precision.HIGHEST) / ncount
    total_gram = lax.psum(local_gram, ("gx", "gy"))
    lower_factor = jnp.linalg.cholesky(total_gram)
    return lax.linalg.triangular_solve(lower_factor, matrix, left_side=True, lower=True)


def on_device(psi, potential):
    orbit_count = psi.shape[0]
    row_count = psi.shape[1]
    lane_count = psi.shape[2]
    field_pot = potential.reshape(1, row_count, lane_count)
    depth_index = lax.broadcasted_iota(jnp.int32, (1, 1, lane_count), 2) % NZ
    level_one = (hamiltonian(psi, field_pot, depth_index) - CENTER * psi) / HALF_WIDTH
    second = (
        2.0 * (hamiltonian(level_one, field_pot, depth_index) - CENTER * level_one) / HALF_WIDTH
        - psi
    )
    filtered = (
        2.0 * (hamiltonian(second, field_pot, depth_index) - CENTER * second) / HALF_WIDTH
        - level_one
    )
    matrix = filtered.reshape(orbit_count, row_count * lane_count)
    ncount = float(row_count * lane_count * lax.axis_size("gx") * lax.axis_size("gy"))
    first_pass = orthonormal(matrix, ncount)
    final_pass = orthonormal(first_pass, ncount)
    return final_pass.reshape(orbit_count, row_count, lane_count)


def solution(mesh):
    in_specs = (P(None, "gx", "gy"), P("gx", "gy"))
    out_specs = P(None, "gx", "gy")
    return jax.shard_map(
        on_device, mesh=mesh, in_specs=in_specs, out_specs=out_specs, check_vma=False
    )
```

profile of v0, /device:TPU:6, one launch (start us, length us, event | category | flops | bytes accessed | tf_op | source)
XLA Modules:
  0.0 261.0 jit_solution(8503108184494606311)
XLA Ops:
  0.0 1.7 collective-permute-start.2
  1.7 1.3 fusion.198
  3.0 6.9 %collective-permute-start = (f32[64,4,256]{2,1,0:T(4,128)S(1)}, f32[64,4,256]{2,1,0:T(4,128)S(1)}, u32[]{:S(2)}, u32[]{:S(2)}) collective-permute-start(f32[64,4,256]{2,1,0:T(4,128)S(1)} %get-tuple-element.112), channel_id=1, source_target_pairs={{16,0},{32,16},{48,32},{64,48},{80,64},{96,80},{112,96},{128,112},... | collective-permute-start | bytes 786440 | tf_op jit(solution)/shard_map/ppermute | solution.py:22
  13.6 9.5 %collective-permute-done = f32[64,4,256]{2,1,0:T(4,128)S(1)} collective-permute-done((f32[64,4,256]{2,1,0:T(4,128)S(1)}, f32[64,4,256]{2,1,0:T(4,128)S(1)}, u32[]{:S(2)}, u32[]{:S(2)}) %collective-permute-start) | collective-permute-done | bytes 262176 | tf_op jit(solution)/shard_map/ppermute | solution.py:22
  23.3 3.4 %broadcast_multiply_fusion = (f32[64,8,256]{2,1,0:T(8,128)S(1)}, f32[64,8,256]{2,1,0:T(8,128)S(1)}) fusion(f32[64,8,256]{2,1,0:T(8,128)S(1)} %copy-done, f32[8,256]{1,0:T(8,128)S(1)} %copy-done.1, f32[64,8,256]{2,1,0:T(8,128)S(1)} %collective-permute-done.2, f32[64,8,256]{2,1,0:T(8,128)S(1)} %collective-permute-done.3, ...), kind=kLoop, calls=%fused_computation.221 | loop fusion | flops 9306112 | bytes 16525312 | tf_op jit(solution)/shard_map/div | solution.py:75
  29.7 7.3 %collective-permute-start.4 = (f32[64,4,256]{2,1,0:T(4,128)S(1)}, f32[64,4,256]{2,1,0:T(4,128)S(1)}, u32[]{:S(2)}, u32[]{:S(2)}) collective-permute-start(f32[64,4,256]{2,1,0:T(4,128)S(1)} %get-tuple-element.75), channel_id=1, source_target_pairs={{16,0},{32,16},{48,32},{64,48},{80,64},{96,80},{112,96},{128,112},... | collective-permute-start | bytes 786440 | tf_op jit(solution)/shard_map/ppermute | solution.py:22
  37.4 4.9 %collective-permute-done.4 = f32[64,4,256]{2,1,0:T(4,128)S(1)} collective-permute-done((f32[64,4,256]{2,1,0:T(4,128)S(1)}, f32[64,4,256]{2,1,0:T(4,128)S(1)}, u32[]{:S(2)}, u32[]{:S(2)}) %collective-permute-start.4) | collective-permute-done | bytes 262176 | tf_op jit(solution)/shard_map/ppermute | solution.py:22
  42.3 8.5 %collective-permute-done.5 = f32[64,4,256]{2,1,0:T(4,128)S(1)} collective-permute-done((f32[64,4,256]{2,1,0:T(4,128)S(1)}, f32[64,4,256]{2,1,0:T(4,128)S(1)}, u32[]{:S(2)}, u32[]{:S(2)}) %collective-permute-start.5) | collective-permute-done | bytes 262176 | tf_op jit(solution)/shard_map/ppermute | solution.py:21
  50.8 3.7 %fusion.33 = f32[64,8,256]{2,1,0:T(8,128)S(1)} fusion(f32[64,8,256]{2,1,0:T(8,128)S(1)} %copy-done, f32[64,8,256]{2,1,0:T(8,128)S(1)} %collective-permute-done.7, f32[64,8,256]{2,1,0:T(8,128)S(1)} %get-tuple-element.6, f32[64,8,256]{2,1,0:T(8,128)S(1)} %collective-permute-done.6, f32[64,4,256]{2,1,0:T(4,128)S(1)} %collective-permute-done.5, ...), kind=kLoop, calls=%fused_computation.81 | loop fusion | flops 10747904 | bytes 12068864 | tf_op jit(solution)/shard_map/sub | solution.py:77
  57.5 5.7 %collective-permute-start.8 = (f32[64,4,256]{2,1,0:T(4,128)S(1)}, f32[64,4,256]{2,1,0:T(4,128)S(1)}, u32[]{:S(2)}, u32[]{:S(2)}) collective-permute-start(f32[64,4,256]{2,1,0:T(4,128)S(1)} %get-tuple-element.41), channel_id=1, source_target_pairs={{16,0},{32,16},{48,32},{64,48},{80,64},{96,80},{112,96},{128,112},... | collective-permute-start | bytes 786440 | tf_op jit(solution)/shard_map/ppermute | solution.py:22
  63.6 13.4 %collective-permute-done.8 = f32[64,4,256]{2,1,0:T(4,128)S(1)} collective-permute-done((f32[64,4,256]{2,1,0:T(4,128)S(1)}, f32[64,4,256]{2,1,0:T(4,128)S(1)}, u32[]{:S(2)}, u32[]{:S(2)}) %collective-permute-start.8) | collective-permute-done | bytes 262176 | tf_op jit(solution)/shard_map/ppermute | solution.py:22
  77.0 0.8 collective-permute-done.9
  77.8 3.7 %fusion.13 = f32[64,8,256]{2,1,0:T(8,128)S(1)} fusion(f32[64,8,256]{2,1,0:T(8,128)S(1)} %collective-permute-done.11, f32[64,8,256]{2,1,0:T(8,128)S(1)} %fusion.33, f32[64,8,256]{2,1,0:T(8,128)S(1)} %collective-permute-done.10, f32[64,4,256]{2,1,0:T(4,128)S(1)} %collective-permute-done.9, f32[64,4,256]{2,1,0:T(4,128)S(1)} %collective-permute-done.8, ...), kind=kLoop, calls=%fused_computation.61 | loop fusion | flops 10878976 | bytes 11544576 | tf_op jit(solution)/shard_map/sub | solution.py:81
  81.5 0.7 fusion
  82.3 77.7 %psum.14 = f32[64,64]{0,1:T(8,128)S(1)} all-reduce(f32[64,64]{0,1:T(8,128)S(1)} %fusion), channel_id=1, replica_groups=mesh['gx'=16,'gy'=16] {'gx','gy'}, use_global_device_ids=true, to_apply=%region_0.1 | all-reduce | flops 4096 | bytes 32768 | tf_op jit(solution)/shard_map/psum | solution.py:64
  160.0 5.8 %cholesky.44 = f32[64,64]{1,0:T(8,128)S(1)} custom-call(f32[64,64]{1,0:T(8,128)S(1)} %fusion.144), custom_call_target="Cholesky" | custom-call | tf_op jit(solution)/shard_map/jit(cholesky)/cholesky | solution.py:65
  165.9 0.6 compare_reduce_fusion.1
  166.6 0.7 fusion.137
  167.2 4.9 %custom-call.6 = f32[1,64,64]{1,2,0:T(8,128)S(1)} custom-call(f32[1,64,64]{2,1,0:T(8,128)S(1)} %fusion.137), custom_call_target="InvertDiagBlocksLowerTriangular" | custom-call | tf_op jit(solution)/shard_map/triangular_solve/custom-call.0 | solution.py:66
  173.5 73.8 %psum.15 = f32[64,64]{0,1:T(8,128)S(1)} all-reduce(f32[64,64]{0,1:T(8,128)S(1)} %convolution_multiply_fusion), channel_id=1, replica_groups=mesh['gx'=16,'gy'=16] {'gx','gy'}, use_global_device_ids=true, to_apply=%region_3.6 | all-reduce | flops 4096 | bytes 32768 | tf_op jit(solution)/shard_map/psum | solution.py:64
  247.4 5.8 %cholesky.55 = f32[64,64]{1,0:T(8,128)S(1)} custom-call(f32[64,64]{1,0:T(8,128)S(1)} %fusion.141), custom_call_target="Cholesky" | custom-call | tf_op jit(solution)/shard_map/jit(cholesky)/cholesky | solution.py:65
  253.9 0.7 fusion.138
  254.5 4.9 %custom-call.7 = f32[1,64,64]{1,2,0:T(8,128)S(1)} custom-call(f32[1,64,64]{2,1,0:T(8,128)S(1)} %fusion.138), custom_call_target="InvertDiagBlocksLowerTriangular" | custom-call | tf_op jit(solution)/shard_map/triangular_solve/custom-call.0 | solution.py:66
  260.1 1.0 copy.13
  (89 shorter events, 13.2 us)
Async XLA Ops:
  0.0 10.0 %copy-start = (f32[64,8,256]{2,1,0:T(8,128)S(1)}, f32[64,8,256]{2,1,0:T(8,128)}, u32[]{:S(2)}) copy-start(f32[64,8,256]{2,1,0:T(8,128)} %param.5) | copy-start | bytes 1572868
  0.0 13.3 %collective-permute-start.3 = (f32[64,8,256]{2,1,0:T(8,128)}, f32[64,8,256]{2,1,0:T(8,128)S(1)}, u32[]{:S(2)}, u32[]{:S(2)}) collective-permute-start(f32[64,8,256]{2,1,0:T(8,128)} %param.5), channel_id=1, source_target_pairs={{0,1},{1,2},{2,3},{3,4},{4,5},{5,6},{6,7},{7,8},{8,9},{9,10},{10,1... | collective-permute-start | bytes 1572872 | tf_op jit(solution)/shard_map/ppermute | solution.py:21
  0.0 23.2 %collective-permute-start.2 = (f32[64,8,256]{2,1,0:T(8,128)}, f32[64,8,256]{2,1,0:T(8,128)S(1)}, u32[]{:S(2)}, u32[]{:S(2)}) collective-permute-start(f32[64,8,256]{2,1,0:T(8,128)} %param.5), channel_id=1, source_target_pairs={{1,0},{2,1},{3,2},{4,3},{5,4},{6,5},{7,6},{8,7},{9,8},{10,9},{11,1... | collective-permute-start | bytes 1572872 | tf_op jit(solution)/shard_map/ppermute | solution.py:22
  3.0 20.0 %collective-permute-start = (f32[64,4,256]{2,1,0:T(4,128)S(1)}, f32[64,4,256]{2,1,0:T(4,128)S(1)}, u32[]{:S(2)}, u32[]{:S(2)}) collective-permute-start(f32[64,4,256]{2,1,0:T(4,128)S(1)} %get-tuple-element.112), channel_id=1, source_target_pairs={{16,0},{32,16},{48,32},{64,48},{80,64},{96,80},{112,96},{128,112},... | collective-permute-start | bytes 786440 | tf_op jit(solution)/shard_map/ppermute | solution.py:22
  10.0 13.3 %collective-permute-start.1 = (f32[64,4,256]{2,1,0:T(4,128)S(1)}, f32[64,4,256]{2,1,0:T(4,128)S(1)}, u32[]{:S(2)}, u32[]{:S(2)}) collective-permute-start(f32[64,4,256]{2,1,0:T(4,128)S(1)} %get-tuple-element.113), channel_id=1, source_target_pairs={{0,16},{16,32},{32,48},{48,64},{64,80},{80,96},{96,112},{112,128},... | collective-permute-start | bytes 786440 | tf_op jit(solution)/shard_map/ppermute | solution.py:21
  12.4 0.7 copy-start.1
  29.1 21.7 %collective-permute-start.6 = (f32[64,8,256]{2,1,0:T(8,128)S(1)}, f32[64,8,256]{2,1,0:T(8,128)S(1)}, u32[]{:S(2)}, u32[]{:S(2)}) collective-permute-start(f32[64,8,256]{2,1,0:T(8,128)S(1)} %get-tuple-element.6), channel_id=1, source_target_pairs={{1,0},{2,1},{3,2},{4,3},{5,4},{6,5},{7,6},{8,7},{9,8},{10,9},{11,1... | collective-permute-start | bytes 1572872 | tf_op jit(solution)/shard_map/ppermute | solution.py:22
  29.2 21.6 %collective-permute-start.7 = (f32[64,8,256]{2,1,0:T(8,128)S(1)}, f32[64,8,256]{2,1,0:T(8,128)S(1)}, u32[]{:S(2)}, u32[]{:S(2)}) collective-permute-start(f32[64,8,256]{2,1,0:T(8,128)S(1)} %get-tuple-element.6), channel_id=1, source_target_pairs={{0,1},{1,2},{2,3},{3,4},{4,5},{5,6},{6,7},{7,8},{8,9},{9,10},{10,1... | collective-permute-start | bytes 1572872 | tf_op jit(solution)/shard_map/ppermute | solution.py:21
  29.7 12.6 %collective-permute-start.4 = (f32[64,4,256]{2,1,0:T(4,128)S(1)}, f32[64,4,256]{2,1,0:T(4,128)S(1)}, u32[]{:S(2)}, u32[]{:S(2)}) collective-permute-start(f32[64,4,256]{2,1,0:T(4,128)S(1)} %get-tuple-element.75), channel_id=1, source_target_pairs={{16,0},{32,16},{48,32},{64,48},{80,64},{96,80},{112,96},{128,112},... | collective-permute-start | bytes 786440 | tf_op jit(solution)/shard_map/ppermute | solution.py:22
  37.0 13.8 %collective-permute-start.5 = (f32[64,4,256]{2,1,0:T(4,128)S(1)}, f32[64,4,256]{2,1,0:T(4,128)S(1)}, u32[]{:S(2)}, u32[]{:S(2)}) collective-permute-start(f32[64,4,256]{2,1,0:T(4,128)S(1)} %get-tuple-element.76), channel_id=1, source_target_pairs={{0,16},{16,32},{32,48},{48,64},{64,80},{80,96},{96,112},{112,128},... | collective-permute-start | bytes 786440 | tf_op jit(solution)/shard_map/ppermute | solution.py:21
  55.8 21.9 %collective-permute-start.10 = (f32[64,8,256]{2,1,0:T(8,128)S(1)}, f32[64,8,256]{2,1,0:T(8,128)S(1)}, u32[]{:S(2)}, u32[]{:S(2)}) collective-permute-start(f32[64,8,256]{2,1,0:T(8,128)S(1)} %fusion.33), channel_id=1, source_target_pairs={{1,0},{2,1},{3,2},{4,3},{5,4},{6,5},{7,6},{8,7},{9,8},{10,9},{11,1... | collective-permute-start | bytes 1572872 | tf_op jit(solution)/shard_map/ppermute | solution.py:22
  55.9 21.9 %collective-permute-start.11 = (f32[64,8,256]{2,1,0:T(8,128)S(1)}, f32[64,8,256]{2,1,0:T(8,128)S(1)}, u32[]{:S(2)}, u32[]{:S(2)}) collective-permute-start(f32[64,8,256]{2,1,0:T(8,128)S(1)} %fusion.33), channel_id=1, source_target_pairs={{0,1},{1,2},{2,3},{3,4},{4,5},{5,6},{6,7},{7,8},{8,9},{9,10},{10,1... | collective-permute-start | bytes 1572872 | tf_op jit(solution)/shard_map/ppermute | solution.py:21
  57.5 19.5 %collective-permute-start.8 = (f32[64,4,256]{2,1,0:T(4,128)S(1)}, f32[64,4,256]{2,1,0:T(4,128)S(1)}, u32[]{:S(2)}, u32[]{:S(2)}) collective-permute-start(f32[64,4,256]{2,1,0:T(4,128)S(1)} %get-tuple-element.41), channel_id=1, source_target_pairs={{16,0},{32,16},{48,32},{64,48},{80,64},{96,80},{112,96},{128,112},... | collective-permute-start | bytes 786440 | tf_op jit(solution)/shard_map/ppermute | solution.py:22
  63.2 14.6 %collective-permute-start.9 = (f32[64,4,256]{2,1,0:T(4,128)S(1)}, f32[64,4,256]{2,1,0:T(4,128)S(1)}, u32[]{:S(2)}, u32[]{:S(2)}) collective-permute-start(f32[64,4,256]{2,1,0:T(4,128)S(1)} %get-tuple-element.42), channel_id=1, source_target_pairs={{0,16},{16,32},{32,48},{48,64},{64,80},{80,96},{96,112},{112,128},... | collective-permute-start | bytes 786440 | tf_op jit(solution)/shard_map/ppermute | solution.py:21
where the time goes:
time: 263 us; the launch traced here: 261 us
  blocking collectives  151 us (57%)
  waiting for transfers between devices  37.1 us (14%)
  other arithmetic  35.1 us (13%)
  starting transfers between devices  22.8 us (9%)
  local copies, waits for them, and re-layouts  11.6 us (4%)
    psum x2, blocking collectives, orthonormal(): total_gram = lax.psum(local_gram, ('gx', 'gy'))  151 us
    ppermute x6, waiting for transfers between devices, padded(): after = lax.ppermute(first, axis, down)  27.8 us
    ppermute x6, starting transfers between devices, padded(): after = lax.ppermute(first, axis, down)  21.8 us
    another operation x6, other arithmetic, orthonormal(): lower_factor = jnp.linalg.cholesky(total_gram)  13 us
    another operation x4, other arithmetic, orthonormal(): lax.linalg.triangular_solve(lower_factor, matrix, left_side=True, lower=T...  11.1 us
    ppermute x6, waiting for transfers between devices, padded(): before = lax.ppermute(last, axis, up)  9.31 us
  transfers between devices with their start and end apart: 12, of which 5 were waited for; matrix products, arithmetic and copies ran while one was open for 2% of the time, Pallas kernels for 0%

commit v1 on v0

--- a/solution.py
+++ b/solution.py
@@ -1,6 +1,11 @@
+import functools
+import math
+
 import jax
 import jax.numpy as jnp
 from jax import lax
+from jax.experimental import pallas as pl
+from jax.experimental.pallas import tpu as pltpu
 from jax.sharding import PartitionSpec as P
 
 NZ = 64
@@ -9,6 +14,8 @@
 COEFS = (-205.0 / 72.0, 8.0 / 5.0, -1.0 / 5.0, 8.0 / 315.0, -1.0 / 560.0)
 CENTER = 6.5
 HALF_WIDTH = 5.5
+VMEM = pl.BlockSpec(memory_space=pltpu.VMEM)
+NT = (((1,), (1,)), ((), ()))
 
 
 def padded(array, sides, width):
@@ -59,17 +66,168 @@
     return -0.5 * laplace + field_pot * field
 
 
-def orthonormal(matrix, ncount):
-    local_gram = jnp.dot(matrix, matrix.T, precision=lax.Precision.HIGHEST) / ncount
-    total_gram = lax.psum(local_gram, ("gx", "gy"))
-    lower_factor = jnp.linalg.cholesky(total_gram)
-    return lax.linalg.triangular_solve(lower_factor, matrix, left_side=True, lower=True)
+def two_sum(a, b):
+    s = a + b
+    t = s - a
+    return s, (a - (s - t)) + (b - t)
+
+
+def slices(hi, lo, count, shift, bits):
+    top = jnp.max(jnp.abs(hi), axis=1, keepdims=True)
+    rest, out = hi, []
+    for k in range(count):
+        if k == 3 and lo is not None:
+            rest = rest + lo
+        grain = top * (1.5 * 2.0 ** (shift - bits * k))
+        part = (rest + grain) - grain
+        rest = rest - part
+        out.append(part.astype(jnp.bfloat16))
+    return out, rest
+
+
+def gram_kernel(x_ref, o_ref):
+    m, rows, _ = x_ref.shape
+    top = jnp.max(jnp.abs(x_ref[:, 0, :]), axis=1, keepdims=True)
+    for r in range(1, rows):
+        top = jnp.maximum(top, jnp.max(jnp.abs(x_ref[:, r, :]), axis=1, keepdims=True))
+    g0 = top * (1.5 * 2.0**17)
+    g1 = top * (1.5 * 2.0**11)
+    total = None
+    for r in range(rows):
+        x = x_ref[:, r, :]
+        s0 = (x + g0) - g0
+        x = x - s0
+        s1 = (x + g1) - g1
+        x = x - s1
+        s2 = x.astype(jnp.bfloat16)
+        s3 = (x - s2.astype(jnp.float32)).astype(jnp.bfloat16)
+        z = jnp.concatenate([s0.astype(jnp.bfloat16), s1.astype(jnp.bfloat16), s2, s3], axis=0)
+        part = lax.dot_general(z, z, NT, preferred_element_type=jnp.float32)
+        total = part if total is None else total + part
+
+    def block(a, b):
+        return total[a * m : (a + 1) * m, b * m : (b + 1) * m]
+
+    hi, lo = two_sum(block(0, 0), block(0, 1) + block(1, 0))
+    small = block(0, 3) + block(3, 0) + block(1, 2) + block(2, 1)
+    small = small + (block(1, 3) + block(3, 1) + block(2, 2))
+    lo = lo + ((block(1, 1) + (block(0, 2) + block(2, 0))) + small)
+    hi, lo = two_sum(hi, lo)
+    h = m // 2
+    o_ref[:h, :] = jnp.concatenate([hi[:h], hi[h:]], axis=1)
+    o_ref[h:, :] = jnp.concatenate([lo[:h], lo[h:]], axis=1)
+
+
+def pair_add(a, b):
+    h = a.shape[0] // 2
+    s, e = two_sum(a[:h], b[:h])
+    s, e = two_sum(s, e + (a[h:] + b[h:]))
+    return jnp.concatenate([s, e], axis=0)
+
+
+def reduce_pairs(x):
+    def swapped(mask):
+        return lax.ppermute(x, ("gx", "gy"), [(i, i ^ mask) for i in range(256)])
+
+    for masks in ((1,), (2,), (6,), (16,), (24,), (32,), (64,), (128,)):
+        if len(masks) == 1:
+            x = pair_add(x, swapped(masks[0]))
+        else:
+            a, b, c = (swapped(mask) for mask in masks)
+            x = pair_add(pair_add(x, a), pair_add(b, c))
+    return x
+
+
+def lower_inverse(g):
+    m = g.shape[0]
+    lane = lax.broadcasted_iota(jnp.int32, (8, 2 * m), 1)
+    sub = lax.broadcasted_iota(jnp.int32, (8, 2 * m), 0)
+    tiles = []
+    for t in range(m // 8):
+        left = jnp.concatenate([g[8 * t : 8 * t + 8, :]] * 2, axis=1)
+        unit = jnp.where(lane == sub + (8 * t + m), 1.0, 0.0)
+        tiles.append(jnp.where(lane < m, left, unit))
+    for j in range(m):
+        own, s = divmod(j, 8)
+        row = jnp.broadcast_to(tiles[own][s : s + 1, :], (8, 2 * m))
+        pivot = jnp.broadcast_to(row[:, j : j + 1], (8, 2 * m))
+        row = row / pivot
+        for t in range(own, m // 8):
+            if t == own and s == 7:
+                continue
+            factor = jnp.broadcast_to(tiles[t][:, j : j + 1], (8, 2 * m))
+            if t == own:
+                factor = jnp.where(sub > s, factor, 0.0)
+            tiles[t] = tiles[t] - factor * row
+    out = []
+    for t in range(m // 8):
+        diag = jnp.sum(jnp.where(lane == sub + 8 * t, tiles[t], 0.0), axis=1, keepdims=True)
+        out.append(tiles[t][:, m:] * (1.0 / jnp.sqrt(diag)))
+    return jnp.concatenate(out, axis=0)
+
+
+def exact_product(a_parts, b_parts):
+    n, m = len(a_parts), a_parts[0].shape[0]
+    p = lax.dot_general(
+        jnp.concatenate(a_parts, axis=0),
+        jnp.concatenate(b_parts, axis=0),
+        NT,
+        preferred_element_type=jnp.float32,
+    )
+    hi = lo = None
+    for level in range(n):
+        term = None
+        for i in range(level + 1):
+            j = level - i
+            piece = p[i * m : (i + 1) * m, j * m : (j + 1) * m]
+            term = piece if term is None else term + piece
+        if hi is None:
+            hi, lo = term, jnp.zeros_like(term)
+        else:
+            hi, e = two_sum(hi, term)
+            lo = lo + e
+    return two_sum(hi, lo)
+
+
+def rotate_kernel(ncount, p_ref, x_ref, o_ref):
+    m, rows, _ = x_ref.shape
+    h = m // 2
+    hi, lo = p_ref[:h, :] * (1.0 / ncount), p_ref[h:, :] * (1.0 / ncount)
+    hi = jnp.concatenate([hi[:, :m], hi[:, m:]], axis=0)
+    lo = jnp.concatenate([lo[:, :m], lo[:, m:]], axis=0)
+    inverse1 = lower_inverse(hi)
+    w_parts, _ = slices(inverse1, None, 6, 16, 7)
+    g_parts, _ = slices(hi, lo, 6, 16, 7)
+    t_hi, t_lo = exact_product(w_parts, g_parts)
+    t_parts, _ = slices(t_hi, t_lo, 6, 16, 7)
+    gram2, _ = exact_product(t_parts, w_parts)
+    inverse2 = lower_inverse(gram2)
+    both = jnp.dot(inverse2, inverse1, precision=lax.Precision.HIGHEST)
+    for r in range(rows):
+        o_ref[:, r, :] = jnp.dot(both, x_ref[:, r, :], precision=lax.Precision.HIGHEST)
+
+
+def orthonormal(block, ncount):
+    m = block.shape[0]
+    local = pl.pallas_call(
+        gram_kernel,
+        out_shape=jax.ShapeDtypeStruct((m, 2 * m), jnp.float32),
+        in_specs=[VMEM],
+        out_specs=VMEM,
+        name="gram",
+    )(block)
+    total = reduce_pairs(local)
+    return pl.pallas_call(
+        functools.partial(rotate_kernel, ncount),
+        out_shape=jax.ShapeDtypeStruct(block.shape, jnp.float32),
+        in_specs=[VMEM, VMEM],
+        out_specs=VMEM,
+        name="rotate",
+    )(total, block)
 
 
 def on_device(psi, potential):
-    orbit_count = psi.shape[0]
-    row_count = psi.shape[1]
-    lane_count = psi.shape[2]
+    orbit_count, row_count, lane_count = psi.shape
     field_pot = potential.reshape(1, row_count, lane_count)
     depth_index = lax.broadcasted_iota(jnp.int32, (1, 1, lane_count), 2) % NZ
     level_one = (hamiltonian(psi, field_pot, depth_index) - CENTER * psi) / HALF_WIDTH
@@ -81,11 +239,8 @@
         2.0 * (hamiltonian(second, field_pot, depth_index) - CENTER * second) / HALF_WIDTH
         - level_one
     )
-    matrix = filtered.reshape(orbit_count, row_count * lane_count)
     ncount = float(row_count * lane_count * lax.axis_size("gx") * lax.axis_size("gy"))
-    first_pass = orthonormal(matrix, ncount)
-    final_pass = orthonormal(first_pass, ncount)
-    return final_pass.reshape(orbit_count, row_count, lane_count)
+    return orthonormal(filtered, ncount)
 
 
 def solution(mesh):

time: 263 us -> 146 us (0.56)
  blocking collectives: 151 us -> 0 us
  Pallas kernels: 0 us -> 23.7 us
  waiting for transfers between devices: 37.1 us -> 59.2 us
  other arithmetic: 35.1 us -> 13.1 us
  starting transfers between devices: 22.8 us -> 38 us
    psum x2 -> x0, blocking collectives: 151 us -> none  [orthonormal(): total_gram = lax.psum(local_gram, ('gx', 'gy'))]
    another operation x10 -> x0, other arithmetic: 24.1 us -> none  [the longest x6 13 us: orthonormal(): lower_factor = jnp.linalg.cholesky(total_gram)]
    pallas_call x0 -> x2, Pallas kernels: none -> 23.7 us  [the longest x1 20.8 us: orthonormal(): pl.pallas_call(functools.partial(rotate_kernel, ncount), out_shape=jax.Sh...]
    ppermute x0 -> x8, waiting for transfers between devices: none -> 22.1 us  [swapped(): return lax.ppermute(x, ('gx', 'gy'), [(i, i ^ mask) for i in range(256)])]
    ppermute x0 -> x8, starting transfers between devices: none -> 15.2 us  [swapped(): return lax.ppermute(x, ('gx', 'gy'), [(i, i ^ mask) for i in range(256)])]
  transfers between devices with their start and end apart: 12 -> 20, of which waited for: 5 -> 13; matrix products, arithmetic and copies ran while one was open for 2% -> 4% of each run, Pallas kernels for 0% -> 0%
where the time goes in v1:
time: 146 us; the launch traced here: 145 us
  waiting for transfers between devices  59.2 us (41%)
  starting transfers between devices  38 us (26%)
  Pallas kernels  23.7 us (16%)
  other arithmetic  13.1 us (9%)
  local copies, waits for them, and re-layouts  10.5 us (7%)
    ppermute x6, waiting for transfers between devices, padded(): after = lax.ppermute(first, axis, down)  27.8 us
    ppermute x8, waiting for transfers between devices, swapped(): return lax.ppermute(x, ('gx', 'gy'), [(i, i ^ mask) for i in range(256)])  22.1 us
    ppermute x6, starting transfers between devices, padded(): after = lax.ppermute(first, axis, down)  21.8 us
    pallas_call x1, Pallas kernels, orthonormal(): pl.pallas_call(functools.partial(rotate_kernel, ncount), out_shape=jax.Sh...  20.8 us
    ppermute x8, starting transfers between devices, swapped(): return lax.ppermute(x, ('gx', 'gy'), [(i, i ^ mask) for i in range(256)])  15.2 us
    ppermute x6, waiting for transfers between devices, padded(): before = lax.ppermute(last, axis, up)  9.31 us
    sub x1, other arithmetic, on_device(): 2.0 * (hamiltonian(second, field_pot, depth_index) - CENTER * second)  4.4 us
    sub x1, other arithmetic, on_device(): 2.0 * (hamiltonian(level_one, field_pot, depth_index) - CENTER * level_one)  3.72 us
  transfers between devices with their start and end apart: 20, of which 13 were waited for; matrix products, arithmetic and copies ran while one was open for 4% of the time, Pallas kernels for 0%

profile of v1, /device:TPU:6, one launch (start us, length us, event | category | flops | bytes accessed | tf_op | source)
XLA Modules:
  0.0 145.0 jit_solution(11358076684514646867)
XLA Ops:
  0.0 1.7 %collective-permute-start.2 = (f32[64,8,256]{2,1,0:T(8,128)}, f32[64,8,256]{2,1,0:T(8,128)S(1)}, u32[]{:S(2)}, u32[]{:S(2)}) collective-permute-start(f32[64,8,256]{2,1,0:T(8,128)} %param.2), channel_id=1, source_target_pairs={{1,0},{2,1},{3,2},{4,3},{5,4},{6,5},{7,6},{8,7},{9,8},{10,9},{11,1... | collective-permute-start | bytes 1572872 | tf_op jit(solution)/shard_map/ppermute | solution.py:29
  3.2 6.9 %collective-permute-start = (f32[64,4,256]{2,1,0:T(4,128)S(1)}, f32[64,4,256]{2,1,0:T(4,128)S(1)}, u32[]{:S(2)}, u32[]{:S(2)}) collective-permute-start(f32[64,4,256]{2,1,0:T(4,128)S(1)} %get-tuple-element.126), channel_id=1, source_target_pairs={{16,0},{32,16},{48,32},{64,48},{80,64},{96,80},{112,96},{128,112},... | collective-permute-start | bytes 786440 | tf_op jit(solution)/shard_map/ppermute | solution.py:29
  13.7 9.5 %collective-permute-done = f32[64,4,256]{2,1,0:T(4,128)S(1)} collective-permute-done((f32[64,4,256]{2,1,0:T(4,128)S(1)}, f32[64,4,256]{2,1,0:T(4,128)S(1)}, u32[]{:S(2)}, u32[]{:S(2)}) %collective-permute-start) | collective-permute-done | bytes 262176 | tf_op jit(solution)/shard_map/ppermute | solution.py:29
  23.4 3.4 %broadcast_multiply_fusion = (f32[64,8,256]{2,1,0:T(8,128)S(1)}, f32[64,8,256]{2,1,0:T(8,128)S(1)}) fusion(f32[64,8,256]{2,1,0:T(8,128)S(1)} %copy-done, f32[8,256]{1,0:T(8,128)S(1)} %copy-done.1, f32[64,8,256]{2,1,0:T(8,128)S(1)} %collective-permute-done.2, f32[64,8,256]{2,1,0:T(8,128)S(1)} %collective-permute-done.3, ...), kind=kLoop, calls=%fused_computation.217 | loop fusion | flops 9306112 | bytes 16525312 | tf_op jit(solution)/shard_map/div | solution.py:233
  29.8 7.3 %collective-permute-start.4 = (f32[64,4,256]{2,1,0:T(4,128)S(1)}, f32[64,4,256]{2,1,0:T(4,128)S(1)}, u32[]{:S(2)}, u32[]{:S(2)}) collective-permute-start(f32[64,4,256]{2,1,0:T(4,128)S(1)} %get-tuple-element.89), channel_id=1, source_target_pairs={{16,0},{32,16},{48,32},{64,48},{80,64},{96,80},{112,96},{128,112},... | collective-permute-start | bytes 786440 | tf_op jit(solution)/shard_map/ppermute | solution.py:29
  37.5 4.9 %collective-permute-done.4 = f32[64,4,256]{2,1,0:T(4,128)S(1)} collective-permute-done((f32[64,4,256]{2,1,0:T(4,128)S(1)}, f32[64,4,256]{2,1,0:T(4,128)S(1)}, u32[]{:S(2)}, u32[]{:S(2)}) %collective-permute-start.4) | collective-permute-done | bytes 262176 | tf_op jit(solution)/shard_map/ppermute | solution.py:29
  42.4 8.5 %collective-permute-done.5 = f32[64,4,256]{2,1,0:T(4,128)S(1)} collective-permute-done((f32[64,4,256]{2,1,0:T(4,128)S(1)}, f32[64,4,256]{2,1,0:T(4,128)S(1)}, u32[]{:S(2)}, u32[]{:S(2)}) %collective-permute-start.5) | collective-permute-done | bytes 262176 | tf_op jit(solution)/shard_map/ppermute | solution.py:28
  50.9 3.7 %fusion.32 = f32[64,8,256]{2,1,0:T(8,128)S(1)} fusion(f32[64,8,256]{2,1,0:T(8,128)S(1)} %copy-done, f32[64,8,256]{2,1,0:T(8,128)S(1)} %collective-permute-done.7, f32[64,8,256]{2,1,0:T(8,128)S(1)} %get-tuple-element.21, f32[64,8,256]{2,1,0:T(8,128)S(1)} %collective-permute-done.6, f32[64,4,256]{2,1,0:T(4,128)S(1)} %collective-permute-done.5, ...), kind=kLoop, calls=%fused_computation.78 | loop fusion | flops 10747904 | bytes 12068864 | tf_op jit(solution)/shard_map/sub | solution.py:235
  57.6 5.7 %collective-permute-start.8 = (f32[64,4,256]{2,1,0:T(4,128)S(1)}, f32[64,4,256]{2,1,0:T(4,128)S(1)}, u32[]{:S(2)}, u32[]{:S(2)}) collective-permute-start(f32[64,4,256]{2,1,0:T(4,128)S(1)} %get-tuple-element.55), channel_id=1, source_target_pairs={{16,0},{32,16},{48,32},{64,48},{80,64},{96,80},{112,96},{128,112},... | collective-permute-start | bytes 786440 | tf_op jit(solution)/shard_map/ppermute | solution.py:29
  63.7 13.4 %collective-permute-done.8 = f32[64,4,256]{2,1,0:T(4,128)S(1)} collective-permute-done((f32[64,4,256]{2,1,0:T(4,128)S(1)}, f32[64,4,256]{2,1,0:T(4,128)S(1)}, u32[]{:S(2)}, u32[]{:S(2)}) %collective-permute-start.8) | collective-permute-done | bytes 262176 | tf_op jit(solution)/shard_map/ppermute | solution.py:29
  77.9 4.4 %fusion.12.x_ref = f32[64,8,256]{2,1,0:T(8,128)} fusion(f32[64,8,256]{2,1,0:T(8,128)S(1)} %collective-permute-done.11, f32[64,8,256]{2,1,0:T(8,128)S(1)} %fusion.32, f32[64,8,256]{2,1,0:T(8,128)S(1)} %collective-permute-done.10, f32[64,4,256]{2,1,0:T(4,128)S(1)} %collective-permute-done.9, f32[64,4,256]{2,1,0:T(4,128)S(1)} %collective-permute-done.8, ...), kind=kLoop, calls=%fused_computation.58 | loop fusion | flops 10878976 | bytes 11544576 | tf_op jit(solution)/shard_map/sub | solution.py:239
  82.3 2.9 %gram.1 = f32[64,128]{1,0:T(8,128)} custom-call(f32[64,8,256]{2,1,0:T(8,128)} %fusion.12.x_ref), custom_call_target="tpu_custom_call" | custom-call | tf_op jit(solution)/shard_map/gram/pallas_call | solution.py:212
  87.8 3.9 %collective-permute-done.13 = f32[64,128]{1,0:T(8,128)S(1)} collective-permute-done((f32[64,128]{1,0:T(8,128)S(1)}, f32[64,128]{1,0:T(8,128)S(1)}, u32[]{:S(2)}, u32[]{:S(2)}) %collective-permute-start.13) | collective-permute-done | bytes 32800 | tf_op jit(solution)/shard_map/ppermute | solution.py:130
  93.2 3.8 %collective-permute-done.14 = f32[64,128]{1,0:T(8,128)S(1)} collective-permute-done((f32[64,128]{1,0:T(8,128)S(1)}, f32[64,128]{1,0:T(8,128)S(1)}, u32[]{:S(2)}, u32[]{:S(2)}) %collective-permute-start.14) | collective-permute-done | bytes 32800 | tf_op jit(solution)/shard_map/ppermute | solution.py:130
  96.9 2.5 %collective-permute-start.15 = (f32[64,128]{1,0:T(8,128)S(1)}, f32[64,128]{1,0:T(8,128)S(1)}, u32[]{:S(2)}, u32[]{:S(2)}) collective-permute-start(f32[64,128]{1,0:T(8,128)S(1)} %pad_maximum_fusion.11), channel_id=1, source_target_pairs={{0,16},{1,17},{2,18},{3,19},{4,20},{5,21},{6,22},{7,23},{8,24},{9,... | collective-permute-start | bytes 98312 | tf_op jit(solution)/shard_map/ppermute | solution.py:130
  99.5 1.9 %collective-permute-done.15 = f32[64,128]{1,0:T(8,128)S(1)} collective-permute-done((f32[64,128]{1,0:T(8,128)S(1)}, f32[64,128]{1,0:T(8,128)S(1)}, u32[]{:S(2)}, u32[]{:S(2)}) %collective-permute-start.15) | collective-permute-done | bytes 32800 | tf_op jit(solution)/shard_map/ppermute | solution.py:130
  101.4 2.2 %collective-permute-start.16 = (f32[64,128]{1,0:T(8,128)S(1)}, f32[64,128]{1,0:T(8,128)S(1)}, u32[]{:S(2)}, u32[]{:S(2)}) collective-permute-start(f32[64,128]{1,0:T(8,128)S(1)} %pad_maximum_fusion.12), channel_id=1, source_target_pairs={{0,24},{1,25},{2,26},{3,27},{4,28},{5,29},{6,30},{7,31},{8,16},{9,... | collective-permute-start | bytes 98312 | tf_op jit(solution)/shard_map/ppermute | solution.py:130
  103.6 3.0 %collective-permute-done.16 = f32[64,128]{1,0:T(8,128)S(1)} collective-permute-done((f32[64,128]{1,0:T(8,128)S(1)}, f32[64,128]{1,0:T(8,128)S(1)}, u32[]{:S(2)}, u32[]{:S(2)}) %collective-permute-start.16) | collective-permute-done | bytes 32800 | tf_op jit(solution)/shard_map/ppermute | solution.py:130
  107.4 3.3 %collective-permute-done.17 = f32[64,128]{1,0:T(8,128)S(1)} collective-permute-done((f32[64,128]{1,0:T(8,128)S(1)}, f32[64,128]{1,0:T(8,128)S(1)}, u32[]{:S(2)}, u32[]{:S(2)}) %collective-permute-start.17) | collective-permute-done | bytes 32800 | tf_op jit(solution)/shard_map/ppermute | solution.py:130
  110.7 2.0 %collective-permute-start.18 = (f32[64,128]{1,0:T(8,128)S(1)}, f32[64,128]{1,0:T(8,128)S(1)}, u32[]{:S(2)}, u32[]{:S(2)}) collective-permute-start(f32[64,128]{1,0:T(8,128)S(1)} %pad_maximum_fusion.14), channel_id=1, source_target_pairs={{0,64},{1,65},{2,66},{3,67},{4,68},{5,69},{6,70},{7,71},{8,72},{9,... | collective-permute-start | bytes 98312 | tf_op jit(solution)/shard_map/ppermute | solution.py:130
  112.6 2.9 %collective-permute-done.18 = f32[64,128]{1,0:T(8,128)S(1)} collective-permute-done((f32[64,128]{1,0:T(8,128)S(1)}, f32[64,128]{1,0:T(8,128)S(1)}, u32[]{:S(2)}, u32[]{:S(2)}) %collective-permute-start.18) | collective-permute-done | bytes 32800 | tf_op jit(solution)/shard_map/ppermute | solution.py:130
  115.6 5.7 %collective-permute-start.19 = (f32[64,128]{1,0:T(8,128)S(1)}, f32[64,128]{1,0:T(8,128)S(1)}, u32[]{:S(2)}, u32[]{:S(2)}) collective-permute-start(f32[64,128]{1,0:T(8,128)S(1)} %pad_maximum_fusion.15), channel_id=1, source_target_pairs={{0,128},{1,129},{2,130},{3,131},{4,132},{5,133},{6,134},{7,135},{8... | collective-permute-start | bytes 98312 | tf_op jit(solution)/shard_map/ppermute | solution.py:130
  121.3 2.2 %collective-permute-done.19 = f32[64,128]{1,0:T(8,128)S(1)} collective-permute-done((f32[64,128]{1,0:T(8,128)S(1)}, f32[64,128]{1,0:T(8,128)S(1)}, u32[]{:S(2)}, u32[]{:S(2)}) %collective-permute-start.19) | collective-permute-done | bytes 32800 | tf_op jit(solution)/shard_map/ppermute | solution.py:130
  124.1 20.8 %rotate.1 = f32[64,8,256]{2,1,0:T(8,128)} custom-call(f32[64,128]{1,0:T(8,128)} %pad_maximum_fusion.16.p_ref, f32[64,8,256]{2,1,0:T(8,128)} %fusion.12.x_ref), custom_call_target="tpu_custom_call" | custom-call | tf_op jit(solution)/shard_map/rotate/pallas_call | solution.py:220
  (101 shorter events, 18.0 us)
Async XLA Ops:
  0.0 10.1 %copy-start = (f32[64,8,256]{2,1,0:T(8,128)S(1)}, f32[64,8,256]{2,1,0:T(8,128)}, u32[]{:S(2)}) copy-start(f32[64,8,256]{2,1,0:T(8,128)} %param.2) | copy-start | bytes 1572868
  0.0 13.4 %collective-permute-start.3 = (f32[64,8,256]{2,1,0:T(8,128)}, f32[64,8,256]{2,1,0:T(8,128)S(1)}, u32[]{:S(2)}, u32[]{:S(2)}) collective-permute-start(f32[64,8,256]{2,1,0:T(8,128)} %param.2), channel_id=1, source_target_pairs={{0,1},{1,2},{2,3},{3,4},{4,5},{5,6},{6,7},{7,8},{8,9},{9,10},{10,1... | collective-permute-start | bytes 1572872 | tf_op jit(solution)/shard_map/ppermute | solution.py:28
  0.0 23.3 %collective-permute-start.2 = (f32[64,8,256]{2,1,0:T(8,128)}, f32[64,8,256]{2,1,0:T(8,128)S(1)}, u32[]{:S(2)}, u32[]{:S(2)}) collective-permute-start(f32[64,8,256]{2,1,0:T(8,128)} %param.2), channel_id=1, source_target_pairs={{1,0},{2,1},{3,2},{4,3},{5,4},{6,5},{7,6},{8,7},{9,8},{10,9},{11,1... | collective-permute-start | bytes 1572872 | tf_op jit(solution)/shard_map/ppermute | solution.py:29
  3.2 20.0 %collective-permute-start = (f32[64,4,256]{2,1,0:T(4,128)S(1)}, f32[64,4,256]{2,1,0:T(4,128)S(1)}, u32[]{:S(2)}, u32[]{:S(2)}) collective-permute-start(f32[64,4,256]{2,1,0:T(4,128)S(1)} %get-tuple-element.126), channel_id=1, source_target_pairs={{16,0},{32,16},{48,32},{64,48},{80,64},{96,80},{112,96},{128,112},... | collective-permute-start | bytes 786440 | tf_op jit(solution)/shard_map/ppermute | solution.py:29
  10.1 13.3 %collective-permute-start.1 = (f32[64,4,256]{2,1,0:T(4,128)S(1)}, f32[64,4,256]{2,1,0:T(4,128)S(1)}, u32[]{:S(2)}, u32[]{:S(2)}) collective-permute-start(f32[64,4,256]{2,1,0:T(4,128)S(1)} %get-tuple-element.127), channel_id=1, source_target_pairs={{0,16},{16,32},{32,48},{48,64},{64,80},{80,96},{96,112},{112,128},... | collective-permute-start | bytes 786440 | tf_op jit(solution)/shard_map/ppermute | solution.py:28
  12.5 0.7 copy-start.1
  29.2 21.7 %collective-permute-start.6 = (f32[64,8,256]{2,1,0:T(8,128)S(1)}, f32[64,8,256]{2,1,0:T(8,128)S(1)}, u32[]{:S(2)}, u32[]{:S(2)}) collective-permute-start(f32[64,8,256]{2,1,0:T(8,128)S(1)} %get-tuple-element.21), channel_id=1, source_target_pairs={{1,0},{2,1},{3,2},{4,3},{5,4},{6,5},{7,6},{8,7},{9,8},{10,9},{11,1... | collective-permute-start | bytes 1572872 | tf_op jit(solution)/shard_map/ppermute | solution.py:29
  29.3 21.6 %collective-permute-start.7 = (f32[64,8,256]{2,1,0:T(8,128)S(1)}, f32[64,8,256]{2,1,0:T(8,128)S(1)}, u32[]{:S(2)}, u32[]{:S(2)}) collective-permute-start(f32[64,8,256]{2,1,0:T(8,128)S(1)} %get-tuple-element.21), channel_id=1, source_target_pairs={{0,1},{1,2},{2,3},{3,4},{4,5},{5,6},{6,7},{7,8},{8,9},{9,10},{10,1... | collective-permute-start | bytes 1572872 | tf_op jit(solution)/shard_map/ppermute | solution.py:28
  29.8 12.6 %collective-permute-start.4 = (f32[64,4,256]{2,1,0:T(4,128)S(1)}, f32[64,4,256]{2,1,0:T(4,128)S(1)}, u32[]{:S(2)}, u32[]{:S(2)}) collective-permute-start(f32[64,4,256]{2,1,0:T(4,128)S(1)} %get-tuple-element.89), channel_id=1, source_target_pairs={{16,0},{32,16},{48,32},{64,48},{80,64},{96,80},{112,96},{128,112},... | collective-permute-start | bytes 786440 | tf_op jit(solution)/shard_map/ppermute | solution.py:29
  37.1 13.8 %collective-permute-start.5 = (f32[64,4,256]{2,1,0:T(4,128)S(1)}, f32[64,4,256]{2,1,0:T(4,128)S(1)}, u32[]{:S(2)}, u32[]{:S(2)}) collective-permute-start(f32[64,4,256]{2,1,0:T(4,128)S(1)} %get-tuple-element.90), channel_id=1, source_target_pairs={{0,16},{16,32},{32,48},{48,64},{64,80},{80,96},{96,112},{112,128},... | collective-permute-start | bytes 786440 | tf_op jit(solution)/shard_map/ppermute | solution.py:28
  55.9 21.9 %collective-permute-start.10 = (f32[64,8,256]{2,1,0:T(8,128)S(1)}, f32[64,8,256]{2,1,0:T(8,128)S(1)}, u32[]{:S(2)}, u32[]{:S(2)}) collective-permute-start(f32[64,8,256]{2,1,0:T(8,128)S(1)} %fusion.32), channel_id=1, source_target_pairs={{1,0},{2,1},{3,2},{4,3},{5,4},{6,5},{7,6},{8,7},{9,8},{10,9},{11,1... | collective-permute-start | bytes 1572872 | tf_op jit(solution)/shard_map/ppermute | solution.py:29
  56.0 21.9 %collective-permute-start.11 = (f32[64,8,256]{2,1,0:T(8,128)S(1)}, f32[64,8,256]{2,1,0:T(8,128)S(1)}, u32[]{:S(2)}, u32[]{:S(2)}) collective-permute-start(f32[64,8,256]{2,1,0:T(8,128)S(1)} %fusion.32), channel_id=1, source_target_pairs={{0,1},{1,2},{2,3},{3,4},{4,5},{5,6},{6,7},{7,8},{8,9},{9,10},{10,1... | collective-permute-start | bytes 1572872 | tf_op jit(solution)/shard_map/ppermute | solution.py:28
  57.6 19.5 %collective-permute-start.8 = (f32[64,4,256]{2,1,0:T(4,128)S(1)}, f32[64,4,256]{2,1,0:T(4,128)S(1)}, u32[]{:S(2)}, u32[]{:S(2)}) collective-permute-start(f32[64,4,256]{2,1,0:T(4,128)S(1)} %get-tuple-element.55), channel_id=1, source_target_pairs={{16,0},{32,16},{48,32},{64,48},{80,64},{96,80},{112,96},{128,112},... | collective-permute-start | bytes 786440 | tf_op jit(solution)/shard_map/ppermute | solution.py:29
  63.3 14.6 %collective-permute-start.9 = (f32[64,4,256]{2,1,0:T(4,128)S(1)}, f32[64,4,256]{2,1,0:T(4,128)S(1)}, u32[]{:S(2)}, u32[]{:S(2)}) collective-permute-start(f32[64,4,256]{2,1,0:T(4,128)S(1)} %get-tuple-element.56), channel_id=1, source_target_pairs={{0,16},{16,32},{32,48},{48,64},{64,80},{80,96},{96,112},{112,128},... | collective-permute-start | bytes 786440 | tf_op jit(solution)/shard_map/ppermute | solution.py:28
  85.2 1.7 %collective-permute-start.12 = (f32[64,128]{1,0:T(8,128)}, f32[64,128]{1,0:T(8,128)S(1)}, u32[]{:S(2)}, u32[]{:S(2)}) collective-permute-start(f32[64,128]{1,0:T(8,128)} %gram.1), channel_id=1, source_target_pairs={{0,1},{1,0},{2,3},{3,2},{4,5},{5,4},{6,7},{7,6},{8,9},{9,8},{10,11... | collective-permute-start | bytes 98312 | tf_op jit(solution)/shard_map/ppermute | solution.py:130
  87.7 4.0 %collective-permute-start.13 = (f32[64,128]{1,0:T(8,128)S(1)}, f32[64,128]{1,0:T(8,128)S(1)}, u32[]{:S(2)}, u32[]{:S(2)}) collective-permute-start(f32[64,128]{1,0:T(8,128)S(1)} %pad_maximum_fusion.9), channel_id=1, source_target_pairs={{0,2},{1,3},{2,0},{3,1},{4,6},{5,7},{6,4},{7,5},{8,10},{9,11},{10,... | collective-permute-start | bytes 98312 | tf_op jit(solution)/shard_map/ppermute | solution.py:130
  91.7 5.2 %collective-permute-start.14 = (f32[64,128]{1,0:T(8,128)S(1)}, f32[64,128]{1,0:T(8,128)S(1)}, u32[]{:S(2)}, u32[]{:S(2)}) collective-permute-start(f32[64,128]{1,0:T(8,128)S(1)} %pad_maximum_fusion.10), channel_id=1, source_target_pairs={{0,6},{1,7},{2,4},{3,5},{4,2},{5,3},{6,0},{7,1},{8,14},{9,15},{10,... | collective-permute-start | bytes 98312 | tf_op jit(solution)/shard_map/ppermute | solution.py:130
  96.9 4.4 %collective-permute-start.15 = (f32[64,128]{1,0:T(8,128)S(1)}, f32[64,128]{1,0:T(8,128)S(1)}, u32[]{:S(2)}, u32[]{:S(2)}) collective-permute-start(f32[64,128]{1,0:T(8,128)S(1)} %pad_maximum_fusion.11), channel_id=1, source_target_pairs={{0,16},{1,17},{2,18},{3,19},{4,20},{5,21},{6,22},{7,23},{8,24},{9,... | collective-permute-start | bytes 98312 | tf_op jit(solution)/shard_map/ppermute | solution.py:130
  101.4 5.2 %collective-permute-start.16 = (f32[64,128]{1,0:T(8,128)S(1)}, f32[64,128]{1,0:T(8,128)S(1)}, u32[]{:S(2)}, u32[]{:S(2)}) collective-permute-start(f32[64,128]{1,0:T(8,128)S(1)} %pad_maximum_fusion.12), channel_id=1, source_target_pairs={{0,24},{1,25},{2,26},{3,27},{4,28},{5,29},{6,30},{7,31},{8,16},{9,... | collective-permute-start | bytes 98312 | tf_op jit(solution)/shard_map/ppermute | solution.py:130
  106.6 4.0 %collective-permute-start.17 = (f32[64,128]{1,0:T(8,128)S(1)}, f32[64,128]{1,0:T(8,128)S(1)}, u32[]{:S(2)}, u32[]{:S(2)}) collective-permute-start(f32[64,128]{1,0:T(8,128)S(1)} %pad_maximum_fusion.13), channel_id=1, source_target_pairs={{0,32},{1,33},{2,34},{3,35},{4,36},{5,37},{6,38},{7,39},{8,40},{9,... | collective-permute-start | bytes 98312 | tf_op jit(solution)/shard_map/ppermute | solution.py:130
  110.7 4.9 %collective-permute-start.18 = (f32[64,128]{1,0:T(8,128)S(1)}, f32[64,128]{1,0:T(8,128)S(1)}, u32[]{:S(2)}, u32[]{:S(2)}) collective-permute-start(f32[64,128]{1,0:T(8,128)S(1)} %pad_maximum_fusion.14), channel_id=1, source_target_pairs={{0,64},{1,65},{2,66},{3,67},{4,68},{5,69},{6,70},{7,71},{8,72},{9,... | collective-permute-start | bytes 98312 | tf_op jit(solution)/shard_map/ppermute | solution.py:130
  115.6 7.9 %collective-permute-start.19 = (f32[64,128]{1,0:T(8,128)S(1)}, f32[64,128]{1,0:T(8,128)S(1)}, u32[]{:S(2)}, u32[]{:S(2)}) collective-permute-start(f32[64,128]{1,0:T(8,128)S(1)} %pad_maximum_fusion.15), channel_id=1, source_target_pairs={{0,128},{1,129},{2,130},{3,131},{4,132},{5,133},{6,134},{7,135},{8... | collective-permute-start | bytes 98312 | tf_op jit(solution)/shard_map/ppermute | solution.py:130

commit v2 on v1

--- a/solution.py
+++ b/solution.py
@@ -140,29 +140,58 @@
 
 def lower_inverse(g):
     m = g.shape[0]
-    lane = lax.broadcasted_iota(jnp.int32, (8, 2 * m), 1)
-    sub = lax.broadcasted_iota(jnp.int32, (8, 2 * m), 0)
+    b = 8
+    shape = (b, 2 * m)
+    lane = lax.broadcasted_iota(jnp.int32, shape, 1)
+    sub = lax.broadcasted_iota(jnp.int32, shape, 0)
+    is_row = [sub == i for i in range(b)]
+
+    def spread(tile, i):
+        return jnp.broadcast_to(tile[i : i + 1, :], shape)
+
+    def column(entries):
+        out = None
+        for i, value in entries:
+            out = jnp.where(is_row[i], value, 0.0 if out is None else out)
+        return out
+
     tiles = []
-    for t in range(m // 8):
-        left = jnp.concatenate([g[8 * t : 8 * t + 8, :]] * 2, axis=1)
-        unit = jnp.where(lane == sub + (8 * t + m), 1.0, 0.0)
+    for t in range(m // b):
+        left = jnp.concatenate([g[b * t : b * t + b, :]] * 2, axis=1)
+        unit = jnp.where(lane == sub + (b * t + m), 1.0, 0.0)
         tiles.append(jnp.where(lane < m, left, unit))
-    for j in range(m):
-        own, s = divmod(j, 8)
-        row = jnp.broadcast_to(tiles[own][s : s + 1, :], (8, 2 * m))
-        pivot = jnp.broadcast_to(row[:, j : j + 1], (8, 2 * m))
-        row = row / pivot
-        for t in range(own, m // 8):
-            if t == own and s == 7:
-                continue
-            factor = jnp.broadcast_to(tiles[t][:, j : j + 1], (8, 2 * m))
-            if t == own:
-                factor = jnp.where(sub > s, factor, 0.0)
-            tiles[t] = tiles[t] - factor * row
     out = []
-    for t in range(m // 8):
-        diag = jnp.sum(jnp.where(lane == sub + 8 * t, tiles[t], 0.0), axis=1, keepdims=True)
-        out.append(tiles[t][:, m:] * (1.0 / jnp.sqrt(diag)))
+    for k in range(m // b):
+        cols = [
+            [jnp.broadcast_to(tiles[t][:, b * k + c : b * k + c + 1], shape) for c in range(b)]
+            for t in range(k, m // b)
+        ]
+        a = [[spread(cols[0][c], i) if i >= c else None for c in range(b)] for i in range(b)]
+        low = [[None] * b for _ in range(b)]
+        inv = []
+        for c in range(b):
+            r = 1.0 / a[c][c]
+            inv.append(r)
+            for i in range(c + 1, b):
+                low[i][c] = a[i][c] * r
+            for j in range(c + 1, b):
+                for i in range(j, b):
+                    a[i][j] = a[i][j] - low[i][c] * a[j][c]
+        y = tiles[k]
+        rows = []
+        for c in range(b):
+            rows.append(spread(y, c))
+            if c + 1 < b:
+                y = y - column([(i, low[i][c]) for i in range(c + 1, b)]) * rows[c]
+        scaled = [rows[c] * inv[c] for c in range(b)]
+        for t in range(k + 1, m // b):
+            col = cols[t - k]
+            for c in range(b):
+                for q in range(c):
+                    col[c] = col[c] - col[q] * low[c][q]
+                tiles[t] = tiles[t] - col[c] * scaled[c]
+        root = 1.0 / jnp.sqrt(column(list(enumerate(a[i][i] for i in range(b)))))
+        out.append((y * root)[:, m:])
     return jnp.concatenate(out, axis=0)
 
 

time: 146 us -> 133 us (0.911)
  Pallas kernels: 23.7 us -> 11 us
    pallas_call x1, Pallas kernels: 20.8 us -> 8.08 us  [orthonormal(): pl.pallas_call(functools.partial(rotate_kernel, ncount), out_shape=jax.Sh...]
  transfers between devices with their start and end apart: 20 -> 20, of which waited for: 13 -> 13; matrix products, arithmetic and copies ran while one was open for 4% -> 5% of each run, Pallas kernels for 0% -> 0%
where the time goes in v2:
time: 133 us; the launch traced here: 132 us
  waiting for transfers between devices  59.2 us (45%)
  starting transfers between devices  38 us (29%)
  other arithmetic  13.1 us (10%)
  Pallas kernels  11 us (8%)
  local copies, waits for them, and re-layouts  10.5 us (8%)
    ppermute x6, waiting for transfers between devices, padded(): after = lax.ppermute(first, axis, down)  27.8 us
    ppermute x8, waiting for transfers between devices, swapped(): return lax.ppermute(x, ('gx', 'gy'), [(i, i ^ mask) for i in range(256)])  22.1 us
    ppermute x6, starting transfers between devices, padded(): after = lax.ppermute(first, axis, down)  21.8 us
    ppermute x8, starting transfers between devices, swapped(): return lax.ppermute(x, ('gx', 'gy'), [(i, i ^ mask) for i in range(256)])  15.2 us
    ppermute x6, waiting for transfers between devices, padded(): before = lax.ppermute(last, axis, up)  9.31 us
    pallas_call x1, Pallas kernels, orthonormal(): pl.pallas_call(functools.partial(rotate_kernel, ncount), out_shape=jax.Sh...  8.08 us
    sub x1, other arithmetic, on_device(): 2.0 * (hamiltonian(second, field_pot, depth_index) - CENTER * second)  4.4 us
    sub x1, other arithmetic, on_device(): 2.0 * (hamiltonian(level_one, field_pot, depth_index) - CENTER * level_one)  3.72 us
  transfers between devices with their start and end apart: 20, of which 13 were waited for; matrix products, arithmetic and copies ran while one was open for 5% of the time, Pallas kernels for 0%

profile of v2, /device:TPU:6, one launch (start us, length us, event | category | flops | bytes accessed | tf_op | source)
XLA Modules:
  0.0 132.2 jit_solution(4550570209714358991)
XLA Ops:
  0.0 1.7 %collective-permute-start.2 = (f32[64,8,256]{2,1,0:T(8,128)}, f32[64,8,256]{2,1,0:T(8,128)S(1)}, u32[]{:S(2)}, u32[]{:S(2)}) collective-permute-start(f32[64,8,256]{2,1,0:T(8,128)} %param.2), channel_id=1, source_target_pairs={{1,0},{2,1},{3,2},{4,3},{5,4},{6,5},{7,6},{8,7},{9,8},{10,9},{11,1... | collective-permute-start | bytes 1572872 | tf_op jit(solution)/shard_map/ppermute | solution.py:29
  3.2 6.9 %collective-permute-start = (f32[64,4,256]{2,1,0:T(4,128)S(1)}, f32[64,4,256]{2,1,0:T(4,128)S(1)}, u32[]{:S(2)}, u32[]{:S(2)}) collective-permute-start(f32[64,4,256]{2,1,0:T(4,128)S(1)} %get-tuple-element.126), channel_id=1, source_target_pairs={{16,0},{32,16},{48,32},{64,48},{80,64},{96,80},{112,96},{128,112},... | collective-permute-start | bytes 786440 | tf_op jit(solution)/shard_map/ppermute | solution.py:29
  13.7 9.5 %collective-permute-done = f32[64,4,256]{2,1,0:T(4,128)S(1)} collective-permute-done((f32[64,4,256]{2,1,0:T(4,128)S(1)}, f32[64,4,256]{2,1,0:T(4,128)S(1)}, u32[]{:S(2)}, u32[]{:S(2)}) %collective-permute-start) | collective-permute-done | bytes 262176 | tf_op jit(solution)/shard_map/ppermute | solution.py:29
  23.4 3.4 %broadcast_multiply_fusion = (f32[64,8,256]{2,1,0:T(8,128)S(1)}, f32[64,8,256]{2,1,0:T(8,128)S(1)}) fusion(f32[64,8,256]{2,1,0:T(8,128)S(1)} %copy-done, f32[8,256]{1,0:T(8,128)S(1)} %copy-done.1, f32[64,8,256]{2,1,0:T(8,128)S(1)} %collective-permute-done.2, f32[64,8,256]{2,1,0:T(8,128)S(1)} %collective-permute-done.3, ...), kind=kLoop, calls=%fused_computation.217 | loop fusion | flops 9306112 | bytes 16525312 | tf_op jit(solution)/shard_map/div | solution.py:262
  29.8 7.3 %collective-permute-start.4 = (f32[64,4,256]{2,1,0:T(4,128)S(1)}, f32[64,4,256]{2,1,0:T(4,128)S(1)}, u32[]{:S(2)}, u32[]{:S(2)}) collective-permute-start(f32[64,4,256]{2,1,0:T(4,128)S(1)} %get-tuple-element.89), channel_id=1, source_target_pairs={{16,0},{32,16},{48,32},{64,48},{80,64},{96,80},{112,96},{128,112},... | collective-permute-start | bytes 786440 | tf_op jit(solution)/shard_map/ppermute | solution.py:29
  37.5 4.9 %collective-permute-done.4 = f32[64,4,256]{2,1,0:T(4,128)S(1)} collective-permute-done((f32[64,4,256]{2,1,0:T(4,128)S(1)}, f32[64,4,256]{2,1,0:T(4,128)S(1)}, u32[]{:S(2)}, u32[]{:S(2)}) %collective-permute-start.4) | collective-permute-done | bytes 262176 | tf_op jit(solution)/shard_map/ppermute | solution.py:29
  42.4 8.5 %collective-permute-done.5 = f32[64,4,256]{2,1,0:T(4,128)S(1)} collective-permute-done((f32[64,4,256]{2,1,0:T(4,128)S(1)}, f32[64,4,256]{2,1,0:T(4,128)S(1)}, u32[]{:S(2)}, u32[]{:S(2)}) %collective-permute-start.5) | collective-permute-done | bytes 262176 | tf_op jit(solution)/shard_map/ppermute | solution.py:28
  50.9 3.7 %fusion.32 = f32[64,8,256]{2,1,0:T(8,128)S(1)} fusion(f32[64,8,256]{2,1,0:T(8,128)S(1)} %copy-done, f32[64,8,256]{2,1,0:T(8,128)S(1)} %collective-permute-done.7, f32[64,8,256]{2,1,0:T(8,128)S(1)} %get-tuple-element.21, f32[64,8,256]{2,1,0:T(8,128)S(1)} %collective-permute-done.6, f32[64,4,256]{2,1,0:T(4,128)S(1)} %collective-permute-done.5, ...), kind=kLoop, calls=%fused_computation.78 | loop fusion | flops 10747904 | bytes 12068864 | tf_op jit(solution)/shard_map/sub | solution.py:264
  57.6 5.7 %collective-permute-start.8 = (f32[64,4,256]{2,1,0:T(4,128)S(1)}, f32[64,4,256]{2,1,0:T(4,128)S(1)}, u32[]{:S(2)}, u32[]{:S(2)}) collective-permute-start(f32[64,4,256]{2,1,0:T(4,128)S(1)} %get-tuple-element.55), channel_id=1, source_target_pairs={{16,0},{32,16},{48,32},{64,48},{80,64},{96,80},{112,96},{128,112},... | collective-permute-start | bytes 786440 | tf_op jit(solution)/shard_map/ppermute | solution.py:29
  63.7 13.4 %collective-permute-done.8 = f32[64,4,256]{2,1,0:T(4,128)S(1)} collective-permute-done((f32[64,4,256]{2,1,0:T(4,128)S(1)}, f32[64,4,256]{2,1,0:T(4,128)S(1)}, u32[]{:S(2)}, u32[]{:S(2)}) %collective-permute-start.8) | collective-permute-done | bytes 262176 | tf_op jit(solution)/shard_map/ppermute | solution.py:29
  77.9 4.4 %fusion.12.x_ref = f32[64,8,256]{2,1,0:T(8,128)} fusion(f32[64,8,256]{2,1,0:T(8,128)S(1)} %collective-permute-done.11, f32[64,8,256]{2,1,0:T(8,128)S(1)} %fusion.32, f32[64,8,256]{2,1,0:T(8,128)S(1)} %collective-permute-done.10, f32[64,4,256]{2,1,0:T(4,128)S(1)} %collective-permute-done.9, f32[64,4,256]{2,1,0:T(4,128)S(1)} %collective-permute-done.8, ...), kind=kLoop, calls=%fused_computation.58 | loop fusion | flops 10878976 | bytes 11544576 | tf_op jit(solution)/shard_map/sub | solution.py:268
  82.3 2.9 %gram.1 = f32[64,128]{1,0:T(8,128)} custom-call(f32[64,8,256]{2,1,0:T(8,128)} %fusion.12.x_ref), custom_call_target="tpu_custom_call" | custom-call | tf_op jit(solution)/shard_map/gram/pallas_call | solution.py:241
  87.8 3.9 %collective-permute-done.13 = f32[64,128]{1,0:T(8,128)S(1)} collective-permute-done((f32[64,128]{1,0:T(8,128)S(1)}, f32[64,128]{1,0:T(8,128)S(1)}, u32[]{:S(2)}, u32[]{:S(2)}) %collective-permute-start.13) | collective-permute-done | bytes 32800 | tf_op jit(solution)/shard_map/ppermute | solution.py:130
  93.2 3.8 %collective-permute-done.14 = f32[64,128]{1,0:T(8,128)S(1)} collective-permute-done((f32[64,128]{1,0:T(8,128)S(1)}, f32[64,128]{1,0:T(8,128)S(1)}, u32[]{:S(2)}, u32[]{:S(2)}) %collective-permute-start.14) | collective-permute-done | bytes 32800 | tf_op jit(solution)/shard_map/ppermute | solution.py:130
  96.9 2.5 %collective-permute-start.15 = (f32[64,128]{1,0:T(8,128)S(1)}, f32[64,128]{1,0:T(8,128)S(1)}, u32[]{:S(2)}, u32[]{:S(2)}) collective-permute-start(f32[64,128]{1,0:T(8,128)S(1)} %pad_maximum_fusion.11), channel_id=1, source_target_pairs={{0,16},{1,17},{2,18},{3,19},{4,20},{5,21},{6,22},{7,23},{8,24},{9,... | collective-permute-start | bytes 98312 | tf_op jit(solution)/shard_map/ppermute | solution.py:130
  99.5 1.9 %collective-permute-done.15 = f32[64,128]{1,0:T(8,128)S(1)} collective-permute-done((f32[64,128]{1,0:T(8,128)S(1)}, f32[64,128]{1,0:T(8,128)S(1)}, u32[]{:S(2)}, u32[]{:S(2)}) %collective-permute-start.15) | collective-permute-done | bytes 32800 | tf_op jit(solution)/shard_map/ppermute | solution.py:130
  101.4 2.2 %collective-permute-start.16 = (f32[64,128]{1,0:T(8,128)S(1)}, f32[64,128]{1,0:T(8,128)S(1)}, u32[]{:S(2)}, u32[]{:S(2)}) collective-permute-start(f32[64,128]{1,0:T(8,128)S(1)} %pad_maximum_fusion.12), channel_id=1, source_target_pairs={{0,24},{1,25},{2,26},{3,27},{4,28},{5,29},{6,30},{7,31},{8,16},{9,... | collective-permute-start | bytes 98312 | tf_op jit(solution)/shard_map/ppermute | solution.py:130
  103.6 3.0 %collective-permute-done.16 = f32[64,128]{1,0:T(8,128)S(1)} collective-permute-done((f32[64,128]{1,0:T(8,128)S(1)}, f32[64,128]{1,0:T(8,128)S(1)}, u32[]{:S(2)}, u32[]{:S(2)}) %collective-permute-start.16) | collective-permute-done | bytes 32800 | tf_op jit(solution)/shard_map/ppermute | solution.py:130
  107.4 3.3 %collective-permute-done.17 = f32[64,128]{1,0:T(8,128)S(1)} collective-permute-done((f32[64,128]{1,0:T(8,128)S(1)}, f32[64,128]{1,0:T(8,128)S(1)}, u32[]{:S(2)}, u32[]{:S(2)}) %collective-permute-start.17) | collective-permute-done | bytes 32800 | tf_op jit(solution)/shard_map/ppermute | solution.py:130
  110.7 2.0 %collective-permute-start.18 = (f32[64,128]{1,0:T(8,128)S(1)}, f32[64,128]{1,0:T(8,128)S(1)}, u32[]{:S(2)}, u32[]{:S(2)}) collective-permute-start(f32[64,128]{1,0:T(8,128)S(1)} %pad_maximum_fusion.14), channel_id=1, source_target_pairs={{0,64},{1,65},{2,66},{3,67},{4,68},{5,69},{6,70},{7,71},{8,72},{9,... | collective-permute-start | bytes 98312 | tf_op jit(solution)/shard_map/ppermute | solution.py:130
  112.6 2.9 %collective-permute-done.18 = f32[64,128]{1,0:T(8,128)S(1)} collective-permute-done((f32[64,128]{1,0:T(8,128)S(1)}, f32[64,128]{1,0:T(8,128)S(1)}, u32[]{:S(2)}, u32[]{:S(2)}) %collective-permute-start.18) | collective-permute-done | bytes 32800 | tf_op jit(solution)/shard_map/ppermute | solution.py:130
  115.6 5.7 %collective-permute-start.19 = (f32[64,128]{1,0:T(8,128)S(1)}, f32[64,128]{1,0:T(8,128)S(1)}, u32[]{:S(2)}, u32[]{:S(2)}) collective-permute-start(f32[64,128]{1,0:T(8,128)S(1)} %pad_maximum_fusion.15), channel_id=1, source_target_pairs={{0,128},{1,129},{2,130},{3,131},{4,132},{5,133},{6,134},{7,135},{8... | collective-permute-start | bytes 98312 | tf_op jit(solution)/shard_map/ppermute | solution.py:130
  121.3 2.2 %collective-permute-done.19 = f32[64,128]{1,0:T(8,128)S(1)} collective-permute-done((f32[64,128]{1,0:T(8,128)S(1)}, f32[64,128]{1,0:T(8,128)S(1)}, u32[]{:S(2)}, u32[]{:S(2)}) %collective-permute-start.19) | collective-permute-done | bytes 32800 | tf_op jit(solution)/shard_map/ppermute | solution.py:130
  124.1 8.1 %rotate.1 = f32[64,8,256]{2,1,0:T(8,128)} custom-call(f32[64,128]{1,0:T(8,128)} %pad_maximum_fusion.16.p_ref, f32[64,8,256]{2,1,0:T(8,128)} %fusion.12.x_ref), custom_call_target="tpu_custom_call" | custom-call | tf_op jit(solution)/shard_map/rotate/pallas_call | solution.py:249
  (101 shorter events, 18.0 us)
Async XLA Ops:
  0.0 10.1 %copy-start = (f32[64,8,256]{2,1,0:T(8,128)S(1)}, f32[64,8,256]{2,1,0:T(8,128)}, u32[]{:S(2)}) copy-start(f32[64,8,256]{2,1,0:T(8,128)} %param.2) | copy-start | bytes 1572868
  0.0 13.4 %collective-permute-start.3 = (f32[64,8,256]{2,1,0:T(8,128)}, f32[64,8,256]{2,1,0:T(8,128)S(1)}, u32[]{:S(2)}, u32[]{:S(2)}) collective-permute-start(f32[64,8,256]{2,1,0:T(8,128)} %param.2), channel_id=1, source_target_pairs={{0,1},{1,2},{2,3},{3,4},{4,5},{5,6},{6,7},{7,8},{8,9},{9,10},{10,1... | collective-permute-start | bytes 1572872 | tf_op jit(solution)/shard_map/ppermute | solution.py:28
  0.0 23.3 %collective-permute-start.2 = (f32[64,8,256]{2,1,0:T(8,128)}, f32[64,8,256]{2,1,0:T(8,128)S(1)}, u32[]{:S(2)}, u32[]{:S(2)}) collective-permute-start(f32[64,8,256]{2,1,0:T(8,128)} %param.2), channel_id=1, source_target_pairs={{1,0},{2,1},{3,2},{4,3},{5,4},{6,5},{7,6},{8,7},{9,8},{10,9},{11,1... | collective-permute-start | bytes 1572872 | tf_op jit(solution)/shard_map/ppermute | solution.py:29
  3.2 20.0 %collective-permute-start = (f32[64,4,256]{2,1,0:T(4,128)S(1)}, f32[64,4,256]{2,1,0:T(4,128)S(1)}, u32[]{:S(2)}, u32[]{:S(2)}) collective-permute-start(f32[64,4,256]{2,1,0:T(4,128)S(1)} %get-tuple-element.126), channel_id=1, source_target_pairs={{16,0},{32,16},{48,32},{64,48},{80,64},{96,80},{112,96},{128,112},... | collective-permute-start | bytes 786440 | tf_op jit(solution)/shard_map/ppermute | solution.py:29
  10.1 13.3 %collective-permute-start.1 = (f32[64,4,256]{2,1,0:T(4,128)S(1)}, f32[64,4,256]{2,1,0:T(4,128)S(1)}, u32[]{:S(2)}, u32[]{:S(2)}) collective-permute-start(f32[64,4,256]{2,1,0:T(4,128)S(1)} %get-tuple-element.127), channel_id=1, source_target_pairs={{0,16},{16,32},{32,48},{48,64},{64,80},{80,96},{96,112},{112,128},... | collective-permute-start | bytes 786440 | tf_op jit(solution)/shard_map/ppermute | solution.py:28
  12.5 0.7 copy-start.1
  29.2 21.7 %collective-permute-start.6 = (f32[64,8,256]{2,1,0:T(8,128)S(1)}, f32[64,8,256]{2,1,0:T(8,128)S(1)}, u32[]{:S(2)}, u32[]{:S(2)}) collective-permute-start(f32[64,8,256]{2,1,0:T(8,128)S(1)} %get-tuple-element.21), channel_id=1, source_target_pairs={{1,0},{2,1},{3,2},{4,3},{5,4},{6,5},{7,6},{8,7},{9,8},{10,9},{11,1... | collective-permute-start | bytes 1572872 | tf_op jit(solution)/shard_map/ppermute | solution.py:29
  29.3 21.6 %collective-permute-start.7 = (f32[64,8,256]{2,1,0:T(8,128)S(1)}, f32[64,8,256]{2,1,0:T(8,128)S(1)}, u32[]{:S(2)}, u32[]{:S(2)}) collective-permute-start(f32[64,8,256]{2,1,0:T(8,128)S(1)} %get-tuple-element.21), channel_id=1, source_target_pairs={{0,1},{1,2},{2,3},{3,4},{4,5},{5,6},{6,7},{7,8},{8,9},{9,10},{10,1... | collective-permute-start | bytes 1572872 | tf_op jit(solution)/shard_map/ppermute | solution.py:28
  29.8 12.6 %collective-permute-start.4 = (f32[64,4,256]{2,1,0:T(4,128)S(1)}, f32[64,4,256]{2,1,0:T(4,128)S(1)}, u32[]{:S(2)}, u32[]{:S(2)}) collective-permute-start(f32[64,4,256]{2,1,0:T(4,128)S(1)} %get-tuple-element.89), channel_id=1, source_target_pairs={{16,0},{32,16},{48,32},{64,48},{80,64},{96,80},{112,96},{128,112},... | collective-permute-start | bytes 786440 | tf_op jit(solution)/shard_map/ppermute | solution.py:29
  37.1 13.8 %collective-permute-start.5 = (f32[64,4,256]{2,1,0:T(4,128)S(1)}, f32[64,4,256]{2,1,0:T(4,128)S(1)}, u32[]{:S(2)}, u32[]{:S(2)}) collective-permute-start(f32[64,4,256]{2,1,0:T(4,128)S(1)} %get-tuple-element.90), channel_id=1, source_target_pairs={{0,16},{16,32},{32,48},{48,64},{64,80},{80,96},{96,112},{112,128},... | collective-permute-start | bytes 786440 | tf_op jit(solution)/shard_map/ppermute | solution.py:28
  55.9 21.9 %collective-permute-start.10 = (f32[64,8,256]{2,1,0:T(8,128)S(1)}, f32[64,8,256]{2,1,0:T(8,128)S(1)}, u32[]{:S(2)}, u32[]{:S(2)}) collective-permute-start(f32[64,8,256]{2,1,0:T(8,128)S(1)} %fusion.32), channel_id=1, source_target_pairs={{1,0},{2,1},{3,2},{4,3},{5,4},{6,5},{7,6},{8,7},{9,8},{10,9},{11,1... | collective-permute-start | bytes 1572872 | tf_op jit(solution)/shard_map/ppermute | solution.py:29
  56.0 21.9 %collective-permute-start.11 = (f32[64,8,256]{2,1,0:T(8,128)S(1)}, f32[64,8,256]{2,1,0:T(8,128)S(1)}, u32[]{:S(2)}, u32[]{:S(2)}) collective-permute-start(f32[64,8,256]{2,1,0:T(8,128)S(1)} %fusion.32), channel_id=1, source_target_pairs={{0,1},{1,2},{2,3},{3,4},{4,5},{5,6},{6,7},{7,8},{8,9},{9,10},{10,1... | collective-permute-start | bytes 1572872 | tf_op jit(solution)/shard_map/ppermute | solution.py:28
  57.6 19.5 %collective-permute-start.8 = (f32[64,4,256]{2,1,0:T(4,128)S(1)}, f32[64,4,256]{2,1,0:T(4,128)S(1)}, u32[]{:S(2)}, u32[]{:S(2)}) collective-permute-start(f32[64,4,256]{2,1,0:T(4,128)S(1)} %get-tuple-element.55), channel_id=1, source_target_pairs={{16,0},{32,16},{48,32},{64,48},{80,64},{96,80},{112,96},{128,112},... | collective-permute-start | bytes 786440 | tf_op jit(solution)/shard_map/ppermute | solution.py:29
  63.3 14.6 %collective-permute-start.9 = (f32[64,4,256]{2,1,0:T(4,128)S(1)}, f32[64,4,256]{2,1,0:T(4,128)S(1)}, u32[]{:S(2)}, u32[]{:S(2)}) collective-permute-start(f32[64,4,256]{2,1,0:T(4,128)S(1)} %get-tuple-element.56), channel_id=1, source_target_pairs={{0,16},{16,32},{32,48},{48,64},{64,80},{80,96},{96,112},{112,128},... | collective-permute-start | bytes 786440 | tf_op jit(solution)/shard_map/ppermute | solution.py:28
  85.2 1.7 %collective-permute-start.12 = (f32[64,128]{1,0:T(8,128)}, f32[64,128]{1,0:T(8,128)S(1)}, u32[]{:S(2)}, u32[]{:S(2)}) collective-permute-start(f32[64,128]{1,0:T(8,128)} %gram.1), channel_id=1, source_target_pairs={{0,1},{1,0},{2,3},{3,2},{4,5},{5,4},{6,7},{7,6},{8,9},{9,8},{10,11... | collective-permute-start | bytes 98312 | tf_op jit(solution)/shard_map/ppermute | solution.py:130
  87.7 4.0 %collective-permute-start.13 = (f32[64,128]{1,0:T(8,128)S(1)}, f32[64,128]{1,0:T(8,128)S(1)}, u32[]{:S(2)}, u32[]{:S(2)}) collective-permute-start(f32[64,128]{1,0:T(8,128)S(1)} %pad_maximum_fusion.9), channel_id=1, source_target_pairs={{0,2},{1,3},{2,0},{3,1},{4,6},{5,7},{6,4},{7,5},{8,10},{9,11},{10,... | collective-permute-start | bytes 98312 | tf_op jit(solution)/shard_map/ppermute | solution.py:130
  91.7 5.2 %collective-permute-start.14 = (f32[64,128]{1,0:T(8,128)S(1)}, f32[64,128]{1,0:T(8,128)S(1)}, u32[]{:S(2)}, u32[]{:S(2)}) collective-permute-start(f32[64,128]{1,0:T(8,128)S(1)} %pad_maximum_fusion.10), channel_id=1, source_target_pairs={{0,6},{1,7},{2,4},{3,5},{4,2},{5,3},{6,0},{7,1},{8,14},{9,15},{10,... | collective-permute-start | bytes 98312 | tf_op jit(solution)/shard_map/ppermute | solution.py:130
  96.9 4.4 %collective-permute-start.15 = (f32[64,128]{1,0:T(8,128)S(1)}, f32[64,128]{1,0:T(8,128)S(1)}, u32[]{:S(2)}, u32[]{:S(2)}) collective-permute-start(f32[64,128]{1,0:T(8,128)S(1)} %pad_maximum_fusion.11), channel_id=1, source_target_pairs={{0,16},{1,17},{2,18},{3,19},{4,20},{5,21},{6,22},{7,23},{8,24},{9,... | collective-permute-start | bytes 98312 | tf_op jit(solution)/shard_map/ppermute | solution.py:130
  101.4 5.2 %collective-permute-start.16 = (f32[64,128]{1,0:T(8,128)S(1)}, f32[64,128]{1,0:T(8,128)S(1)}, u32[]{:S(2)}, u32[]{:S(2)}) collective-permute-start(f32[64,128]{1,0:T(8,128)S(1)} %pad_maximum_fusion.12), channel_id=1, source_target_pairs={{0,24},{1,25},{2,26},{3,27},{4,28},{5,29},{6,30},{7,31},{8,16},{9,... | collective-permute-start | bytes 98312 | tf_op jit(solution)/shard_map/ppermute | solution.py:130
  106.6 4.0 %collective-permute-start.17 = (f32[64,128]{1,0:T(8,128)S(1)}, f32[64,128]{1,0:T(8,128)S(1)}, u32[]{:S(2)}, u32[]{:S(2)}) collective-permute-start(f32[64,128]{1,0:T(8,128)S(1)} %pad_maximum_fusion.13), channel_id=1, source_target_pairs={{0,32},{1,33},{2,34},{3,35},{4,36},{5,37},{6,38},{7,39},{8,40},{9,... | collective-permute-start | bytes 98312 | tf_op jit(solution)/shard_map/ppermute | solution.py:130
  110.7 4.9 %collective-permute-start.18 = (f32[64,128]{1,0:T(8,128)S(1)}, f32[64,128]{1,0:T(8,128)S(1)}, u32[]{:S(2)}, u32[]{:S(2)}) collective-permute-start(f32[64,128]{1,0:T(8,128)S(1)} %pad_maximum_fusion.14), channel_id=1, source_target_pairs={{0,64},{1,65},{2,66},{3,67},{4,68},{5,69},{6,70},{7,71},{8,72},{9,... | collective-permute-start | bytes 98312 | tf_op jit(solution)/shard_map/ppermute | solution.py:130
  115.6 7.9 %collective-permute-start.19 = (f32[64,128]{1,0:T(8,128)S(1)}, f32[64,128]{1,0:T(8,128)S(1)}, u32[]{:S(2)}, u32[]{:S(2)}) collective-permute-start(f32[64,128]{1,0:T(8,128)S(1)} %pad_maximum_fusion.15), channel_id=1, source_target_pairs={{0,128},{1,129},{2,130},{3,131},{4,132},{5,133},{6,134},{7,135},{8... | collective-permute-start | bytes 98312 | tf_op jit(solution)/shard_map/ppermute | solution.py:130

commit v3 on v2

--- a/solution.py
+++ b/solution.py
@@ -1,69 +1,144 @@
 import functools
-import math
 
 import jax
 import jax.numpy as jnp
+import numpy as np
 from jax import lax
 from jax.experimental import pallas as pl
 from jax.experimental.pallas import tpu as pltpu
 from jax.sharding import PartitionSpec as P
 
 NZ = 64
-
-
+AXES = ("gx", "gy")
 COEFS = (-205.0 / 72.0, 8.0 / 5.0, -1.0 / 5.0, 8.0 / 315.0, -1.0 / 560.0)
+SCALE = 5040
+WEIGHTS = (8064, -1008, 128, -9)
 CENTER = 6.5
 HALF_WIDTH = 5.5
 VMEM = pl.BlockSpec(memory_space=pltpu.VMEM)
 NT = (((1,), (1,)), ((), ()))
-
-
-def padded(array, sides, width):
-    for axis, dim in sides:
-        size, length = (lax.axis_size(axis), array.shape[dim])
-        up = [(i, (i + 1) % size) for i in range(size)]
-        down = [(j, i) for i, j in up]
-        last = lax.slice_in_dim(array, length - width, length, axis=dim)
-        first = lax.slice_in_dim(array, 0, width, axis=dim)
-        before = lax.ppermute(last, axis, up)
-        after = lax.ppermute(first, axis, down)
-        array = jnp.concatenate([before, array, after], axis=dim)
-    return array
-
-
-def along_third(field, depth_index):
-    laplace = 3.0 * COEFS[0] * field
-    for distance in range(1, 5):
-        forward = jnp.where(
-            depth_index < NZ - distance,
-            jnp.roll(field, -distance, 2),
-            jnp.roll(field, NZ - distance, 2),
-        )
-        behind = jnp.where(
-            depth_index >= distance, jnp.roll(field, distance, 2), jnp.roll(field, distance - NZ, 2)
-        )
-        laplace = laplace + COEFS[distance] * (forward + behind)
-    return laplace
-
-
-def hamiltonian(field, field_pot, depth_index):
-    row_count = field.shape[1]
-    lane_count = field.shape[2]
-    padded_x = padded(field, (("gx", 1),), 4)
-    laplace = along_third(field, depth_index)
-    padded_y = padded(field, (("gy", 2),), 4 * NZ)
-    for distance in range(1, 5):
-        laplace = laplace + COEFS[distance] * (
-            padded_x[:, 4 + distance : 4 + distance + row_count]
-            + padded_x[:, 4 - distance : 4 - distance + row_count]
-        )
-        ahead_start = (4 + distance) * NZ
-        back_start = (4 - distance) * NZ
-        laplace = laplace + COEFS[distance] * (
-            padded_y[:, :, ahead_start : ahead_start + lane_count]
-            + padded_y[:, :, back_start : back_start + lane_count]
-        )
-    return -0.5 * laplace + field_pot * field
+Y_MASKS = (0, 8, 16, 24)
+
+
+def stencil_matrix(cells):
+    lanes = cells * NZ
+    out = np.zeros((3 * lanes, lanes), np.float32)
+    for j in range(cells):
+        for z in range(NZ):
+            for d in range(1, 5):
+                for s in (-d, d):
+                    out[lanes + j * NZ + (z + s) % NZ, j * NZ + z] += WEIGHTS[d - 1]
+                    out[lanes + (j + s) * NZ + z, j * NZ + z] += WEIGHTS[d - 1]
+    return jnp.asarray(out, jnp.bfloat16)
+
+
+def place():
+    gx, gy = lax.axis_index("gx"), lax.axis_index("gy")
+    return gx // 2, gx % 2, gy // 8, (gy % 8) // 2, gy % 2
+
+
+def permute(x, target):
+    return lax.ppermute(x, AXES, [(i, target(i)) for i in range(256)])
+
+
+def swap(x, mask):
+    return permute(x, lambda i: i ^ mask)
+
+
+def z_even(i):
+    return i ^ 32
+
+
+def z_odd(i):
+    z = i // 32
+    return (z + (1 if z % 2 else 7)) % 8 * 32 + i % 32
+
+
+def y_up(i):
+    return i // 8 * 8 + (i + 1) % 8
+
+
+def y_down(i):
+    return i // 8 * 8 + (i + 7) % 8
+
+
+def split_kernel(x_ref, v_ref, *o_refs):
+    _, y_lo, y_hi, _, _ = place()
+    part = x_ref.shape[0] // 4
+    for k, o_ref in enumerate(o_refs):
+        q = (y_lo ^ (k // 2)) * 2 + (y_hi ^ (k % 2))
+        for r in range(8):
+            o_ref[r] = x_ref[pl.ds(q * part, part), r, :]
+        o_ref[8, 0:8, :] = v_ref[...]
+        o_ref[8, 8:16, :] = v_ref[...]
+
+
+def send_faces(even, field, p, f1_ref, f2_ref):
+    low, high = field[0:4], field[12:16]
+    f1_ref[p] = jnp.where(even, high, low)
+    f2_ref[p] = jnp.where(even, low, high)
+
+
+def join_kernel(*refs):
+    parts, (f_ref, v_ref, f1_ref, f2_ref) = refs[:4], refs[4:]
+    z, y_lo, _, _, _ = place()
+    even = z % 2 == 0
+    for k, ref in enumerate(parts):
+        start = (y_lo ^ (k // 2)) * 8
+        f_ref[k % 2, pl.ds(start, 8)] = ref[0:8]
+        v = (ref[8, 0:8, :] - (CENTER + 1.5 * COEFS[0])) * (2.0 / HALF_WIDTH)
+        for r in range(8):
+            v_ref[k % 2, start + r] = jnp.broadcast_to(v[r : r + 1, :], v.shape)
+    for p in range(2):
+        send_faces(even, f_ref.at[p], p, f1_ref, f2_ref)
+
+
+def level_kernel(level, *refs):
+    f_ref, l_ref, r_ref, z1_ref, z2_ref, v_ref, m_ref = refs[:7]
+    refs = refs[7:]
+    if level > 1:
+        old_ref, refs = refs[0], refs[1:]
+    z, y_lo, _, x, core = place()
+    even = z % 2 == 0
+    rows, orbs, lanes = f_ref.shape[1:]
+    flat = (rows * orbs, lanes)
+    left_flip = jnp.where((x == 0) & (core == 0), 1, 0)
+    right_flip = jnp.where((x == 3) & (core == 1), 1, 0)
+    factor = 2.0 if level > 1 else 1.0
+    alpha = -0.5 * factor / (HALF_WIDTH * SCALE)
+    for p in range(2):
+        near = []
+        for ref, q in ((l_ref, p ^ left_flip), (f_ref, p), (r_ref, p ^ right_flip)):
+            rest = ref[q].reshape(flat)
+            pieces = []
+            for _ in range(2):
+                pieces.append(rest.astype(jnp.bfloat16))
+                rest = rest - pieces[-1].astype(jnp.float32)
+            near.append(pieces + [rest.astype(jnp.bfloat16)])
+        total = None
+        for s in (2, 1, 0):
+            lhs = jnp.concatenate([near[b][s] for b in range(3)], axis=1)
+            term = jnp.dot(lhs, m_ref[...], preferred_element_type=jnp.float32)
+            total = term if total is None else total + term
+        below = jnp.where(even, z2_ref[p], z1_ref[p])
+        above = jnp.where(even, z1_ref[p], z2_ref[p])
+        tall = jnp.concatenate([below, f_ref[p], above], axis=0)
+        total = total.reshape(rows, orbs, lanes)
+        for d in (4, 3, 2, 1):
+            pair = tall[4 + d : 4 + d + rows] + tall[4 - d : 4 - d + rows]
+            total = total + float(WEIGHTS[d - 1]) * pair
+        v = v_ref[p] if level > 1 else 0.5 * v_ref[p]
+        v = jnp.concatenate([v] * (orbs // 8), axis=1)
+        out = alpha * total + v * f_ref[p]
+        if level > 1:
+            out = out - old_ref[p]
+        if level < 3:
+            refs[0][p] = out
+            send_faces(even, out, p, refs[1], refs[2])
+        else:
+            refs[4][...] = out
+            for k in (p, p + 2):
+                refs[k][...] = refs[4][pl.ds((y_lo ^ (k // 2)) * 8, 8)]
 
 
 def two_sum(a, b):
@@ -85,16 +160,19 @@
     return out, rest
 
 
-def gram_kernel(x_ref, o_ref):
-    m, rows, _ = x_ref.shape
-    top = jnp.max(jnp.abs(x_ref[:, 0, :]), axis=1, keepdims=True)
-    for r in range(1, rows):
-        top = jnp.maximum(top, jnp.max(jnp.abs(x_ref[:, r, :]), axis=1, keepdims=True))
+def gram_kernel(*refs):
+    parts, (x_ref, o_ref) = refs[:4], refs[4:]
+    rows, m, _ = x_ref.shape
+    _, y_lo, y_hi, _, _ = place()
+    for k, ref in enumerate(parts):
+        q = (y_lo ^ (k // 2)) * 2 + (y_hi ^ (k % 2))
+        x_ref[:, pl.ds(pl.multiple_of(q * (m // 4), m // 4), m // 4), :] = ref[...]
+    top = jnp.max(jnp.max(jnp.abs(x_ref[...]), axis=0), axis=1, keepdims=True)
     g0 = top * (1.5 * 2.0**17)
     g1 = top * (1.5 * 2.0**11)
     total = None
     for r in range(rows):
-        x = x_ref[:, r, :]
+        x = x_ref[r]
         s0 = (x + g0) - g0
         x = x - s0
         s1 = (x + g1) - g1
@@ -127,7 +205,7 @@
 
 def reduce_pairs(x):
     def swapped(mask):
-        return lax.ppermute(x, ("gx", "gy"), [(i, i ^ mask) for i in range(256)])
+        return lax.ppermute(x, AXES, [(i, i ^ mask) for i in range(256)])
 
     for masks in ((1,), (2,), (6,), (16,), (24,), (32,), (64,), (128,)):
         if len(masks) == 1:
@@ -219,7 +297,7 @@
 
 
 def rotate_kernel(ncount, p_ref, x_ref, o_ref):
-    m, rows, _ = x_ref.shape
+    rows, m, _ = x_ref.shape
     h = m // 2
     hi, lo = p_ref[:h, :] * (1.0 / ncount), p_ref[h:, :] * (1.0 / ncount)
     hi = jnp.concatenate([hi[:, :m], hi[:, m:]], axis=0)
@@ -233,43 +311,50 @@
     inverse2 = lower_inverse(gram2)
     both = jnp.dot(inverse2, inverse1, precision=lax.Precision.HIGHEST)
     for r in range(rows):
-        o_ref[:, r, :] = jnp.dot(both, x_ref[:, r, :], precision=lax.Precision.HIGHEST)
-
-
-def orthonormal(block, ncount):
-    m = block.shape[0]
-    local = pl.pallas_call(
-        gram_kernel,
-        out_shape=jax.ShapeDtypeStruct((m, 2 * m), jnp.float32),
-        in_specs=[VMEM],
-        out_specs=VMEM,
-        name="gram",
-    )(block)
-    total = reduce_pairs(local)
+        o_ref[:, r, :] = jnp.dot(both, x_ref[r], precision=lax.Precision.HIGHEST)
+
+
+def call(kernel, name, outs, *args, scratch=()):
+    single = len(outs) == 1
+    shapes = [jax.ShapeDtypeStruct(shape, jnp.float32) for shape in outs]
     return pl.pallas_call(
-        functools.partial(rotate_kernel, ncount),
-        out_shape=jax.ShapeDtypeStruct(block.shape, jnp.float32),
-        in_specs=[VMEM, VMEM],
-        out_specs=VMEM,
-        name="rotate",
-    )(total, block)
+        kernel,
+        out_shape=shapes[0] if single else shapes,
+        in_specs=[VMEM] * len(args),
+        out_specs=VMEM if single else [VMEM] * len(shapes),
+        scratch_shapes=[pltpu.VMEM(shape, jnp.float32) for shape in scratch],
+        compiler_params=pltpu.CompilerParams(vmem_limit_bytes=32 << 20),
+        name=name,
+    )(*args)
 
 
 def on_device(psi, potential):
-    orbit_count, row_count, lane_count = psi.shape
-    field_pot = potential.reshape(1, row_count, lane_count)
-    depth_index = lax.broadcasted_iota(jnp.int32, (1, 1, lane_count), 2) % NZ
-    level_one = (hamiltonian(psi, field_pot, depth_index) - CENTER * psi) / HALF_WIDTH
-    second = (
-        2.0 * (hamiltonian(level_one, field_pot, depth_index) - CENTER * level_one) / HALF_WIDTH
-        - psi
-    )
-    filtered = (
-        2.0 * (hamiltonian(second, field_pot, depth_index) - CENTER * second) / HALF_WIDTH
-        - level_one
-    )
-    ncount = float(row_count * lane_count * lax.axis_size("gx") * lax.axis_size("gy"))
-    return orthonormal(filtered, ncount)
+    m, rows, lanes = psi.shape
+    orbs = m // 4
+    part = (rows, orbs, lanes)
+    field = (2, 2 * rows, orbs, lanes)
+    face = (2, 4, orbs, lanes)
+    matrix = stencil_matrix(lanes // NZ)
+    parts = call(split_kernel, "split", [(rows + 1, orbs, lanes)] * 4, psi, potential)
+    parts = [parts[0]] + [swap(parts[k], Y_MASKS[k]) for k in (1, 2, 3)]
+    joined = [field, (2, 2 * rows, 8, lanes), face, face]
+    now, v, face1, face2 = call(join_kernel, "join", joined, *parts)
+    old = None
+    for level in (1, 2, 3):
+        left, right = permute(now, y_up), permute(now, y_down)
+        face1, face2 = permute(face1, z_even), permute(face2, z_odd)
+        args = [now, left, right, face1, face2, v, matrix] + ([] if old is None else [old])
+        kernel = functools.partial(level_kernel, level)
+        if level < 3:
+            outs = call(kernel, f"level{level}", [field, face, face], *args)
+            old, (now, face1, face2) = now, outs
+        else:
+            parts = call(kernel, "level3", [part] * 4, *args, scratch=[field[1:]])
+    parts = [parts[0]] + [swap(parts[k], Y_MASKS[k]) for k in (1, 2, 3)]
+    block, local = call(gram_kernel, "gram", [(rows, m, lanes), (m, 2 * m)], *parts)
+    ncount = float(rows * lanes * lax.axis_size("gx") * lax.axis_size("gy"))
+    kernel = functools.partial(rotate_kernel, ncount)
+    return call(kernel, "rotate", [psi.shape], reduce_pairs(local), block)
 
 
 def solution(mesh):

time: 133 us -> 103 us (0.77)
  other arithmetic: 13.1 us -> 0.16 us
  waiting for transfers between devices: 59.2 us -> 49 us
  local copies, waits for them, and re-layouts: 10.5 us -> 1.74 us
  starting transfers between devices: 38 us -> 39.4 us
    ppermute x20 -> x26, waiting for transfers between devices: 59.2 us -> 49 us  [the longest x18 26 us: permute(): return lax.ppermute(x, AXES, [(i, target(i)) for i in range(256)])]
    slice x51 -> x0, local copies, waits for them, and re-layouts: 9.57 us -> none  [the longest x16 2.68 us: along_third(): jnp.roll(field, distance, 2)]
    sub x2 -> x0, other arithmetic: 8.12 us -> none  [the longest x1 4.4 us: on_device(): 2.0 * (hamiltonian(second, field_pot, depth_index) - CENTER * second)]
    div x1 -> x0, other arithmetic: 3.45 us -> none  [on_device(): (hamiltonian(psi, field_pot, depth_index) - CENTER * psi) / HALF_WIDTH]
    ppermute x20 -> x26, starting transfers between devices: 38 us -> 39.4 us  [the longest x18 25.5 us: permute(): return lax.ppermute(x, AXES, [(i, target(i)) for i in range(256)])]
    pallas_call x2 -> x7, Pallas kernels: 11 us -> 11.3 us  [call(): pl.pallas_call(kernel, out_shape=shapes[0] if single else shapes, in_spec...]
  transfers between devices with their start and end apart: 20 -> 26, of which waited for: 13 -> 21; matrix products, arithmetic and copies ran while one was open for 5% -> 0% of each run, Pallas kernels for 0% -> 0%
where the time goes in v3:
time: 103 us; the launch traced here: 102 us
  waiting for transfers between devices  49 us (48%)
  starting transfers between devices  39.4 us (38%)
  Pallas kernels  11.3 us (11%)
  local copies, waits for them, and re-layouts  1.74 us (2%)
    ppermute x18, waiting for transfers between devices, permute(): return lax.ppermute(x, AXES, [(i, target(i)) for i in range(256)])  26 us
    ppermute x18, starting transfers between devices, permute(): return lax.ppermute(x, AXES, [(i, target(i)) for i in range(256)])  25.5 us
    ppermute x8, waiting for transfers between devices, swapped(): return lax.ppermute(x, AXES, [(i, i ^ mask) for i in range(256)])  23 us
    ppermute x8, starting transfers between devices, swapped(): return lax.ppermute(x, AXES, [(i, i ^ mask) for i in range(256)])  13.9 us
    pallas_call x7, Pallas kernels, call(): pl.pallas_call(kernel, out_shape=shapes[0] if single else shapes, in_spec...  11.3 us
  transfers between devices with their start and end apart: 26, of which 21 were waited for; matrix products, arithmetic and copies ran while one was open for 0% of the time, Pallas kernels for 0%

profile of v3, /device:TPU:6, one launch (start us, length us, event | category | flops | bytes accessed | tf_op | source)
XLA Modules:
  0.0 101.7 jit_solution(18295433561779229941)
XLA Ops:
  1.9 3.3 %collective-permute-start = (f32[9,16,256]{2,1,0:T(8,128)S(1)}, f32[9,16,256]{2,1,0:T(8,128)S(1)}, u32[]{:S(2)}, u32[]{:S(2)}) collective-permute-start(f32[9,16,256]{2,1,0:T(8,128)S(1)} %get-tuple-element.26), channel_id=1, source_target_pairs={{0,8},{1,9},{2,10},{3,11},{4,12},{5,13},{6,14},{7,15},{8,0},{9,1},... | collective-permute-start | bytes 442376 | tf_op jit(solution)/shard_map/ppermute | solution.py:41
  6.3 4.0 %collective-permute-done.refs_1_ = f32[9,16,256]{2,1,0:T(8,128)S(1)} collective-permute-done((f32[9,16,256]{2,1,0:T(8,128)S(1)}, f32[9,16,256]{2,1,0:T(8,128)S(1)}, u32[]{:S(2)}, u32[]{:S(2)}) %collective-permute-start) | collective-permute-done | bytes 147488 | tf_op jit(solution)/shard_map/ppermute | solution.py:41
  10.2 2.4 %collective-permute-done.1.refs_2_ = f32[9,16,256]{2,1,0:T(8,128)S(1)} collective-permute-done((f32[9,16,256]{2,1,0:T(8,128)S(1)}, f32[9,16,256]{2,1,0:T(8,128)S(1)}, u32[]{:S(2)}, u32[]{:S(2)}) %collective-permute-start.1) | collective-permute-done | bytes 147488 | tf_op jit(solution)/shard_map/ppermute | solution.py:41
  13.4 1.9 %collective-permute-start.5 = (f32[2,4,16,256]{3,2,1,0:T(8,128)S(1)}, f32[2,4,16,256]{3,2,1,0:T(8,128)S(1)}, u32[]{:S(2)}, u32[]{:S(2)}) collective-permute-start(f32[2,4,16,256]{3,2,1,0:T(8,128)S(1)} %get-tuple-element.30), channel_id=1, source_target_pairs={{0,32},{1,33},{2,34},{3,35},{4,36},{5,37},{6,38},{7,39},{8,40},{9,... | collective-permute-start | bytes 393224 | tf_op jit(solution)/shard_map/ppermute | solution.py:41
  15.3 4.9 %collective-permute-start.6 = (f32[2,4,16,256]{3,2,1,0:T(8,128)S(1)}, f32[2,4,16,256]{3,2,1,0:T(8,128)S(1)}, u32[]{:S(2)}, u32[]{:S(2)}) collective-permute-start(f32[2,4,16,256]{3,2,1,0:T(8,128)S(1)} %get-tuple-element.31), channel_id=1, source_target_pairs={{0,224},{1,225},{2,226},{3,227},{4,228},{5,229},{6,230},{7,231},{8... | collective-permute-start | bytes 393224 | tf_op jit(solution)/shard_map/ppermute | solution.py:41
  20.2 3.9 %collective-permute-done.6.refs_4_ = f32[2,4,16,256]{3,2,1,0:T(8,128)S(1)} collective-permute-done((f32[2,4,16,256]{3,2,1,0:T(8,128)S(1)}, f32[2,4,16,256]{3,2,1,0:T(8,128)S(1)}, u32[]{:S(2)}, u32[]{:S(2)}) %collective-permute-start.6) | collective-permute-done | bytes 131104 | tf_op jit(solution)/shard_map/ppermute | solution.py:41
  25.9 4.0 %collective-permute-start.10 = (f32[2,4,16,256]{3,2,1,0:T(8,128)S(1)}, f32[2,4,16,256]{3,2,1,0:T(8,128)S(1)}, u32[]{:S(2)}, u32[]{:S(2)}) collective-permute-start(f32[2,4,16,256]{3,2,1,0:T(8,128)S(1)} %get-tuple-element.35), channel_id=1, source_target_pairs={{0,224},{1,225},{2,226},{3,227},{4,228},{5,229},{6,230},{7,231},{8... | collective-permute-start | bytes 393224 | tf_op jit(solution)/shard_map/ppermute | solution.py:41
  30.8 2.0 %collective-permute-done.10.refs_4_ = f32[2,4,16,256]{3,2,1,0:T(8,128)S(1)} collective-permute-done((f32[2,4,16,256]{3,2,1,0:T(8,128)S(1)}, f32[2,4,16,256]{3,2,1,0:T(8,128)S(1)}, u32[]{:S(2)}, u32[]{:S(2)}) %collective-permute-start.10) | collective-permute-done | bytes 131104 | tf_op jit(solution)/shard_map/ppermute | solution.py:41
  36.3 4.1 %collective-permute-start.14 = (f32[2,4,16,256]{3,2,1,0:T(8,128)S(1)}, f32[2,4,16,256]{3,2,1,0:T(8,128)S(1)}, u32[]{:S(2)}, u32[]{:S(2)}) collective-permute-start(f32[2,4,16,256]{3,2,1,0:T(8,128)S(1)} %get-tuple-element.38), channel_id=1, source_target_pairs={{0,224},{1,225},{2,226},{3,227},{4,228},{5,229},{6,230},{7,231},{8... | collective-permute-start | bytes 393224 | tf_op jit(solution)/shard_map/ppermute | solution.py:41
  41.3 2.1 %collective-permute-done.14.refs_4_ = f32[2,4,16,256]{3,2,1,0:T(8,128)S(1)} collective-permute-done((f32[2,4,16,256]{3,2,1,0:T(8,128)S(1)}, f32[2,4,16,256]{3,2,1,0:T(8,128)S(1)}, u32[]{:S(2)}, u32[]{:S(2)}) %collective-permute-start.14) | collective-permute-done | bytes 131104 | tf_op jit(solution)/shard_map/ppermute | solution.py:41
  45.4 2.8 %collective-permute-start.15 = (f32[8,16,256]{2,1,0:T(8,128)S(1)}, f32[8,16,256]{2,1,0:T(8,128)S(1)}, u32[]{:S(2)}, u32[]{:S(2)}) collective-permute-start(f32[8,16,256]{2,1,0:T(8,128)S(1)} %get-tuple-element.40), channel_id=1, source_target_pairs={{0,8},{1,9},{2,10},{3,11},{4,12},{5,13},{6,14},{7,15},{8,0},{9,1},... | collective-permute-start | bytes 393224 | tf_op jit(solution)/shard_map/ppermute | solution.py:41
  49.6 3.1 %collective-permute-done.15.refs_1_ = f32[8,16,256]{2,1,0:T(8,128)S(1)} collective-permute-done((f32[8,16,256]{2,1,0:T(8,128)S(1)}, f32[8,16,256]{2,1,0:T(8,128)S(1)}, u32[]{:S(2)}, u32[]{:S(2)}) %collective-permute-start.15) | collective-permute-done | bytes 131104 | tf_op jit(solution)/shard_map/ppermute | solution.py:41
  52.7 2.6 %collective-permute-done.16.refs_2_ = f32[8,16,256]{2,1,0:T(8,128)S(1)} collective-permute-done((f32[8,16,256]{2,1,0:T(8,128)S(1)}, f32[8,16,256]{2,1,0:T(8,128)S(1)}, u32[]{:S(2)}, u32[]{:S(2)}) %collective-permute-start.16) | collective-permute-done | bytes 131104 | tf_op jit(solution)/shard_map/ppermute | solution.py:41
  59.0 3.9 %collective-permute-done.19 = f32[64,128]{1,0:T(8,128)S(1)} collective-permute-done((f32[64,128]{1,0:T(8,128)S(1)}, f32[64,128]{1,0:T(8,128)S(1)}, u32[]{:S(2)}, u32[]{:S(2)}) %collective-permute-start.19) | collective-permute-done | bytes 32800 | tf_op jit(solution)/shard_map/ppermute | solution.py:208
  62.9 3.5 %collective-permute-start.20 = (f32[64,128]{1,0:T(8,128)S(1)}, f32[64,128]{1,0:T(8,128)S(1)}, u32[]{:S(2)}, u32[]{:S(2)}) collective-permute-start(f32[64,128]{1,0:T(8,128)S(1)} %pad_maximum_fusion.1), channel_id=1, source_target_pairs={{0,6},{1,7},{2,4},{3,5},{4,2},{5,3},{6,0},{7,1},{8,14},{9,15},{10,... | collective-permute-start | bytes 98312 | tf_op jit(solution)/shard_map/ppermute | solution.py:208
  66.4 1.9 %collective-permute-done.20 = f32[64,128]{1,0:T(8,128)S(1)} collective-permute-done((f32[64,128]{1,0:T(8,128)S(1)}, f32[64,128]{1,0:T(8,128)S(1)}, u32[]{:S(2)}, u32[]{:S(2)}) %collective-permute-start.20) | collective-permute-done | bytes 32800 | tf_op jit(solution)/shard_map/ppermute | solution.py:208
  69.2 3.1 %collective-permute-done.21 = f32[64,128]{1,0:T(8,128)S(1)} collective-permute-done((f32[64,128]{1,0:T(8,128)S(1)}, f32[64,128]{1,0:T(8,128)S(1)}, u32[]{:S(2)}, u32[]{:S(2)}) %collective-permute-start.21) | collective-permute-done | bytes 32800 | tf_op jit(solution)/shard_map/ppermute | solution.py:208
  72.4 2.3 %collective-permute-start.22 = (f32[64,128]{1,0:T(8,128)S(1)}, f32[64,128]{1,0:T(8,128)S(1)}, u32[]{:S(2)}, u32[]{:S(2)}) collective-permute-start(f32[64,128]{1,0:T(8,128)S(1)} %pad_maximum_fusion.3), channel_id=1, source_target_pairs={{0,24},{1,25},{2,26},{3,27},{4,28},{5,29},{6,30},{7,31},{8,16},{9,... | collective-permute-start | bytes 98312 | tf_op jit(solution)/shard_map/ppermute | solution.py:208
  74.6 2.9 %collective-permute-done.22 = f32[64,128]{1,0:T(8,128)S(1)} collective-permute-done((f32[64,128]{1,0:T(8,128)S(1)}, f32[64,128]{1,0:T(8,128)S(1)}, u32[]{:S(2)}, u32[]{:S(2)}) %collective-permute-start.22) | collective-permute-done | bytes 32800 | tf_op jit(solution)/shard_map/ppermute | solution.py:208
  77.8 3.8 %collective-permute-done.23 = f32[64,128]{1,0:T(8,128)S(1)} collective-permute-done((f32[64,128]{1,0:T(8,128)S(1)}, f32[64,128]{1,0:T(8,128)S(1)}, u32[]{:S(2)}, u32[]{:S(2)}) %collective-permute-start.23) | collective-permute-done | bytes 32800 | tf_op jit(solution)/shard_map/ppermute | solution.py:208
  83.2 3.6 %collective-permute-done.24 = f32[64,128]{1,0:T(8,128)S(1)} collective-permute-done((f32[64,128]{1,0:T(8,128)S(1)}, f32[64,128]{1,0:T(8,128)S(1)}, u32[]{:S(2)}, u32[]{:S(2)}) %collective-permute-start.24) | collective-permute-done | bytes 32800 | tf_op jit(solution)/shard_map/ppermute | solution.py:208
  86.8 5.2 %collective-permute-start.25 = (f32[64,128]{1,0:T(8,128)S(1)}, f32[64,128]{1,0:T(8,128)S(1)}, u32[]{:S(2)}, u32[]{:S(2)}) collective-permute-start(f32[64,128]{1,0:T(8,128)S(1)} %pad_maximum_fusion.6), channel_id=1, source_target_pairs={{0,128},{1,129},{2,130},{3,131},{4,132},{5,133},{6,134},{7,135},{8... | collective-permute-start | bytes 98312 | tf_op jit(solution)/shard_map/ppermute | solution.py:208
  92.0 2.7 %collective-permute-done.25 = f32[64,128]{1,0:T(8,128)S(1)} collective-permute-done((f32[64,128]{1,0:T(8,128)S(1)}, f32[64,128]{1,0:T(8,128)S(1)}, u32[]{:S(2)}, u32[]{:S(2)}) %collective-permute-start.25) | collective-permute-done | bytes 32800 | tf_op jit(solution)/shard_map/ppermute | solution.py:208
  94.7 7.0 %rotate.1 = f32[64,8,256]{2,1,0:T(8,128)} custom-call(f32[64,128]{1,0:T(8,128)S(1)} %pad_maximum_fusion.7.p_ref, f32[8,64,256]{2,1,0:T(8,128)S(1)} %get-tuple-element.44.x_ref), custom_call_target="tpu_custom_call" | custom-call | tf_op jit(solution)/shard_map/rotate/pallas_call | solution.py:320
  (57 shorter events, 20.6 us)
Async XLA Ops:
  1.9 8.3 %collective-permute-start = (f32[9,16,256]{2,1,0:T(8,128)S(1)}, f32[9,16,256]{2,1,0:T(8,128)S(1)}, u32[]{:S(2)}, u32[]{:S(2)}) collective-permute-start(f32[9,16,256]{2,1,0:T(8,128)S(1)} %get-tuple-element.26), channel_id=1, source_target_pairs={{0,8},{1,9},{2,10},{3,11},{4,12},{5,13},{6,14},{7,15},{8,0},{9,1},... | collective-permute-start | bytes 442376 | tf_op jit(solution)/shard_map/ppermute | solution.py:41
  5.2 7.4 %collective-permute-start.1 = (f32[9,16,256]{2,1,0:T(8,128)S(1)}, f32[9,16,256]{2,1,0:T(8,128)S(1)}, u32[]{:S(2)}, u32[]{:S(2)}) collective-permute-start(f32[9,16,256]{2,1,0:T(8,128)S(1)} %get-tuple-element.27), channel_id=1, source_target_pairs={{0,16},{1,17},{2,18},{3,19},{4,20},{5,21},{6,22},{7,23},{8,24},{9,... | collective-permute-start | bytes 442376 | tf_op jit(solution)/shard_map/ppermute | solution.py:41
  5.9 6.9 %collective-permute-start.2 = (f32[9,16,256]{2,1,0:T(8,128)S(1)}, f32[9,16,256]{2,1,0:T(8,128)S(1)}, u32[]{:S(2)}, u32[]{:S(2)}) collective-permute-start(f32[9,16,256]{2,1,0:T(8,128)S(1)} %get-tuple-element.28), channel_id=1, source_target_pairs={{0,24},{1,25},{2,26},{3,27},{4,28},{5,29},{6,30},{7,31},{8,16},{9,... | collective-permute-start | bytes 442376 | tf_op jit(solution)/shard_map/ppermute | solution.py:41
  12.9 11.3 %collective-permute-start.4 = (f32[2,16,16,256]{3,2,1,0:T(8,128)S(1)}, f32[2,16,16,256]{3,2,1,0:T(8,128)S(1)}, u32[]{:S(2)}, u32[]{:S(2)}) collective-permute-start(f32[2,16,16,256]{3,2,1,0:T(8,128)S(1)} %get-tuple-element.29.refs_0_.refs_7_), channel_id=1, source_target_pairs={{0,7},{1,0},{2,1},{3,2},{4,3},{5,4},{6,5},{7,6},{8,15},{9,8},{10,9... | collective-permute-start | bytes 1572872 | tf_op jit(solution)/shard_map/ppermute | solution.py:41
  12.9 11.3 %collective-permute-start.3 = (f32[2,16,16,256]{3,2,1,0:T(8,128)S(1)}, f32[2,16,16,256]{3,2,1,0:T(8,128)S(1)}, u32[]{:S(2)}, u32[]{:S(2)}) collective-permute-start(f32[2,16,16,256]{3,2,1,0:T(8,128)S(1)} %get-tuple-element.29.refs_0_.refs_7_), channel_id=1, source_target_pairs={{0,1},{1,2},{2,3},{3,4},{4,5},{5,6},{6,7},{7,0},{8,9},{9,10},{10,1... | collective-permute-start | bytes 1572872 | tf_op jit(solution)/shard_map/ppermute | solution.py:41
  13.4 6.9 %collective-permute-start.5 = (f32[2,4,16,256]{3,2,1,0:T(8,128)S(1)}, f32[2,4,16,256]{3,2,1,0:T(8,128)S(1)}, u32[]{:S(2)}, u32[]{:S(2)}) collective-permute-start(f32[2,4,16,256]{3,2,1,0:T(8,128)S(1)} %get-tuple-element.30), channel_id=1, source_target_pairs={{0,32},{1,33},{2,34},{3,35},{4,36},{5,37},{6,38},{7,39},{8,40},{9,... | collective-permute-start | bytes 393224 | tf_op jit(solution)/shard_map/ppermute | solution.py:41
  15.3 8.9 %collective-permute-start.6 = (f32[2,4,16,256]{3,2,1,0:T(8,128)S(1)}, f32[2,4,16,256]{3,2,1,0:T(8,128)S(1)}, u32[]{:S(2)}, u32[]{:S(2)}) collective-permute-start(f32[2,4,16,256]{3,2,1,0:T(8,128)S(1)} %get-tuple-element.31), channel_id=1, source_target_pairs={{0,224},{1,225},{2,226},{3,227},{4,228},{5,229},{6,230},{7,231},{8... | collective-permute-start | bytes 393224 | tf_op jit(solution)/shard_map/ppermute | solution.py:41
  25.2 7.6 %collective-permute-start.8 = (f32[2,16,16,256]{3,2,1,0:T(8,128)S(1)}, f32[2,16,16,256]{3,2,1,0:T(8,128)S(1)}, u32[]{:S(2)}, u32[]{:S(2)}) collective-permute-start(f32[2,16,16,256]{3,2,1,0:T(8,128)S(1)} %get-tuple-element.33.refs_0_.refs_7_), channel_id=1, source_target_pairs={{0,7},{1,0},{2,1},{3,2},{4,3},{5,4},{6,5},{7,6},{8,15},{9,8},{10,9... | collective-permute-start | bytes 1572872 | tf_op jit(solution)/shard_map/ppermute | solution.py:41
  25.9 8.6 %collective-permute-start.7 = (f32[2,16,16,256]{3,2,1,0:T(8,128)S(1)}, f32[2,16,16,256]{3,2,1,0:T(8,128)S(1)}, u32[]{:S(2)}, u32[]{:S(2)}) collective-permute-start(f32[2,16,16,256]{3,2,1,0:T(8,128)S(1)} %get-tuple-element.33.refs_0_.refs_7_), channel_id=1, source_target_pairs={{0,1},{1,2},{2,3},{3,4},{4,5},{5,6},{6,7},{7,0},{8,9},{9,10},{10,1... | collective-permute-start | bytes 1572872 | tf_op jit(solution)/shard_map/ppermute | solution.py:41
  25.9 5.0 %collective-permute-start.9 = (f32[2,4,16,256]{3,2,1,0:T(8,128)S(1)}, f32[2,4,16,256]{3,2,1,0:T(8,128)S(1)}, u32[]{:S(2)}, u32[]{:S(2)}) collective-permute-start(f32[2,4,16,256]{3,2,1,0:T(8,128)S(1)} %get-tuple-element.34), channel_id=1, source_target_pairs={{0,32},{1,33},{2,34},{3,35},{4,36},{5,37},{6,38},{7,39},{8,40},{9,... | collective-permute-start | bytes 393224 | tf_op jit(solution)/shard_map/ppermute | solution.py:41
  25.9 7.0 %collective-permute-start.10 = (f32[2,4,16,256]{3,2,1,0:T(8,128)S(1)}, f32[2,4,16,256]{3,2,1,0:T(8,128)S(1)}, u32[]{:S(2)}, u32[]{:S(2)}) collective-permute-start(f32[2,4,16,256]{3,2,1,0:T(8,128)S(1)} %get-tuple-element.35), channel_id=1, source_target_pairs={{0,224},{1,225},{2,226},{3,227},{4,228},{5,229},{6,230},{7,231},{8... | collective-permute-start | bytes 393224 | tf_op jit(solution)/shard_map/ppermute | solution.py:41
  35.5 7.9 %collective-permute-start.12 = (f32[2,16,16,256]{3,2,1,0:T(8,128)S(1)}, f32[2,16,16,256]{3,2,1,0:T(8,128)S(1)}, u32[]{:S(2)}, u32[]{:S(2)}) collective-permute-start(f32[2,16,16,256]{3,2,1,0:T(8,128)S(1)} %get-tuple-element.36.refs_0_), channel_id=1, source_target_pairs={{0,7},{1,0},{2,1},{3,2},{4,3},{5,4},{6,5},{7,6},{8,15},{9,8},{10,9... | collective-permute-start | bytes 1572872 | tf_op jit(solution)/shard_map/ppermute | solution.py:41
  35.8 8.6 %collective-permute-start.11 = (f32[2,16,16,256]{3,2,1,0:T(8,128)S(1)}, f32[2,16,16,256]{3,2,1,0:T(8,128)S(1)}, u32[]{:S(2)}, u32[]{:S(2)}) collective-permute-start(f32[2,16,16,256]{3,2,1,0:T(8,128)S(1)} %get-tuple-element.36.refs_0_), channel_id=1, source_target_pairs={{0,1},{1,2},{2,3},{3,4},{4,5},{5,6},{6,7},{7,0},{8,9},{9,10},{10,1... | collective-permute-start | bytes 1572872 | tf_op jit(solution)/shard_map/ppermute | solution.py:41
  36.3 5.0 %collective-permute-start.13 = (f32[2,4,16,256]{3,2,1,0:T(8,128)S(1)}, f32[2,4,16,256]{3,2,1,0:T(8,128)S(1)}, u32[]{:S(2)}, u32[]{:S(2)}) collective-permute-start(f32[2,4,16,256]{3,2,1,0:T(8,128)S(1)} %get-tuple-element.37), channel_id=1, source_target_pairs={{0,32},{1,33},{2,34},{3,35},{4,36},{5,37},{6,38},{7,39},{8,40},{9,... | collective-permute-start | bytes 393224 | tf_op jit(solution)/shard_map/ppermute | solution.py:41
  36.3 7.1 %collective-permute-start.14 = (f32[2,4,16,256]{3,2,1,0:T(8,128)S(1)}, f32[2,4,16,256]{3,2,1,0:T(8,128)S(1)}, u32[]{:S(2)}, u32[]{:S(2)}) collective-permute-start(f32[2,4,16,256]{3,2,1,0:T(8,128)S(1)} %get-tuple-element.38), channel_id=1, source_target_pairs={{0,224},{1,225},{2,226},{3,227},{4,228},{5,229},{6,230},{7,231},{8... | collective-permute-start | bytes 393224 | tf_op jit(solution)/shard_map/ppermute | solution.py:41
  45.4 7.3 %collective-permute-start.15 = (f32[8,16,256]{2,1,0:T(8,128)S(1)}, f32[8,16,256]{2,1,0:T(8,128)S(1)}, u32[]{:S(2)}, u32[]{:S(2)}) collective-permute-start(f32[8,16,256]{2,1,0:T(8,128)S(1)} %get-tuple-element.40), channel_id=1, source_target_pairs={{0,8},{1,9},{2,10},{3,11},{4,12},{5,13},{6,14},{7,15},{8,0},{9,1},... | collective-permute-start | bytes 393224 | tf_op jit(solution)/shard_map/ppermute | solution.py:41
  48.2 7.1 %collective-permute-start.16 = (f32[8,16,256]{2,1,0:T(8,128)S(1)}, f32[8,16,256]{2,1,0:T(8,128)S(1)}, u32[]{:S(2)}, u32[]{:S(2)}) collective-permute-start(f32[8,16,256]{2,1,0:T(8,128)S(1)} %get-tuple-element.41), channel_id=1, source_target_pairs={{0,16},{1,17},{2,18},{3,19},{4,20},{5,21},{6,22},{7,23},{8,24},{9,... | collective-permute-start | bytes 393224 | tf_op jit(solution)/shard_map/ppermute | solution.py:41
  48.9 7.6 %collective-permute-start.17 = (f32[8,16,256]{2,1,0:T(8,128)S(1)}, f32[8,16,256]{2,1,0:T(8,128)S(1)}, u32[]{:S(2)}, u32[]{:S(2)}) collective-permute-start(f32[8,16,256]{2,1,0:T(8,128)S(1)} %get-tuple-element.42), channel_id=1, source_target_pairs={{0,24},{1,25},{2,26},{3,27},{4,28},{5,29},{6,30},{7,31},{8,16},{9,... | collective-permute-start | bytes 393224 | tf_op jit(solution)/shard_map/ppermute | solution.py:41
  58.9 4.0 %collective-permute-start.19 = (f32[64,128]{1,0:T(8,128)S(1)}, f32[64,128]{1,0:T(8,128)S(1)}, u32[]{:S(2)}, u32[]{:S(2)}) collective-permute-start(f32[64,128]{1,0:T(8,128)S(1)} %pad_maximum_fusion), channel_id=1, source_target_pairs={{0,2},{1,3},{2,0},{3,1},{4,6},{5,7},{6,4},{7,5},{8,10},{9,11},{10,... | collective-permute-start | bytes 98312 | tf_op jit(solution)/shard_map/ppermute | solution.py:208
  62.9 5.4 %collective-permute-start.20 = (f32[64,128]{1,0:T(8,128)S(1)}, f32[64,128]{1,0:T(8,128)S(1)}, u32[]{:S(2)}, u32[]{:S(2)}) collective-permute-start(f32[64,128]{1,0:T(8,128)S(1)} %pad_maximum_fusion.1), channel_id=1, source_target_pairs={{0,6},{1,7},{2,4},{3,5},{4,2},{5,3},{6,0},{7,1},{8,14},{9,15},{10,... | collective-permute-start | bytes 98312 | tf_op jit(solution)/shard_map/ppermute | solution.py:208
  72.4 5.2 %collective-permute-start.22 = (f32[64,128]{1,0:T(8,128)S(1)}, f32[64,128]{1,0:T(8,128)S(1)}, u32[]{:S(2)}, u32[]{:S(2)}) collective-permute-start(f32[64,128]{1,0:T(8,128)S(1)} %pad_maximum_fusion.3), channel_id=1, source_target_pairs={{0,24},{1,25},{2,26},{3,27},{4,28},{5,29},{6,30},{7,31},{8,16},{9,... | collective-permute-start | bytes 98312 | tf_op jit(solution)/shard_map/ppermute | solution.py:208
  77.6 4.0 %collective-permute-start.23 = (f32[64,128]{1,0:T(8,128)S(1)}, f32[64,128]{1,0:T(8,128)S(1)}, u32[]{:S(2)}, u32[]{:S(2)}) collective-permute-start(f32[64,128]{1,0:T(8,128)S(1)} %pad_maximum_fusion.4), channel_id=1, source_target_pairs={{0,32},{1,33},{2,34},{3,35},{4,36},{5,37},{6,38},{7,39},{8,40},{9,... | collective-permute-start | bytes 98312 | tf_op jit(solution)/shard_map/ppermute | solution.py:208
  81.6 5.1 %collective-permute-start.24 = (f32[64,128]{1,0:T(8,128)S(1)}, f32[64,128]{1,0:T(8,128)S(1)}, u32[]{:S(2)}, u32[]{:S(2)}) collective-permute-start(f32[64,128]{1,0:T(8,128)S(1)} %pad_maximum_fusion.5), channel_id=1, source_target_pairs={{0,64},{1,65},{2,66},{3,67},{4,68},{5,69},{6,70},{7,71},{8,72},{9,... | collective-permute-start | bytes 98312 | tf_op jit(solution)/shard_map/ppermute | solution.py:208
  86.8 7.9 %collective-permute-start.25 = (f32[64,128]{1,0:T(8,128)S(1)}, f32[64,128]{1,0:T(8,128)S(1)}, u32[]{:S(2)}, u32[]{:S(2)}) collective-permute-start(f32[64,128]{1,0:T(8,128)S(1)} %pad_maximum_fusion.6), channel_id=1, source_target_pairs={{0,128},{1,129},{2,130},{3,131},{4,132},{5,133},{6,134},{7,135},{8... | collective-permute-start | bytes 98312 | tf_op jit(solution)/shard_map/ppermute | solution.py:208
  (5 other events, 29.3 us)

commit v4 on v3

--- a/solution.py
+++ b/solution.py
@@ -207,7 +207,7 @@
     def swapped(mask):
         return lax.ppermute(x, AXES, [(i, i ^ mask) for i in range(256)])
 
-    for masks in ((1,), (2,), (6,), (16,), (24,), (32,), (64,), (128,)):
+    for masks in ((1,), (2, 16, 18), (6, 24, 30), (32, 64, 96), (192,)):
         if len(masks) == 1:
             x = pair_add(x, swapped(masks[0]))
         else:

time: 103 us -> 96.7 us (0.939); the launches traced: 102 us -> 96.5 us
  waiting for transfers between devices: 49 us -> 39.2 us
  starting transfers between devices: 39.4 us -> 44 us
    ppermute x8 -> x11, waiting for transfers between devices: 23 us -> 13.2 us  [swapped(): return lax.ppermute(x, AXES, [(i, i ^ mask) for i in range(256)])]
    ppermute x8 -> x11, starting transfers between devices: 13.9 us -> 18.5 us  [swapped(): return lax.ppermute(x, AXES, [(i, i ^ mask) for i in range(256)])]
  transfers between devices with their start and end apart: 26 -> 29, of which waited for: 21 -> 22; matrix products, arithmetic and copies ran while one was open for 0% -> 0% of each run, Pallas kernels for 0% -> 0%
where the time goes in v4:
time: 96.7 us; the launch traced here: 96.5 us
  starting transfers between devices  44 us (46%)
  waiting for transfers between devices  39.2 us (41%)
  Pallas kernels  11.3 us (12%)
  local copies, waits for them, and re-layouts  1.74 us (2%)
    ppermute x18, waiting for transfers between devices, permute(): return lax.ppermute(x, AXES, [(i, target(i)) for i in range(256)])  26 us
    ppermute x18, starting transfers between devices, permute(): return lax.ppermute(x, AXES, [(i, target(i)) for i in range(256)])  25.5 us
    ppermute x11, starting transfers between devices, swapped(): return lax.ppermute(x, AXES, [(i, i ^ mask) for i in range(256)])  18.5 us
    ppermute x11, waiting for transfers between devices, swapped(): return lax.ppermute(x, AXES, [(i, i ^ mask) for i in range(256)])  13.2 us
    pallas_call x7, Pallas kernels, call(): pl.pallas_call(kernel, out_shape=shapes[0] if single else shapes, in_spec...  11.3 us
  transfers between devices with their start and end apart: 29, of which 22 were waited for; matrix products, arithmetic and copies ran while one was open for 0% of the time, Pallas kernels for 0%

profile of v4, /device:TPU:6, one launch (start us, length us, event | category | flops | bytes accessed | tf_op | source)
XLA Modules:
  0.0 96.5 jit_solution(10394507055593592913)
XLA Ops:
  1.9 3.3 %collective-permute-start = (f32[9,16,256]{2,1,0:T(8,128)S(1)}, f32[9,16,256]{2,1,0:T(8,128)S(1)}, u32[]{:S(2)}, u32[]{:S(2)}) collective-permute-start(f32[9,16,256]{2,1,0:T(8,128)S(1)} %get-tuple-element.26), channel_id=1, source_target_pairs={{0,8},{1,9},{2,10},{3,11},{4,12},{5,13},{6,14},{7,15},{8,0},{9,1},... | collective-permute-start | bytes 442376 | tf_op jit(solution)/shard_map/ppermute | solution.py:41
  6.3 4.0 %collective-permute-done.refs_1_ = f32[9,16,256]{2,1,0:T(8,128)S(1)} collective-permute-done((f32[9,16,256]{2,1,0:T(8,128)S(1)}, f32[9,16,256]{2,1,0:T(8,128)S(1)}, u32[]{:S(2)}, u32[]{:S(2)}) %collective-permute-start) | collective-permute-done | bytes 147488 | tf_op jit(solution)/shard_map/ppermute | solution.py:41
  10.2 2.4 %collective-permute-done.1.refs_2_ = f32[9,16,256]{2,1,0:T(8,128)S(1)} collective-permute-done((f32[9,16,256]{2,1,0:T(8,128)S(1)}, f32[9,16,256]{2,1,0:T(8,128)S(1)}, u32[]{:S(2)}, u32[]{:S(2)}) %collective-permute-start.1) | collective-permute-done | bytes 147488 | tf_op jit(solution)/shard_map/ppermute | solution.py:41
  13.4 1.9 %collective-permute-start.5 = (f32[2,4,16,256]{3,2,1,0:T(8,128)S(1)}, f32[2,4,16,256]{3,2,1,0:T(8,128)S(1)}, u32[]{:S(2)}, u32[]{:S(2)}) collective-permute-start(f32[2,4,16,256]{3,2,1,0:T(8,128)S(1)} %get-tuple-element.30), channel_id=1, source_target_pairs={{0,32},{1,33},{2,34},{3,35},{4,36},{5,37},{6,38},{7,39},{8,40},{9,... | collective-permute-start | bytes 393224 | tf_op jit(solution)/shard_map/ppermute | solution.py:41
  15.3 4.9 %collective-permute-start.6 = (f32[2,4,16,256]{3,2,1,0:T(8,128)S(1)}, f32[2,4,16,256]{3,2,1,0:T(8,128)S(1)}, u32[]{:S(2)}, u32[]{:S(2)}) collective-permute-start(f32[2,4,16,256]{3,2,1,0:T(8,128)S(1)} %get-tuple-element.31), channel_id=1, source_target_pairs={{0,224},{1,225},{2,226},{3,227},{4,228},{5,229},{6,230},{7,231},{8... | collective-permute-start | bytes 393224 | tf_op jit(solution)/shard_map/ppermute | solution.py:41
  20.2 3.9 %collective-permute-done.6.refs_4_ = f32[2,4,16,256]{3,2,1,0:T(8,128)S(1)} collective-permute-done((f32[2,4,16,256]{3,2,1,0:T(8,128)S(1)}, f32[2,4,16,256]{3,2,1,0:T(8,128)S(1)}, u32[]{:S(2)}, u32[]{:S(2)}) %collective-permute-start.6) | collective-permute-done | bytes 131104 | tf_op jit(solution)/shard_map/ppermute | solution.py:41
  25.9 4.0 %collective-permute-start.10 = (f32[2,4,16,256]{3,2,1,0:T(8,128)S(1)}, f32[2,4,16,256]{3,2,1,0:T(8,128)S(1)}, u32[]{:S(2)}, u32[]{:S(2)}) collective-permute-start(f32[2,4,16,256]{3,2,1,0:T(8,128)S(1)} %get-tuple-element.35), channel_id=1, source_target_pairs={{0,224},{1,225},{2,226},{3,227},{4,228},{5,229},{6,230},{7,231},{8... | collective-permute-start | bytes 393224 | tf_op jit(solution)/shard_map/ppermute | solution.py:41
  30.8 2.0 %collective-permute-done.10.refs_4_ = f32[2,4,16,256]{3,2,1,0:T(8,128)S(1)} collective-permute-done((f32[2,4,16,256]{3,2,1,0:T(8,128)S(1)}, f32[2,4,16,256]{3,2,1,0:T(8,128)S(1)}, u32[]{:S(2)}, u32[]{:S(2)}) %collective-permute-start.10) | collective-permute-done | bytes 131104 | tf_op jit(solution)/shard_map/ppermute | solution.py:41
  32.8 1.6 %collective-permute-done.7.refs_1_ = f32[2,16,16,256]{3,2,1,0:T(8,128)S(1)} collective-permute-done((f32[2,16,16,256]{3,2,1,0:T(8,128)S(1)}, f32[2,16,16,256]{3,2,1,0:T(8,128)S(1)}, u32[]{:S(2)}, u32[]{:S(2)}) %collective-permute-start.7) | collective-permute-done | bytes 524320 | tf_op jit(solution)/shard_map/ppermute | solution.py:41
  36.3 4.1 %collective-permute-start.14 = (f32[2,4,16,256]{3,2,1,0:T(8,128)S(1)}, f32[2,4,16,256]{3,2,1,0:T(8,128)S(1)}, u32[]{:S(2)}, u32[]{:S(2)}) collective-permute-start(f32[2,4,16,256]{3,2,1,0:T(8,128)S(1)} %get-tuple-element.38), channel_id=1, source_target_pairs={{0,224},{1,225},{2,226},{3,227},{4,228},{5,229},{6,230},{7,231},{8... | collective-permute-start | bytes 393224 | tf_op jit(solution)/shard_map/ppermute | solution.py:41
  41.3 2.1 %collective-permute-done.14.refs_4_ = f32[2,4,16,256]{3,2,1,0:T(8,128)S(1)} collective-permute-done((f32[2,4,16,256]{3,2,1,0:T(8,128)S(1)}, f32[2,4,16,256]{3,2,1,0:T(8,128)S(1)}, u32[]{:S(2)}, u32[]{:S(2)}) %collective-permute-start.14) | collective-permute-done | bytes 131104 | tf_op jit(solution)/shard_map/ppermute | solution.py:41
  45.4 2.8 %collective-permute-start.15 = (f32[8,16,256]{2,1,0:T(8,128)S(1)}, f32[8,16,256]{2,1,0:T(8,128)S(1)}, u32[]{:S(2)}, u32[]{:S(2)}) collective-permute-start(f32[8,16,256]{2,1,0:T(8,128)S(1)} %get-tuple-element.40), channel_id=1, source_target_pairs={{0,8},{1,9},{2,10},{3,11},{4,12},{5,13},{6,14},{7,15},{8,0},{9,1},... | collective-permute-start | bytes 393224 | tf_op jit(solution)/shard_map/ppermute | solution.py:41
  49.6 3.1 %collective-permute-done.15.refs_1_ = f32[8,16,256]{2,1,0:T(8,128)S(1)} collective-permute-done((f32[8,16,256]{2,1,0:T(8,128)S(1)}, f32[8,16,256]{2,1,0:T(8,128)S(1)}, u32[]{:S(2)}, u32[]{:S(2)}) %collective-permute-start.15) | collective-permute-done | bytes 131104 | tf_op jit(solution)/shard_map/ppermute | solution.py:41
  52.7 2.6 %collective-permute-done.16.refs_2_ = f32[8,16,256]{2,1,0:T(8,128)S(1)} collective-permute-done((f32[8,16,256]{2,1,0:T(8,128)S(1)}, f32[8,16,256]{2,1,0:T(8,128)S(1)}, u32[]{:S(2)}, u32[]{:S(2)}) %collective-permute-start.16) | collective-permute-done | bytes 131104 | tf_op jit(solution)/shard_map/ppermute | solution.py:41
  60.1 2.4 %collective-permute-start.19 = (f32[64,128]{1,0:T(8,128)S(1)}, f32[64,128]{1,0:T(8,128)S(1)}, u32[]{:S(2)}, u32[]{:S(2)}) collective-permute-start(f32[64,128]{1,0:T(8,128)S(1)} %pad_maximum_fusion), channel_id=1, source_target_pairs={{0,2},{1,3},{2,0},{3,1},{4,6},{5,7},{6,4},{7,5},{8,10},{9,11},{10,... | collective-permute-start | bytes 98312 | tf_op jit(solution)/shard_map/ppermute | solution.py:208
  64.4 3.7 %collective-permute-start.24 = (f32[64,128]{1,0:T(8,128)S(1)}, f32[64,128]{1,0:T(8,128)S(1)}, u32[]{:S(2)}, u32[]{:S(2)}) collective-permute-start(f32[64,128]{1,0:T(8,128)S(1)} %pad_maximum_fusion.1), channel_id=1, source_target_pairs={{0,30},{1,31},{2,28},{3,29},{4,26},{5,27},{6,24},{7,25},{8,22},{9,... | collective-permute-start | bytes 98312 | tf_op jit(solution)/shard_map/ppermute | solution.py:208
  68.1 2.3 %collective-permute-start.23 = (f32[64,128]{1,0:T(8,128)S(1)}, f32[64,128]{1,0:T(8,128)S(1)}, u32[]{:S(2)}, u32[]{:S(2)}) collective-permute-start(f32[64,128]{1,0:T(8,128)S(1)} %pad_maximum_fusion.1), channel_id=1, source_target_pairs={{0,24},{1,25},{2,26},{3,27},{4,28},{5,29},{6,30},{7,31},{8,16},{9,... | collective-permute-start | bytes 98312 | tf_op jit(solution)/shard_map/ppermute | solution.py:208
  73.2 2.3 %collective-permute-done.22 = f32[64,128]{1,0:T(8,128)S(1)} collective-permute-done((f32[64,128]{1,0:T(8,128)S(1)}, f32[64,128]{1,0:T(8,128)S(1)}, u32[]{:S(2)}, u32[]{:S(2)}) %collective-permute-start.22) | collective-permute-done | bytes 32800 | tf_op jit(solution)/shard_map/ppermute | solution.py:208
  75.5 2.9 %collective-permute-start.27 = (f32[64,128]{1,0:T(8,128)S(1)}, f32[64,128]{1,0:T(8,128)S(1)}, u32[]{:S(2)}, u32[]{:S(2)}) collective-permute-start(f32[64,128]{1,0:T(8,128)S(1)} %pad_maximum_fusion.2), channel_id=1, source_target_pairs={{0,96},{1,97},{2,98},{3,99},{4,100},{5,101},{6,102},{7,103},{8,104... | collective-permute-start | bytes 98312 | tf_op jit(solution)/shard_map/ppermute | solution.py:208
  78.5 1.6 %collective-permute-start.25 = (f32[64,128]{1,0:T(8,128)S(1)}, f32[64,128]{1,0:T(8,128)S(1)}, u32[]{:S(2)}, u32[]{:S(2)}) collective-permute-start(f32[64,128]{1,0:T(8,128)S(1)} %pad_maximum_fusion.2), channel_id=1, source_target_pairs={{0,32},{1,33},{2,34},{3,35},{4,36},{5,37},{6,38},{7,39},{8,40},{9,... | collective-permute-start | bytes 98312 | tf_op jit(solution)/shard_map/ppermute | solution.py:208
  81.4 1.9 %collective-permute-done.26 = f32[64,128]{1,0:T(8,128)S(1)} collective-permute-done((f32[64,128]{1,0:T(8,128)S(1)}, f32[64,128]{1,0:T(8,128)S(1)}, u32[]{:S(2)}, u32[]{:S(2)}) %collective-permute-start.26) | collective-permute-done | bytes 32800 | tf_op jit(solution)/shard_map/ppermute | solution.py:208
  83.3 4.2 %collective-permute-start.28 = (f32[64,128]{1,0:T(8,128)S(1)}, f32[64,128]{1,0:T(8,128)S(1)}, u32[]{:S(2)}, u32[]{:S(2)}) collective-permute-start(f32[64,128]{1,0:T(8,128)S(1)} %pad_maximum_fusion.3), channel_id=1, source_target_pairs={{0,192},{1,193},{2,194},{3,195},{4,196},{5,197},{6,198},{7,199},{8... | collective-permute-start | bytes 98312 | tf_op jit(solution)/shard_map/ppermute | solution.py:208
  87.6 1.9 %collective-permute-done.28 = f32[64,128]{1,0:T(8,128)S(1)} collective-permute-done((f32[64,128]{1,0:T(8,128)S(1)}, f32[64,128]{1,0:T(8,128)S(1)}, u32[]{:S(2)}, u32[]{:S(2)}) %collective-permute-start.28) | collective-permute-done | bytes 32800 | tf_op jit(solution)/shard_map/ppermute | solution.py:208
  89.5 7.0 %rotate.1 = f32[64,8,256]{2,1,0:T(8,128)} custom-call(f32[64,128]{1,0:T(8,128)S(1)} %pad_maximum_fusion.4.p_ref, f32[8,64,256]{2,1,0:T(8,128)S(1)} %get-tuple-element.44.x_ref), custom_call_target="tpu_custom_call" | custom-call | tf_op jit(solution)/shard_map/rotate/pallas_call | solution.py:320
  (60 shorter events, 23.5 us)
Async XLA Ops:
  1.9 8.3 %collective-permute-start = (f32[9,16,256]{2,1,0:T(8,128)S(1)}, f32[9,16,256]{2,1,0:T(8,128)S(1)}, u32[]{:S(2)}, u32[]{:S(2)}) collective-permute-start(f32[9,16,256]{2,1,0:T(8,128)S(1)} %get-tuple-element.26), channel_id=1, source_target_pairs={{0,8},{1,9},{2,10},{3,11},{4,12},{5,13},{6,14},{7,15},{8,0},{9,1},... | collective-permute-start | bytes 442376 | tf_op jit(solution)/shard_map/ppermute | solution.py:41
  5.2 7.4 %collective-permute-start.1 = (f32[9,16,256]{2,1,0:T(8,128)S(1)}, f32[9,16,256]{2,1,0:T(8,128)S(1)}, u32[]{:S(2)}, u32[]{:S(2)}) collective-permute-start(f32[9,16,256]{2,1,0:T(8,128)S(1)} %get-tuple-element.27), channel_id=1, source_target_pairs={{0,16},{1,17},{2,18},{3,19},{4,20},{5,21},{6,22},{7,23},{8,24},{9,... | collective-permute-start | bytes 442376 | tf_op jit(solution)/shard_map/ppermute | solution.py:41
  5.9 6.9 %collective-permute-start.2 = (f32[9,16,256]{2,1,0:T(8,128)S(1)}, f32[9,16,256]{2,1,0:T(8,128)S(1)}, u32[]{:S(2)}, u32[]{:S(2)}) collective-permute-start(f32[9,16,256]{2,1,0:T(8,128)S(1)} %get-tuple-element.28), channel_id=1, source_target_pairs={{0,24},{1,25},{2,26},{3,27},{4,28},{5,29},{6,30},{7,31},{8,16},{9,... | collective-permute-start | bytes 442376 | tf_op jit(solution)/shard_map/ppermute | solution.py:41
  12.9 11.3 %collective-permute-start.4 = (f32[2,16,16,256]{3,2,1,0:T(8,128)S(1)}, f32[2,16,16,256]{3,2,1,0:T(8,128)S(1)}, u32[]{:S(2)}, u32[]{:S(2)}) collective-permute-start(f32[2,16,16,256]{3,2,1,0:T(8,128)S(1)} %get-tuple-element.29.refs_0_.refs_7_), channel_id=1, source_target_pairs={{0,7},{1,0},{2,1},{3,2},{4,3},{5,4},{6,5},{7,6},{8,15},{9,8},{10,9... | collective-permute-start | bytes 1572872 | tf_op jit(solution)/shard_map/ppermute | solution.py:41
  12.9 11.3 %collective-permute-start.3 = (f32[2,16,16,256]{3,2,1,0:T(8,128)S(1)}, f32[2,16,16,256]{3,2,1,0:T(8,128)S(1)}, u32[]{:S(2)}, u32[]{:S(2)}) collective-permute-start(f32[2,16,16,256]{3,2,1,0:T(8,128)S(1)} %get-tuple-element.29.refs_0_.refs_7_), channel_id=1, source_target_pairs={{0,1},{1,2},{2,3},{3,4},{4,5},{5,6},{6,7},{7,0},{8,9},{9,10},{10,1... | collective-permute-start | bytes 1572872 | tf_op jit(solution)/shard_map/ppermute | solution.py:41
  13.4 6.9 %collective-permute-start.5 = (f32[2,4,16,256]{3,2,1,0:T(8,128)S(1)}, f32[2,4,16,256]{3,2,1,0:T(8,128)S(1)}, u32[]{:S(2)}, u32[]{:S(2)}) collective-permute-start(f32[2,4,16,256]{3,2,1,0:T(8,128)S(1)} %get-tuple-element.30), channel_id=1, source_target_pairs={{0,32},{1,33},{2,34},{3,35},{4,36},{5,37},{6,38},{7,39},{8,40},{9,... | collective-permute-start | bytes 393224 | tf_op jit(solution)/shard_map/ppermute | solution.py:41
  15.3 8.9 %collective-permute-start.6 = (f32[2,4,16,256]{3,2,1,0:T(8,128)S(1)}, f32[2,4,16,256]{3,2,1,0:T(8,128)S(1)}, u32[]{:S(2)}, u32[]{:S(2)}) collective-permute-start(f32[2,4,16,256]{3,2,1,0:T(8,128)S(1)} %get-tuple-element.31), channel_id=1, source_target_pairs={{0,224},{1,225},{2,226},{3,227},{4,228},{5,229},{6,230},{7,231},{8... | collective-permute-start | bytes 393224 | tf_op jit(solution)/shard_map/ppermute | solution.py:41
  25.2 7.6 %collective-permute-start.8 = (f32[2,16,16,256]{3,2,1,0:T(8,128)S(1)}, f32[2,16,16,256]{3,2,1,0:T(8,128)S(1)}, u32[]{:S(2)}, u32[]{:S(2)}) collective-permute-start(f32[2,16,16,256]{3,2,1,0:T(8,128)S(1)} %get-tuple-element.33.refs_0_.refs_7_), channel_id=1, source_target_pairs={{0,7},{1,0},{2,1},{3,2},{4,3},{5,4},{6,5},{7,6},{8,15},{9,8},{10,9... | collective-permute-start | bytes 1572872 | tf_op jit(solution)/shard_map/ppermute | solution.py:41
  25.9 8.6 %collective-permute-start.7 = (f32[2,16,16,256]{3,2,1,0:T(8,128)S(1)}, f32[2,16,16,256]{3,2,1,0:T(8,128)S(1)}, u32[]{:S(2)}, u32[]{:S(2)}) collective-permute-start(f32[2,16,16,256]{3,2,1,0:T(8,128)S(1)} %get-tuple-element.33.refs_0_.refs_7_), channel_id=1, source_target_pairs={{0,1},{1,2},{2,3},{3,4},{4,5},{5,6},{6,7},{7,0},{8,9},{9,10},{10,1... | collective-permute-start | bytes 1572872 | tf_op jit(solution)/shard_map/ppermute | solution.py:41
  25.9 5.0 %collective-permute-start.9 = (f32[2,4,16,256]{3,2,1,0:T(8,128)S(1)}, f32[2,4,16,256]{3,2,1,0:T(8,128)S(1)}, u32[]{:S(2)}, u32[]{:S(2)}) collective-permute-start(f32[2,4,16,256]{3,2,1,0:T(8,128)S(1)} %get-tuple-element.34), channel_id=1, source_target_pairs={{0,32},{1,33},{2,34},{3,35},{4,36},{5,37},{6,38},{7,39},{8,40},{9,... | collective-permute-start | bytes 393224 | tf_op jit(solution)/shard_map/ppermute | solution.py:41
  25.9 7.0 %collective-permute-start.10 = (f32[2,4,16,256]{3,2,1,0:T(8,128)S(1)}, f32[2,4,16,256]{3,2,1,0:T(8,128)S(1)}, u32[]{:S(2)}, u32[]{:S(2)}) collective-permute-start(f32[2,4,16,256]{3,2,1,0:T(8,128)S(1)} %get-tuple-element.35), channel_id=1, source_target_pairs={{0,224},{1,225},{2,226},{3,227},{4,228},{5,229},{6,230},{7,231},{8... | collective-permute-start | bytes 393224 | tf_op jit(solution)/shard_map/ppermute | solution.py:41
  35.5 7.9 %collective-permute-start.12 = (f32[2,16,16,256]{3,2,1,0:T(8,128)S(1)}, f32[2,16,16,256]{3,2,1,0:T(8,128)S(1)}, u32[]{:S(2)}, u32[]{:S(2)}) collective-permute-start(f32[2,16,16,256]{3,2,1,0:T(8,128)S(1)} %get-tuple-element.36.refs_0_), channel_id=1, source_target_pairs={{0,7},{1,0},{2,1},{3,2},{4,3},{5,4},{6,5},{7,6},{8,15},{9,8},{10,9... | collective-permute-start | bytes 1572872 | tf_op jit(solution)/shard_map/ppermute | solution.py:41
  35.8 8.6 %collective-permute-start.11 = (f32[2,16,16,256]{3,2,1,0:T(8,128)S(1)}, f32[2,16,16,256]{3,2,1,0:T(8,128)S(1)}, u32[]{:S(2)}, u32[]{:S(2)}) collective-permute-start(f32[2,16,16,256]{3,2,1,0:T(8,128)S(1)} %get-tuple-element.36.refs_0_), channel_id=1, source_target_pairs={{0,1},{1,2},{2,3},{3,4},{4,5},{5,6},{6,7},{7,0},{8,9},{9,10},{10,1... | collective-permute-start | bytes 1572872 | tf_op jit(solution)/shard_map/ppermute | solution.py:41
  36.3 5.0 %collective-permute-start.13 = (f32[2,4,16,256]{3,2,1,0:T(8,128)S(1)}, f32[2,4,16,256]{3,2,1,0:T(8,128)S(1)}, u32[]{:S(2)}, u32[]{:S(2)}) collective-permute-start(f32[2,4,16,256]{3,2,1,0:T(8,128)S(1)} %get-tuple-element.37), channel_id=1, source_target_pairs={{0,32},{1,33},{2,34},{3,35},{4,36},{5,37},{6,38},{7,39},{8,40},{9,... | collective-permute-start | bytes 393224 | tf_op jit(solution)/shard_map/ppermute | solution.py:41
  36.3 7.1 %collective-permute-start.14 = (f32[2,4,16,256]{3,2,1,0:T(8,128)S(1)}, f32[2,4,16,256]{3,2,1,0:T(8,128)S(1)}, u32[]{:S(2)}, u32[]{:S(2)}) collective-permute-start(f32[2,4,16,256]{3,2,1,0:T(8,128)S(1)} %get-tuple-element.38), channel_id=1, source_target_pairs={{0,224},{1,225},{2,226},{3,227},{4,228},{5,229},{6,230},{7,231},{8... | collective-permute-start | bytes 393224 | tf_op jit(solution)/shard_map/ppermute | solution.py:41
  45.4 7.3 %collective-permute-start.15 = (f32[8,16,256]{2,1,0:T(8,128)S(1)}, f32[8,16,256]{2,1,0:T(8,128)S(1)}, u32[]{:S(2)}, u32[]{:S(2)}) collective-permute-start(f32[8,16,256]{2,1,0:T(8,128)S(1)} %get-tuple-element.40), channel_id=1, source_target_pairs={{0,8},{1,9},{2,10},{3,11},{4,12},{5,13},{6,14},{7,15},{8,0},{9,1},... | collective-permute-start | bytes 393224 | tf_op jit(solution)/shard_map/ppermute | solution.py:41
  48.2 7.1 %collective-permute-start.16 = (f32[8,16,256]{2,1,0:T(8,128)S(1)}, f32[8,16,256]{2,1,0:T(8,128)S(1)}, u32[]{:S(2)}, u32[]{:S(2)}) collective-permute-start(f32[8,16,256]{2,1,0:T(8,128)S(1)} %get-tuple-element.41), channel_id=1, source_target_pairs={{0,16},{1,17},{2,18},{3,19},{4,20},{5,21},{6,22},{7,23},{8,24},{9,... | collective-permute-start | bytes 393224 | tf_op jit(solution)/shard_map/ppermute | solution.py:41
  48.9 7.6 %collective-permute-start.17 = (f32[8,16,256]{2,1,0:T(8,128)S(1)}, f32[8,16,256]{2,1,0:T(8,128)S(1)}, u32[]{:S(2)}, u32[]{:S(2)}) collective-permute-start(f32[8,16,256]{2,1,0:T(8,128)S(1)} %get-tuple-element.42), channel_id=1, source_target_pairs={{0,24},{1,25},{2,26},{3,27},{4,28},{5,29},{6,30},{7,31},{8,16},{9,... | collective-permute-start | bytes 393224 | tf_op jit(solution)/shard_map/ppermute | solution.py:41
  58.9 5.0 %collective-permute-start.21 = (f32[64,128]{1,0:T(8,128)S(1)}, f32[64,128]{1,0:T(8,128)S(1)}, u32[]{:S(2)}, u32[]{:S(2)}) collective-permute-start(f32[64,128]{1,0:T(8,128)S(1)} %pad_maximum_fusion), channel_id=1, source_target_pairs={{0,18},{1,19},{2,16},{3,17},{4,22},{5,23},{6,20},{7,21},{8,26},{9,... | collective-permute-start | bytes 98312 | tf_op jit(solution)/shard_map/ppermute | solution.py:208
  64.4 7.3 %collective-permute-start.24 = (f32[64,128]{1,0:T(8,128)S(1)}, f32[64,128]{1,0:T(8,128)S(1)}, u32[]{:S(2)}, u32[]{:S(2)}) collective-permute-start(f32[64,128]{1,0:T(8,128)S(1)} %pad_maximum_fusion.1), channel_id=1, source_target_pairs={{0,30},{1,31},{2,28},{3,29},{4,26},{5,27},{6,24},{7,25},{8,22},{9,... | collective-permute-start | bytes 98312 | tf_op jit(solution)/shard_map/ppermute | solution.py:208
  68.1 5.1 %collective-permute-start.23 = (f32[64,128]{1,0:T(8,128)S(1)}, f32[64,128]{1,0:T(8,128)S(1)}, u32[]{:S(2)}, u32[]{:S(2)}) collective-permute-start(f32[64,128]{1,0:T(8,128)S(1)} %pad_maximum_fusion.1), channel_id=1, source_target_pairs={{0,24},{1,25},{2,26},{3,27},{4,28},{5,29},{6,30},{7,31},{8,16},{9,... | collective-permute-start | bytes 98312 | tf_op jit(solution)/shard_map/ppermute | solution.py:208
  70.4 5.1 %collective-permute-start.22 = (f32[64,128]{1,0:T(8,128)S(1)}, f32[64,128]{1,0:T(8,128)S(1)}, u32[]{:S(2)}, u32[]{:S(2)}) collective-permute-start(f32[64,128]{1,0:T(8,128)S(1)} %pad_maximum_fusion.1), channel_id=1, source_target_pairs={{0,6},{1,7},{2,4},{3,5},{4,2},{5,3},{6,0},{7,1},{8,14},{9,15},{10,... | collective-permute-start | bytes 98312 | tf_op jit(solution)/shard_map/ppermute | solution.py:208
  75.5 5.8 %collective-permute-start.27 = (f32[64,128]{1,0:T(8,128)S(1)}, f32[64,128]{1,0:T(8,128)S(1)}, u32[]{:S(2)}, u32[]{:S(2)}) collective-permute-start(f32[64,128]{1,0:T(8,128)S(1)} %pad_maximum_fusion.2), channel_id=1, source_target_pairs={{0,96},{1,97},{2,98},{3,99},{4,100},{5,101},{6,102},{7,103},{8,104... | collective-permute-start | bytes 98312 | tf_op jit(solution)/shard_map/ppermute | solution.py:208
  83.3 6.1 %collective-permute-start.28 = (f32[64,128]{1,0:T(8,128)S(1)}, f32[64,128]{1,0:T(8,128)S(1)}, u32[]{:S(2)}, u32[]{:S(2)}) collective-permute-start(f32[64,128]{1,0:T(8,128)S(1)} %pad_maximum_fusion.3), channel_id=1, source_target_pairs={{0,192},{1,193},{2,194},{3,195},{4,196},{5,197},{6,198},{7,199},{8... | collective-permute-start | bytes 98312 | tf_op jit(solution)/shard_map/ppermute | solution.py:208
  (8 other events, 44.1 us)

commit v5 on v4

--- a/solution.py
+++ b/solution.py
@@ -86,7 +86,7 @@
     for k, ref in enumerate(parts):
         start = (y_lo ^ (k // 2)) * 8
         f_ref[k % 2, pl.ds(start, 8)] = ref[0:8]
-        v = (ref[8, 0:8, :] - (CENTER + 1.5 * COEFS[0])) * (2.0 / HALF_WIDTH)
+        v = ref[8, 0:8, :]
         for r in range(8):
             v_ref[k % 2, start + r] = jnp.broadcast_to(v[r : r + 1, :], v.shape)
     for p in range(2):
@@ -148,20 +148,21 @@
 
 
 def slices(hi, lo, count, shift, bits):
+    hi = jnp.concatenate([hi, hi], axis=1)
     top = jnp.max(jnp.abs(hi), axis=1, keepdims=True)
     rest, out = hi, []
     for k in range(count):
         if k == 3 and lo is not None:
-            rest = rest + lo
+            rest = rest + jnp.concatenate([lo, lo], axis=1)
         grain = top * (1.5 * 2.0 ** (shift - bits * k))
         part = (rest + grain) - grain
         rest = rest - part
-        out.append(part.astype(jnp.bfloat16))
-    return out, rest
+        out.append(part)
+    return out
 
 
 def gram_kernel(*refs):
-    parts, (x_ref, o_ref) = refs[:4], refs[4:]
+    parts, (z_ref, o_ref, x_ref) = refs[:4], refs[4:]
     rows, m, _ = x_ref.shape
     _, y_lo, y_hi, _, _ = place()
     for k, ref in enumerate(parts):
@@ -180,6 +181,7 @@
         s2 = x.astype(jnp.bfloat16)
         s3 = (x - s2.astype(jnp.float32)).astype(jnp.bfloat16)
         z = jnp.concatenate([s0.astype(jnp.bfloat16), s1.astype(jnp.bfloat16), s2, s3], axis=0)
+        z_ref[r] = z
         part = lax.dot_general(z, z, NT, preferred_element_type=jnp.float32)
         total = part if total is None else total + part
 
@@ -273,21 +275,30 @@
     return jnp.concatenate(out, axis=0)
 
 
-def exact_product(a_parts, b_parts):
-    n, m = len(a_parts), a_parts[0].shape[0]
-    p = lax.dot_general(
-        jnp.concatenate(a_parts, axis=0),
-        jnp.concatenate(b_parts, axis=0),
-        NT,
-        preferred_element_type=jnp.float32,
-    )
+def paired(left, right):
+    lane = lax.broadcasted_iota(jnp.int32, left.shape, 1)
+    return jnp.where(lane < left.shape[1] // 2, left, right).astype(jnp.bfloat16)
+
+
+def left_pairs(parts):
+    return [paired(parts[i], parts[i + 1]) for i in range(0, len(parts), 2)]
+
+
+def right_pairs(parts):
+    before = [jnp.zeros_like(parts[0])] + parts[:-1]
+    return [paired(part, prior) for part, prior in zip(parts, before)]
+
+
+def exact_product(a_pairs, b_pairs):
     hi = lo = None
-    for level in range(n):
-        term = None
-        for i in range(level + 1):
-            j = level - i
-            piece = p[i * m : (i + 1) * m, j * m : (j + 1) * m]
-            term = piece if term is None else term + piece
+    for level in range(len(b_pairs)):
+        used = range(0, level + 1, 2)
+        term = lax.dot_general(
+            jnp.concatenate([a_pairs[i // 2] for i in used], axis=1),
+            jnp.concatenate([b_pairs[level - i] for i in used], axis=1),
+            NT,
+            preferred_element_type=jnp.float32,
+        )
         if hi is None:
             hi, lo = term, jnp.zeros_like(term)
         else:
@@ -296,33 +307,42 @@
     return two_sum(hi, lo)
 
 
-def rotate_kernel(ncount, p_ref, x_ref, o_ref):
-    rows, m, _ = x_ref.shape
+def rotate_kernel(ncount, p_ref, z_ref, o_ref):
+    m, rows, _ = o_ref.shape
     h = m // 2
     hi, lo = p_ref[:h, :] * (1.0 / ncount), p_ref[h:, :] * (1.0 / ncount)
     hi = jnp.concatenate([hi[:, :m], hi[:, m:]], axis=0)
     lo = jnp.concatenate([lo[:, :m], lo[:, m:]], axis=0)
     inverse1 = lower_inverse(hi)
-    w_parts, _ = slices(inverse1, None, 6, 16, 7)
-    g_parts, _ = slices(hi, lo, 6, 16, 7)
-    t_hi, t_lo = exact_product(w_parts, g_parts)
-    t_parts, _ = slices(t_hi, t_lo, 6, 16, 7)
-    gram2, _ = exact_product(t_parts, w_parts)
+    w_parts = slices(inverse1, None, 6, 16, 7)
+    g_parts = slices(hi, lo, 6, 16, 7)
+    t_hi, t_lo = exact_product(left_pairs(w_parts), right_pairs(g_parts))
+    t_parts = slices(t_hi, t_lo, 6, 16, 7)
+    gram2, _ = exact_product(left_pairs(t_parts), right_pairs(w_parts))
     inverse2 = lower_inverse(gram2)
-    both = jnp.dot(inverse2, inverse1, precision=lax.Precision.HIGHEST)
+    rest = jnp.dot(inverse2, inverse1, precision=lax.Precision.HIGHEST)
+    both = []
+    for _ in range(3):
+        both.append(rest.astype(jnp.bfloat16))
+        rest = rest - both[-1].astype(jnp.float32)
+    both = jnp.concatenate([jnp.concatenate([w] * 4, axis=1) for w in both], axis=0)
     for r in range(rows):
-        o_ref[:, r, :] = jnp.dot(both, x_ref[r], precision=lax.Precision.HIGHEST)
+        y = jnp.dot(both, z_ref[r], preferred_element_type=jnp.float32)
+        o_ref[:, r, :] = y[:m] + (y[m : 2 * m] + y[2 * m :])
 
 
 def call(kernel, name, outs, *args, scratch=()):
+    def typed(spec):
+        return spec if isinstance(spec[0], tuple) else (spec, jnp.float32)
+
     single = len(outs) == 1
-    shapes = [jax.ShapeDtypeStruct(shape, jnp.float32) for shape in outs]
+    shapes = [jax.ShapeDtypeStruct(*typed(spec)) for spec in outs]
     return pl.pallas_call(
         kernel,
         out_shape=shapes[0] if single else shapes,
         in_specs=[VMEM] * len(args),
         out_specs=VMEM if single else [VMEM] * len(shapes),
-        scratch_shapes=[pltpu.VMEM(shape, jnp.float32) for shape in scratch],
+        scratch_shapes=[pltpu.VMEM(*typed(spec)) for spec in scratch],
         compiler_params=pltpu.CompilerParams(vmem_limit_bytes=32 << 20),
         name=name,
     )(*args)
@@ -335,7 +355,8 @@
     field = (2, 2 * rows, orbs, lanes)
     face = (2, 4, orbs, lanes)
     matrix = stencil_matrix(lanes // NZ)
-    parts = call(split_kernel, "split", [(rows + 1, orbs, lanes)] * 4, psi, potential)
+    own = (potential - (CENTER + 1.5 * COEFS[0])) * (2.0 / HALF_WIDTH)
+    parts = call(split_kernel, "split", [(rows + 1, orbs, lanes)] * 4, psi, own)
     parts = [parts[0]] + [swap(parts[k], Y_MASKS[k]) for k in (1, 2, 3)]
     joined = [field, (2, 2 * rows, 8, lanes), face, face]
     now, v, face1, face2 = call(join_kernel, "join", joined, *parts)
@@ -351,10 +372,12 @@
         else:
             parts = call(kernel, "level3", [part] * 4, *args, scratch=[field[1:]])
     parts = [parts[0]] + [swap(parts[k], Y_MASKS[k]) for k in (1, 2, 3)]
-    block, local = call(gram_kernel, "gram", [(rows, m, lanes), (m, 2 * m)], *parts)
+    pieces = ((rows, 4 * m, lanes), jnp.bfloat16)
+    whole = [(rows, m, lanes)]
+    pieces, local = call(gram_kernel, "gram", [pieces, (m, 2 * m)], *parts, scratch=whole)
     ncount = float(rows * lanes * lax.axis_size("gx") * lax.axis_size("gy"))
     kernel = functools.partial(rotate_kernel, ncount)
-    return call(kernel, "rotate", [psi.shape], reduce_pairs(local), block)
+    return call(kernel, "rotate", [psi.shape], reduce_pairs(local), pieces)
 
 
 def solution(mesh):

time: 96.7 us -> 95.8 us (level)
  no operation moved by 1% of the time
where the time goes in v5:
time: 95.8 us; the launch traced here: 95.6 us
  starting transfers between devices  44 us (46%)
  waiting for transfers between devices  39.2 us (41%)
  Pallas kernels  10.4 us (11%)
  local copies, waits for them, and re-layouts  1.05 us (1%)
    ppermute x18, waiting for transfers between devices, permute(): return lax.ppermute(x, AXES, [(i, target(i)) for i in range(256)])  26 us
    ppermute x18, starting transfers between devices, permute(): return lax.ppermute(x, AXES, [(i, target(i)) for i in range(256)])  25.5 us
    ppermute x11, starting transfers between devices, swapped(): return lax.ppermute(x, AXES, [(i, i ^ mask) for i in range(256)])  18.5 us
    ppermute x11, waiting for transfers between devices, swapped(): return lax.ppermute(x, AXES, [(i, i ^ mask) for i in range(256)])  13.2 us
    pallas_call x7, Pallas kernels, call(): pl.pallas_call(kernel, out_shape=shapes[0] if single else shapes, in_spec...  10.4 us
  transfers between devices with their start and end apart: 29, of which 22 were waited for; matrix products, arithmetic and copies ran while one was open for 0% of the time, Pallas kernels for 0%

profile of v5, /device:TPU:6, one launch (start us, length us, event | category | flops | bytes accessed | tf_op | source)
XLA Modules:
  0.0 95.6 jit_solution(4725656567328310657)
XLA Ops:
  1.9 3.3 %collective-permute-start = (f32[9,16,256]{2,1,0:T(8,128)S(1)}, f32[9,16,256]{2,1,0:T(8,128)S(1)}, u32[]{:S(2)}, u32[]{:S(2)}) collective-permute-start(f32[9,16,256]{2,1,0:T(8,128)S(1)} %get-tuple-element.26), channel_id=1, source_target_pairs={{0,8},{1,9},{2,10},{3,11},{4,12},{5,13},{6,14},{7,15},{8,0},{9,1},... | collective-permute-start | bytes 442376 | tf_op jit(solution)/shard_map/ppermute | solution.py:41
  6.3 4.0 %collective-permute-done.refs_1_ = f32[9,16,256]{2,1,0:T(8,128)S(1)} collective-permute-done((f32[9,16,256]{2,1,0:T(8,128)S(1)}, f32[9,16,256]{2,1,0:T(8,128)S(1)}, u32[]{:S(2)}, u32[]{:S(2)}) %collective-permute-start) | collective-permute-done | bytes 147488 | tf_op jit(solution)/shard_map/ppermute | solution.py:41
  10.3 2.4 %collective-permute-done.1.refs_2_ = f32[9,16,256]{2,1,0:T(8,128)S(1)} collective-permute-done((f32[9,16,256]{2,1,0:T(8,128)S(1)}, f32[9,16,256]{2,1,0:T(8,128)S(1)}, u32[]{:S(2)}, u32[]{:S(2)}) %collective-permute-start.1) | collective-permute-done | bytes 147488 | tf_op jit(solution)/shard_map/ppermute | solution.py:41
  13.4 1.9 %collective-permute-start.5 = (f32[2,4,16,256]{3,2,1,0:T(8,128)S(1)}, f32[2,4,16,256]{3,2,1,0:T(8,128)S(1)}, u32[]{:S(2)}, u32[]{:S(2)}) collective-permute-start(f32[2,4,16,256]{3,2,1,0:T(8,128)S(1)} %get-tuple-element.30), channel_id=1, source_target_pairs={{0,32},{1,33},{2,34},{3,35},{4,36},{5,37},{6,38},{7,39},{8,40},{9,... | collective-permute-start | bytes 393224 | tf_op jit(solution)/shard_map/ppermute | solution.py:41
  15.3 4.9 %collective-permute-start.6 = (f32[2,4,16,256]{3,2,1,0:T(8,128)S(1)}, f32[2,4,16,256]{3,2,1,0:T(8,128)S(1)}, u32[]{:S(2)}, u32[]{:S(2)}) collective-permute-start(f32[2,4,16,256]{3,2,1,0:T(8,128)S(1)} %get-tuple-element.31), channel_id=1, source_target_pairs={{0,224},{1,225},{2,226},{3,227},{4,228},{5,229},{6,230},{7,231},{8... | collective-permute-start | bytes 393224 | tf_op jit(solution)/shard_map/ppermute | solution.py:41
  20.3 3.9 %collective-permute-done.6.refs_4_ = f32[2,4,16,256]{3,2,1,0:T(8,128)S(1)} collective-permute-done((f32[2,4,16,256]{3,2,1,0:T(8,128)S(1)}, f32[2,4,16,256]{3,2,1,0:T(8,128)S(1)}, u32[]{:S(2)}, u32[]{:S(2)}) %collective-permute-start.6) | collective-permute-done | bytes 131104 | tf_op jit(solution)/shard_map/ppermute | solution.py:41
  25.9 4.0 %collective-permute-start.10 = (f32[2,4,16,256]{3,2,1,0:T(8,128)S(1)}, f32[2,4,16,256]{3,2,1,0:T(8,128)S(1)}, u32[]{:S(2)}, u32[]{:S(2)}) collective-permute-start(f32[2,4,16,256]{3,2,1,0:T(8,128)S(1)} %get-tuple-element.35), channel_id=1, source_target_pairs={{0,224},{1,225},{2,226},{3,227},{4,228},{5,229},{6,230},{7,231},{8... | collective-permute-start | bytes 393224 | tf_op jit(solution)/shard_map/ppermute | solution.py:41
  30.8 2.0 %collective-permute-done.10.refs_4_ = f32[2,4,16,256]{3,2,1,0:T(8,128)S(1)} collective-permute-done((f32[2,4,16,256]{3,2,1,0:T(8,128)S(1)}, f32[2,4,16,256]{3,2,1,0:T(8,128)S(1)}, u32[]{:S(2)}, u32[]{:S(2)}) %collective-permute-start.10) | collective-permute-done | bytes 131104 | tf_op jit(solution)/shard_map/ppermute | solution.py:41
  32.8 1.6 %collective-permute-done.7.refs_1_ = f32[2,16,16,256]{3,2,1,0:T(8,128)S(1)} collective-permute-done((f32[2,16,16,256]{3,2,1,0:T(8,128)S(1)}, f32[2,16,16,256]{3,2,1,0:T(8,128)S(1)}, u32[]{:S(2)}, u32[]{:S(2)}) %collective-permute-start.7) | collective-permute-done | bytes 524320 | tf_op jit(solution)/shard_map/ppermute | solution.py:41
  36.3 4.1 %collective-permute-start.14 = (f32[2,4,16,256]{3,2,1,0:T(8,128)S(1)}, f32[2,4,16,256]{3,2,1,0:T(8,128)S(1)}, u32[]{:S(2)}, u32[]{:S(2)}) collective-permute-start(f32[2,4,16,256]{3,2,1,0:T(8,128)S(1)} %get-tuple-element.38), channel_id=1, source_target_pairs={{0,224},{1,225},{2,226},{3,227},{4,228},{5,229},{6,230},{7,231},{8... | collective-permute-start | bytes 393224 | tf_op jit(solution)/shard_map/ppermute | solution.py:41
  41.3 2.1 %collective-permute-done.14.refs_4_ = f32[2,4,16,256]{3,2,1,0:T(8,128)S(1)} collective-permute-done((f32[2,4,16,256]{3,2,1,0:T(8,128)S(1)}, f32[2,4,16,256]{3,2,1,0:T(8,128)S(1)}, u32[]{:S(2)}, u32[]{:S(2)}) %collective-permute-start.14) | collective-permute-done | bytes 131104 | tf_op jit(solution)/shard_map/ppermute | solution.py:41
  45.4 2.8 %collective-permute-start.15 = (f32[8,16,256]{2,1,0:T(8,128)S(1)}, f32[8,16,256]{2,1,0:T(8,128)S(1)}, u32[]{:S(2)}, u32[]{:S(2)}) collective-permute-start(f32[8,16,256]{2,1,0:T(8,128)S(1)} %get-tuple-element.40), channel_id=1, source_target_pairs={{0,8},{1,9},{2,10},{3,11},{4,12},{5,13},{6,14},{7,15},{8,0},{9,1},... | collective-permute-start | bytes 393224 | tf_op jit(solution)/shard_map/ppermute | solution.py:41
  49.6 3.1 %collective-permute-done.15.refs_1_ = f32[8,16,256]{2,1,0:T(8,128)S(1)} collective-permute-done((f32[8,16,256]{2,1,0:T(8,128)S(1)}, f32[8,16,256]{2,1,0:T(8,128)S(1)}, u32[]{:S(2)}, u32[]{:S(2)}) %collective-permute-start.15) | collective-permute-done | bytes 131104 | tf_op jit(solution)/shard_map/ppermute | solution.py:41
  52.7 2.6 %collective-permute-done.16.refs_2_ = f32[8,16,256]{2,1,0:T(8,128)S(1)} collective-permute-done((f32[8,16,256]{2,1,0:T(8,128)S(1)}, f32[8,16,256]{2,1,0:T(8,128)S(1)}, u32[]{:S(2)}, u32[]{:S(2)}) %collective-permute-start.16) | collective-permute-done | bytes 131104 | tf_op jit(solution)/shard_map/ppermute | solution.py:41
  60.1 2.4 %collective-permute-start.19 = (f32[64,128]{1,0:T(8,128)S(1)}, f32[64,128]{1,0:T(8,128)S(1)}, u32[]{:S(2)}, u32[]{:S(2)}) collective-permute-start(f32[64,128]{1,0:T(8,128)S(1)} %pad_maximum_fusion), channel_id=1, source_target_pairs={{0,2},{1,3},{2,0},{3,1},{4,6},{5,7},{6,4},{7,5},{8,10},{9,11},{10,... | collective-permute-start | bytes 98312 | tf_op jit(solution)/shard_map/ppermute | solution.py:210
  64.4 3.7 %collective-permute-start.24 = (f32[64,128]{1,0:T(8,128)S(1)}, f32[64,128]{1,0:T(8,128)S(1)}, u32[]{:S(2)}, u32[]{:S(2)}) collective-permute-start(f32[64,128]{1,0:T(8,128)S(1)} %pad_maximum_fusion.1), channel_id=1, source_target_pairs={{0,30},{1,31},{2,28},{3,29},{4,26},{5,27},{6,24},{7,25},{8,22},{9,... | collective-permute-start | bytes 98312 | tf_op jit(solution)/shard_map/ppermute | solution.py:210
  68.1 2.3 %collective-permute-start.23 = (f32[64,128]{1,0:T(8,128)S(1)}, f32[64,128]{1,0:T(8,128)S(1)}, u32[]{:S(2)}, u32[]{:S(2)}) collective-permute-start(f32[64,128]{1,0:T(8,128)S(1)} %pad_maximum_fusion.1), channel_id=1, source_target_pairs={{0,24},{1,25},{2,26},{3,27},{4,28},{5,29},{6,30},{7,31},{8,16},{9,... | collective-permute-start | bytes 98312 | tf_op jit(solution)/shard_map/ppermute | solution.py:210
  73.2 2.3 %collective-permute-done.22 = f32[64,128]{1,0:T(8,128)S(1)} collective-permute-done((f32[64,128]{1,0:T(8,128)S(1)}, f32[64,128]{1,0:T(8,128)S(1)}, u32[]{:S(2)}, u32[]{:S(2)}) %collective-permute-start.22) | collective-permute-done | bytes 32800 | tf_op jit(solution)/shard_map/ppermute | solution.py:210
  75.6 2.9 %collective-permute-start.27 = (f32[64,128]{1,0:T(8,128)S(1)}, f32[64,128]{1,0:T(8,128)S(1)}, u32[]{:S(2)}, u32[]{:S(2)}) collective-permute-start(f32[64,128]{1,0:T(8,128)S(1)} %pad_maximum_fusion.2), channel_id=1, source_target_pairs={{0,96},{1,97},{2,98},{3,99},{4,100},{5,101},{6,102},{7,103},{8,104... | collective-permute-start | bytes 98312 | tf_op jit(solution)/shard_map/ppermute | solution.py:210
  78.5 1.5 %collective-permute-start.25 = (f32[64,128]{1,0:T(8,128)S(1)}, f32[64,128]{1,0:T(8,128)S(1)}, u32[]{:S(2)}, u32[]{:S(2)}) collective-permute-start(f32[64,128]{1,0:T(8,128)S(1)} %pad_maximum_fusion.2), channel_id=1, source_target_pairs={{0,32},{1,33},{2,34},{3,35},{4,36},{5,37},{6,38},{7,39},{8,40},{9,... | collective-permute-start | bytes 98312 | tf_op jit(solution)/shard_map/ppermute | solution.py:210
  81.4 1.9 %collective-permute-done.26 = f32[64,128]{1,0:T(8,128)S(1)} collective-permute-done((f32[64,128]{1,0:T(8,128)S(1)}, f32[64,128]{1,0:T(8,128)S(1)}, u32[]{:S(2)}, u32[]{:S(2)}) %collective-permute-start.26) | collective-permute-done | bytes 32800 | tf_op jit(solution)/shard_map/ppermute | solution.py:210
  83.4 4.2 %collective-permute-start.28 = (f32[64,128]{1,0:T(8,128)S(1)}, f32[64,128]{1,0:T(8,128)S(1)}, u32[]{:S(2)}, u32[]{:S(2)}) collective-permute-start(f32[64,128]{1,0:T(8,128)S(1)} %pad_maximum_fusion.3), channel_id=1, source_target_pairs={{0,192},{1,193},{2,194},{3,195},{4,196},{5,197},{6,198},{7,199},{8... | collective-permute-start | bytes 98312 | tf_op jit(solution)/shard_map/ppermute | solution.py:210
  87.6 1.9 %collective-permute-done.28 = f32[64,128]{1,0:T(8,128)S(1)} collective-permute-done((f32[64,128]{1,0:T(8,128)S(1)}, f32[64,128]{1,0:T(8,128)S(1)}, u32[]{:S(2)}, u32[]{:S(2)}) %collective-permute-start.28) | collective-permute-done | bytes 32800 | tf_op jit(solution)/shard_map/ppermute | solution.py:210
  89.5 6.1 %rotate.1 = f32[64,8,256]{2,1,0:T(8,128)} custom-call(f32[64,128]{1,0:T(8,128)S(1)} %pad_maximum_fusion.4.p_ref, bf16[8,256,256]{2,1,0:T(8,128)(2,1)S(1)} %get-tuple-element.44.z_ref), custom_call_target="tpu_custom_call" | custom-call | tf_op jit(solution)/shard_map/rotate/pallas_call | solution.py:340
  (59 shorter events, 23.5 us)
Async XLA Ops:
  1.9 8.3 %collective-permute-start = (f32[9,16,256]{2,1,0:T(8,128)S(1)}, f32[9,16,256]{2,1,0:T(8,128)S(1)}, u32[]{:S(2)}, u32[]{:S(2)}) collective-permute-start(f32[9,16,256]{2,1,0:T(8,128)S(1)} %get-tuple-element.26), channel_id=1, source_target_pairs={{0,8},{1,9},{2,10},{3,11},{4,12},{5,13},{6,14},{7,15},{8,0},{9,1},... | collective-permute-start | bytes 442376 | tf_op jit(solution)/shard_map/ppermute | solution.py:41
  5.2 7.4 %collective-permute-start.1 = (f32[9,16,256]{2,1,0:T(8,128)S(1)}, f32[9,16,256]{2,1,0:T(8,128)S(1)}, u32[]{:S(2)}, u32[]{:S(2)}) collective-permute-start(f32[9,16,256]{2,1,0:T(8,128)S(1)} %get-tuple-element.27), channel_id=1, source_target_pairs={{0,16},{1,17},{2,18},{3,19},{4,20},{5,21},{6,22},{7,23},{8,24},{9,... | collective-permute-start | bytes 442376 | tf_op jit(solution)/shard_map/ppermute | solution.py:41
  5.9 6.9 %collective-permute-start.2 = (f32[9,16,256]{2,1,0:T(8,128)S(1)}, f32[9,16,256]{2,1,0:T(8,128)S(1)}, u32[]{:S(2)}, u32[]{:S(2)}) collective-permute-start(f32[9,16,256]{2,1,0:T(8,128)S(1)} %get-tuple-element.28), channel_id=1, source_target_pairs={{0,24},{1,25},{2,26},{3,27},{4,28},{5,29},{6,30},{7,31},{8,16},{9,... | collective-permute-start | bytes 442376 | tf_op jit(solution)/shard_map/ppermute | solution.py:41
  12.9 11.3 %collective-permute-start.4 = (f32[2,16,16,256]{3,2,1,0:T(8,128)S(1)}, f32[2,16,16,256]{3,2,1,0:T(8,128)S(1)}, u32[]{:S(2)}, u32[]{:S(2)}) collective-permute-start(f32[2,16,16,256]{3,2,1,0:T(8,128)S(1)} %get-tuple-element.29.refs_0_.refs_7_), channel_id=1, source_target_pairs={{0,7},{1,0},{2,1},{3,2},{4,3},{5,4},{6,5},{7,6},{8,15},{9,8},{10,9... | collective-permute-start | bytes 1572872 | tf_op jit(solution)/shard_map/ppermute | solution.py:41
  12.9 11.3 %collective-permute-start.3 = (f32[2,16,16,256]{3,2,1,0:T(8,128)S(1)}, f32[2,16,16,256]{3,2,1,0:T(8,128)S(1)}, u32[]{:S(2)}, u32[]{:S(2)}) collective-permute-start(f32[2,16,16,256]{3,2,1,0:T(8,128)S(1)} %get-tuple-element.29.refs_0_.refs_7_), channel_id=1, source_target_pairs={{0,1},{1,2},{2,3},{3,4},{4,5},{5,6},{6,7},{7,0},{8,9},{9,10},{10,1... | collective-permute-start | bytes 1572872 | tf_op jit(solution)/shard_map/ppermute | solution.py:41
  13.4 6.9 %collective-permute-start.5 = (f32[2,4,16,256]{3,2,1,0:T(8,128)S(1)}, f32[2,4,16,256]{3,2,1,0:T(8,128)S(1)}, u32[]{:S(2)}, u32[]{:S(2)}) collective-permute-start(f32[2,4,16,256]{3,2,1,0:T(8,128)S(1)} %get-tuple-element.30), channel_id=1, source_target_pairs={{0,32},{1,33},{2,34},{3,35},{4,36},{5,37},{6,38},{7,39},{8,40},{9,... | collective-permute-start | bytes 393224 | tf_op jit(solution)/shard_map/ppermute | solution.py:41
  15.3 8.9 %collective-permute-start.6 = (f32[2,4,16,256]{3,2,1,0:T(8,128)S(1)}, f32[2,4,16,256]{3,2,1,0:T(8,128)S(1)}, u32[]{:S(2)}, u32[]{:S(2)}) collective-permute-start(f32[2,4,16,256]{3,2,1,0:T(8,128)S(1)} %get-tuple-element.31), channel_id=1, source_target_pairs={{0,224},{1,225},{2,226},{3,227},{4,228},{5,229},{6,230},{7,231},{8... | collective-permute-start | bytes 393224 | tf_op jit(solution)/shard_map/ppermute | solution.py:41
  25.2 7.6 %collective-permute-start.8 = (f32[2,16,16,256]{3,2,1,0:T(8,128)S(1)}, f32[2,16,16,256]{3,2,1,0:T(8,128)S(1)}, u32[]{:S(2)}, u32[]{:S(2)}) collective-permute-start(f32[2,16,16,256]{3,2,1,0:T(8,128)S(1)} %get-tuple-element.33.refs_0_.refs_7_), channel_id=1, source_target_pairs={{0,7},{1,0},{2,1},{3,2},{4,3},{5,4},{6,5},{7,6},{8,15},{9,8},{10,9... | collective-permute-start | bytes 1572872 | tf_op jit(solution)/shard_map/ppermute | solution.py:41
  25.9 8.6 %collective-permute-start.7 = (f32[2,16,16,256]{3,2,1,0:T(8,128)S(1)}, f32[2,16,16,256]{3,2,1,0:T(8,128)S(1)}, u32[]{:S(2)}, u32[]{:S(2)}) collective-permute-start(f32[2,16,16,256]{3,2,1,0:T(8,128)S(1)} %get-tuple-element.33.refs_0_.refs_7_), channel_id=1, source_target_pairs={{0,1},{1,2},{2,3},{3,4},{4,5},{5,6},{6,7},{7,0},{8,9},{9,10},{10,1... | collective-permute-start | bytes 1572872 | tf_op jit(solution)/shard_map/ppermute | solution.py:41
  25.9 5.0 %collective-permute-start.9 = (f32[2,4,16,256]{3,2,1,0:T(8,128)S(1)}, f32[2,4,16,256]{3,2,1,0:T(8,128)S(1)}, u32[]{:S(2)}, u32[]{:S(2)}) collective-permute-start(f32[2,4,16,256]{3,2,1,0:T(8,128)S(1)} %get-tuple-element.34), channel_id=1, source_target_pairs={{0,32},{1,33},{2,34},{3,35},{4,36},{5,37},{6,38},{7,39},{8,40},{9,... | collective-permute-start | bytes 393224 | tf_op jit(solution)/shard_map/ppermute | solution.py:41
  25.9 6.9 %collective-permute-start.10 = (f32[2,4,16,256]{3,2,1,0:T(8,128)S(1)}, f32[2,4,16,256]{3,2,1,0:T(8,128)S(1)}, u32[]{:S(2)}, u32[]{:S(2)}) collective-permute-start(f32[2,4,16,256]{3,2,1,0:T(8,128)S(1)} %get-tuple-element.35), channel_id=1, source_target_pairs={{0,224},{1,225},{2,226},{3,227},{4,228},{5,229},{6,230},{7,231},{8... | collective-permute-start | bytes 393224 | tf_op jit(solution)/shard_map/ppermute | solution.py:41
  35.5 7.9 %collective-permute-start.12 = (f32[2,16,16,256]{3,2,1,0:T(8,128)S(1)}, f32[2,16,16,256]{3,2,1,0:T(8,128)S(1)}, u32[]{:S(2)}, u32[]{:S(2)}) collective-permute-start(f32[2,16,16,256]{3,2,1,0:T(8,128)S(1)} %get-tuple-element.36.refs_0_), channel_id=1, source_target_pairs={{0,7},{1,0},{2,1},{3,2},{4,3},{5,4},{6,5},{7,6},{8,15},{9,8},{10,9... | collective-permute-start | bytes 1572872 | tf_op jit(solution)/shard_map/ppermute | solution.py:41
  35.8 8.6 %collective-permute-start.11 = (f32[2,16,16,256]{3,2,1,0:T(8,128)S(1)}, f32[2,16,16,256]{3,2,1,0:T(8,128)S(1)}, u32[]{:S(2)}, u32[]{:S(2)}) collective-permute-start(f32[2,16,16,256]{3,2,1,0:T(8,128)S(1)} %get-tuple-element.36.refs_0_), channel_id=1, source_target_pairs={{0,1},{1,2},{2,3},{3,4},{4,5},{5,6},{6,7},{7,0},{8,9},{9,10},{10,1... | collective-permute-start | bytes 1572872 | tf_op jit(solution)/shard_map/ppermute | solution.py:41
  36.3 5.0 %collective-permute-start.13 = (f32[2,4,16,256]{3,2,1,0:T(8,128)S(1)}, f32[2,4,16,256]{3,2,1,0:T(8,128)S(1)}, u32[]{:S(2)}, u32[]{:S(2)}) collective-permute-start(f32[2,4,16,256]{3,2,1,0:T(8,128)S(1)} %get-tuple-element.37), channel_id=1, source_target_pairs={{0,32},{1,33},{2,34},{3,35},{4,36},{5,37},{6,38},{7,39},{8,40},{9,... | collective-permute-start | bytes 393224 | tf_op jit(solution)/shard_map/ppermute | solution.py:41
  36.3 7.1 %collective-permute-start.14 = (f32[2,4,16,256]{3,2,1,0:T(8,128)S(1)}, f32[2,4,16,256]{3,2,1,0:T(8,128)S(1)}, u32[]{:S(2)}, u32[]{:S(2)}) collective-permute-start(f32[2,4,16,256]{3,2,1,0:T(8,128)S(1)} %get-tuple-element.38), channel_id=1, source_target_pairs={{0,224},{1,225},{2,226},{3,227},{4,228},{5,229},{6,230},{7,231},{8... | collective-permute-start | bytes 393224 | tf_op jit(solution)/shard_map/ppermute | solution.py:41
  45.4 7.3 %collective-permute-start.15 = (f32[8,16,256]{2,1,0:T(8,128)S(1)}, f32[8,16,256]{2,1,0:T(8,128)S(1)}, u32[]{:S(2)}, u32[]{:S(2)}) collective-permute-start(f32[8,16,256]{2,1,0:T(8,128)S(1)} %get-tuple-element.40), channel_id=1, source_target_pairs={{0,8},{1,9},{2,10},{3,11},{4,12},{5,13},{6,14},{7,15},{8,0},{9,1},... | collective-permute-start | bytes 393224 | tf_op jit(solution)/shard_map/ppermute | solution.py:41
  48.2 7.1 %collective-permute-start.16 = (f32[8,16,256]{2,1,0:T(8,128)S(1)}, f32[8,16,256]{2,1,0:T(8,128)S(1)}, u32[]{:S(2)}, u32[]{:S(2)}) collective-permute-start(f32[8,16,256]{2,1,0:T(8,128)S(1)} %get-tuple-element.41), channel_id=1, source_target_pairs={{0,16},{1,17},{2,18},{3,19},{4,20},{5,21},{6,22},{7,23},{8,24},{9,... | collective-permute-start | bytes 393224 | tf_op jit(solution)/shard_map/ppermute | solution.py:41
  48.9 7.6 %collective-permute-start.17 = (f32[8,16,256]{2,1,0:T(8,128)S(1)}, f32[8,16,256]{2,1,0:T(8,128)S(1)}, u32[]{:S(2)}, u32[]{:S(2)}) collective-permute-start(f32[8,16,256]{2,1,0:T(8,128)S(1)} %get-tuple-element.42), channel_id=1, source_target_pairs={{0,24},{1,25},{2,26},{3,27},{4,28},{5,29},{6,30},{7,31},{8,16},{9,... | collective-permute-start | bytes 393224 | tf_op jit(solution)/shard_map/ppermute | solution.py:41
  58.9 5.0 %collective-permute-start.21 = (f32[64,128]{1,0:T(8,128)S(1)}, f32[64,128]{1,0:T(8,128)S(1)}, u32[]{:S(2)}, u32[]{:S(2)}) collective-permute-start(f32[64,128]{1,0:T(8,128)S(1)} %pad_maximum_fusion), channel_id=1, source_target_pairs={{0,18},{1,19},{2,16},{3,17},{4,22},{5,23},{6,20},{7,21},{8,26},{9,... | collective-permute-start | bytes 98312 | tf_op jit(solution)/shard_map/ppermute | solution.py:210
  64.4 7.3 %collective-permute-start.24 = (f32[64,128]{1,0:T(8,128)S(1)}, f32[64,128]{1,0:T(8,128)S(1)}, u32[]{:S(2)}, u32[]{:S(2)}) collective-permute-start(f32[64,128]{1,0:T(8,128)S(1)} %pad_maximum_fusion.1), channel_id=1, source_target_pairs={{0,30},{1,31},{2,28},{3,29},{4,26},{5,27},{6,24},{7,25},{8,22},{9,... | collective-permute-start | bytes 98312 | tf_op jit(solution)/shard_map/ppermute | solution.py:210
  68.1 5.1 %collective-permute-start.23 = (f32[64,128]{1,0:T(8,128)S(1)}, f32[64,128]{1,0:T(8,128)S(1)}, u32[]{:S(2)}, u32[]{:S(2)}) collective-permute-start(f32[64,128]{1,0:T(8,128)S(1)} %pad_maximum_fusion.1), channel_id=1, source_target_pairs={{0,24},{1,25},{2,26},{3,27},{4,28},{5,29},{6,30},{7,31},{8,16},{9,... | collective-permute-start | bytes 98312 | tf_op jit(solution)/shard_map/ppermute | solution.py:210
  70.4 5.1 %collective-permute-start.22 = (f32[64,128]{1,0:T(8,128)S(1)}, f32[64,128]{1,0:T(8,128)S(1)}, u32[]{:S(2)}, u32[]{:S(2)}) collective-permute-start(f32[64,128]{1,0:T(8,128)S(1)} %pad_maximum_fusion.1), channel_id=1, source_target_pairs={{0,6},{1,7},{2,4},{3,5},{4,2},{5,3},{6,0},{7,1},{8,14},{9,15},{10,... | collective-permute-start | bytes 98312 | tf_op jit(solution)/shard_map/ppermute | solution.py:210
  75.6 5.8 %collective-permute-start.27 = (f32[64,128]{1,0:T(8,128)S(1)}, f32[64,128]{1,0:T(8,128)S(1)}, u32[]{:S(2)}, u32[]{:S(2)}) collective-permute-start(f32[64,128]{1,0:T(8,128)S(1)} %pad_maximum_fusion.2), channel_id=1, source_target_pairs={{0,96},{1,97},{2,98},{3,99},{4,100},{5,101},{6,102},{7,103},{8,104... | collective-permute-start | bytes 98312 | tf_op jit(solution)/shard_map/ppermute | solution.py:210
  83.4 6.1 %collective-permute-start.28 = (f32[64,128]{1,0:T(8,128)S(1)}, f32[64,128]{1,0:T(8,128)S(1)}, u32[]{:S(2)}, u32[]{:S(2)}) collective-permute-start(f32[64,128]{1,0:T(8,128)S(1)} %pad_maximum_fusion.3), channel_id=1, source_target_pairs={{0,192},{1,193},{2,194},{3,195},{4,196},{5,197},{6,198},{7,199},{8... | collective-permute-start | bytes 98312 | tf_op jit(solution)/shard_map/ppermute | solution.py:210
  (7 other events, 43.4 us)

commit v6 on v5

--- a/solution.py
+++ b/solution.py
@@ -68,9 +68,9 @@
     for k, o_ref in enumerate(o_refs):
         q = (y_lo ^ (k // 2)) * 2 + (y_hi ^ (k % 2))
         for r in range(8):
-            o_ref[r] = x_ref[pl.ds(q * part, part), r, :]
-        o_ref[8, 0:8, :] = v_ref[...]
-        o_ref[8, 8:16, :] = v_ref[...]
+            x = x_ref[pl.ds(q * part, part), r, :]
+            o_ref[2 * r : 2 * r + 2] = x.reshape(2, 8, x.shape[1])
+        o_ref[16] = v_ref[...]
 
 
 def send_faces(even, field, p, f1_ref, f2_ref):
@@ -85,8 +85,8 @@
     even = z % 2 == 0
     for k, ref in enumerate(parts):
         start = (y_lo ^ (k // 2)) * 8
-        f_ref[k % 2, pl.ds(start, 8)] = ref[0:8]
-        v = ref[8, 0:8, :]
+        f_ref[k % 2, pl.ds(start, 8)] = ref[0:16].reshape(8, *f_ref.shape[2:])
+        v = ref[16]
         for r in range(8):
             v_ref[k % 2, start + r] = jnp.broadcast_to(v[r : r + 1, :], v.shape)
     for p in range(2):
@@ -209,7 +209,7 @@
     def swapped(mask):
         return lax.ppermute(x, AXES, [(i, i ^ mask) for i in range(256)])
 
-    for masks in ((1,), (2, 16, 18), (6, 24, 30), (32, 64, 96), (192,)):
+    for masks in ((1,), (2, 32, 34), (16, 64, 80), (6, 24, 30), (192,)):
         if len(masks) == 1:
             x = pair_add(x, swapped(masks[0]))
         else:
@@ -356,7 +356,7 @@
     face = (2, 4, orbs, lanes)
     matrix = stencil_matrix(lanes // NZ)
     own = (potential - (CENTER + 1.5 * COEFS[0])) * (2.0 / HALF_WIDTH)
-    parts = call(split_kernel, "split", [(rows + 1, orbs, lanes)] * 4, psi, own)
+    parts = call(split_kernel, "split", [(2 * rows + 1, 8, lanes)] * 4, psi, own)
     parts = [parts[0]] + [swap(parts[k], Y_MASKS[k]) for k in (1, 2, 3)]
     joined = [field, (2, 2 * rows, 8, lanes), face, face]
     now, v, face1, face2 = call(join_kernel, "join", joined, *parts)

time: 95.8 us -> 94.5 us (0.986)
  waiting for transfers between devices: 39.2 us -> 38 us
    ppermute x11, waiting for transfers between devices: 13.2 us -> 12.1 us  [swapped(): return lax.ppermute(x, AXES, [(i, i ^ mask) for i in range(256)])]
where the time goes in v6:
time: 94.5 us; the launch traced here: 94.4 us
  starting transfers between devices  43.9 us (46%)
  waiting for transfers between devices  38 us (40%)
  Pallas kernels  10.4 us (11%)
  local copies, waits for them, and re-layouts  1.05 us (1%)
    ppermute x18, waiting for transfers between devices, permute(): return lax.ppermute(x, AXES, [(i, target(i)) for i in range(256)])  25.9 us
    ppermute x18, starting transfers between devices, permute(): return lax.ppermute(x, AXES, [(i, target(i)) for i in range(256)])  25.3 us
    ppermute x11, starting transfers between devices, swapped(): return lax.ppermute(x, AXES, [(i, i ^ mask) for i in range(256)])  18.6 us
    ppermute x11, waiting for transfers between devices, swapped(): return lax.ppermute(x, AXES, [(i, i ^ mask) for i in range(256)])  12.1 us
    pallas_call x7, Pallas kernels, call(): pl.pallas_call(kernel, out_shape=shapes[0] if single else shapes, in_spec...  10.4 us
  transfers between devices with their start and end apart: 29, of which 22 were waited for; matrix products, arithmetic and copies ran while one was open for 0% of the time, Pallas kernels for 0%

profile of v6, /device:TPU:6, one launch (start us, length us, event | category | flops | bytes accessed | tf_op | source)
XLA Modules:
  0.0 94.4 jit_solution(4691008584504065951)
XLA Ops:
  1.9 3.3 %collective-permute-start = (f32[17,8,256]{2,1,0:T(8,128)S(1)}, f32[17,8,256]{2,1,0:T(8,128)S(1)}, u32[]{:S(2)}, u32[]{:S(2)}) collective-permute-start(f32[17,8,256]{2,1,0:T(8,128)S(1)} %get-tuple-element.26), channel_id=1, source_target_pairs={{0,8},{1,9},{2,10},{3,11},{4,12},{5,13},{6,14},{7,15},{8,0},{9,1},... | collective-permute-start | bytes 417800 | tf_op jit(solution)/shard_map/ppermute | solution.py:41
  6.3 3.8 %collective-permute-done.refs_1_ = f32[17,8,256]{2,1,0:T(8,128)S(1)} collective-permute-done((f32[17,8,256]{2,1,0:T(8,128)S(1)}, f32[17,8,256]{2,1,0:T(8,128)S(1)}, u32[]{:S(2)}, u32[]{:S(2)}) %collective-permute-start) | collective-permute-done | bytes 139296 | tf_op jit(solution)/shard_map/ppermute | solution.py:41
  10.0 2.2 %collective-permute-done.1.refs_2_ = f32[17,8,256]{2,1,0:T(8,128)S(1)} collective-permute-done((f32[17,8,256]{2,1,0:T(8,128)S(1)}, f32[17,8,256]{2,1,0:T(8,128)S(1)}, u32[]{:S(2)}, u32[]{:S(2)}) %collective-permute-start.1) | collective-permute-done | bytes 139296 | tf_op jit(solution)/shard_map/ppermute | solution.py:41
  13.1 1.9 %collective-permute-start.5 = (f32[2,4,16,256]{3,2,1,0:T(8,128)S(1)}, f32[2,4,16,256]{3,2,1,0:T(8,128)S(1)}, u32[]{:S(2)}, u32[]{:S(2)}) collective-permute-start(f32[2,4,16,256]{3,2,1,0:T(8,128)S(1)} %get-tuple-element.30), channel_id=1, source_target_pairs={{0,32},{1,33},{2,34},{3,35},{4,36},{5,37},{6,38},{7,39},{8,40},{9,... | collective-permute-start | bytes 393224 | tf_op jit(solution)/shard_map/ppermute | solution.py:41
  15.0 4.9 %collective-permute-start.6 = (f32[2,4,16,256]{3,2,1,0:T(8,128)S(1)}, f32[2,4,16,256]{3,2,1,0:T(8,128)S(1)}, u32[]{:S(2)}, u32[]{:S(2)}) collective-permute-start(f32[2,4,16,256]{3,2,1,0:T(8,128)S(1)} %get-tuple-element.31), channel_id=1, source_target_pairs={{0,224},{1,225},{2,226},{3,227},{4,228},{5,229},{6,230},{7,231},{8... | collective-permute-start | bytes 393224 | tf_op jit(solution)/shard_map/ppermute | solution.py:41
  20.0 4.1 %collective-permute-done.6.refs_4_ = f32[2,4,16,256]{3,2,1,0:T(8,128)S(1)} collective-permute-done((f32[2,4,16,256]{3,2,1,0:T(8,128)S(1)}, f32[2,4,16,256]{3,2,1,0:T(8,128)S(1)}, u32[]{:S(2)}, u32[]{:S(2)}) %collective-permute-start.6) | collective-permute-done | bytes 131104 | tf_op jit(solution)/shard_map/ppermute | solution.py:41
  25.6 4.0 %collective-permute-start.10 = (f32[2,4,16,256]{3,2,1,0:T(8,128)S(1)}, f32[2,4,16,256]{3,2,1,0:T(8,128)S(1)}, u32[]{:S(2)}, u32[]{:S(2)}) collective-permute-start(f32[2,4,16,256]{3,2,1,0:T(8,128)S(1)} %get-tuple-element.35), channel_id=1, source_target_pairs={{0,224},{1,225},{2,226},{3,227},{4,228},{5,229},{6,230},{7,231},{8... | collective-permute-start | bytes 393224 | tf_op jit(solution)/shard_map/ppermute | solution.py:41
  30.6 2.0 %collective-permute-done.10.refs_4_ = f32[2,4,16,256]{3,2,1,0:T(8,128)S(1)} collective-permute-done((f32[2,4,16,256]{3,2,1,0:T(8,128)S(1)}, f32[2,4,16,256]{3,2,1,0:T(8,128)S(1)}, u32[]{:S(2)}, u32[]{:S(2)}) %collective-permute-start.10) | collective-permute-done | bytes 131104 | tf_op jit(solution)/shard_map/ppermute | solution.py:41
  32.6 1.6 %collective-permute-done.7.refs_1_ = f32[2,16,16,256]{3,2,1,0:T(8,128)S(1)} collective-permute-done((f32[2,16,16,256]{3,2,1,0:T(8,128)S(1)}, f32[2,16,16,256]{3,2,1,0:T(8,128)S(1)}, u32[]{:S(2)}, u32[]{:S(2)}) %collective-permute-start.7) | collective-permute-done | bytes 524320 | tf_op jit(solution)/shard_map/ppermute | solution.py:41
  36.0 4.0 %collective-permute-start.14 = (f32[2,4,16,256]{3,2,1,0:T(8,128)S(1)}, f32[2,4,16,256]{3,2,1,0:T(8,128)S(1)}, u32[]{:S(2)}, u32[]{:S(2)}) collective-permute-start(f32[2,4,16,256]{3,2,1,0:T(8,128)S(1)} %get-tuple-element.38), channel_id=1, source_target_pairs={{0,224},{1,225},{2,226},{3,227},{4,228},{5,229},{6,230},{7,231},{8... | collective-permute-start | bytes 393224 | tf_op jit(solution)/shard_map/ppermute | solution.py:41
  41.0 2.0 %collective-permute-done.14.refs_4_ = f32[2,4,16,256]{3,2,1,0:T(8,128)S(1)} collective-permute-done((f32[2,4,16,256]{3,2,1,0:T(8,128)S(1)}, f32[2,4,16,256]{3,2,1,0:T(8,128)S(1)}, u32[]{:S(2)}, u32[]{:S(2)}) %collective-permute-start.14) | collective-permute-done | bytes 131104 | tf_op jit(solution)/shard_map/ppermute | solution.py:41
  45.2 2.7 %collective-permute-start.15 = (f32[8,16,256]{2,1,0:T(8,128)S(1)}, f32[8,16,256]{2,1,0:T(8,128)S(1)}, u32[]{:S(2)}, u32[]{:S(2)}) collective-permute-start(f32[8,16,256]{2,1,0:T(8,128)S(1)} %get-tuple-element.40), channel_id=1, source_target_pairs={{0,8},{1,9},{2,10},{3,11},{4,12},{5,13},{6,14},{7,15},{8,0},{9,1},... | collective-permute-start | bytes 393224 | tf_op jit(solution)/shard_map/ppermute | solution.py:41
  49.3 3.1 %collective-permute-done.15.refs_1_ = f32[8,16,256]{2,1,0:T(8,128)S(1)} collective-permute-done((f32[8,16,256]{2,1,0:T(8,128)S(1)}, f32[8,16,256]{2,1,0:T(8,128)S(1)}, u32[]{:S(2)}, u32[]{:S(2)}) %collective-permute-start.15) | collective-permute-done | bytes 131104 | tf_op jit(solution)/shard_map/ppermute | solution.py:41
  52.4 2.5 %collective-permute-done.16.refs_2_ = f32[8,16,256]{2,1,0:T(8,128)S(1)} collective-permute-done((f32[8,16,256]{2,1,0:T(8,128)S(1)}, f32[8,16,256]{2,1,0:T(8,128)S(1)}, u32[]{:S(2)}, u32[]{:S(2)}) %collective-permute-start.16) | collective-permute-done | bytes 131104 | tf_op jit(solution)/shard_map/ppermute | solution.py:41
  59.6 2.6 %collective-permute-start.19 = (f32[64,128]{1,0:T(8,128)S(1)}, f32[64,128]{1,0:T(8,128)S(1)}, u32[]{:S(2)}, u32[]{:S(2)}) collective-permute-start(f32[64,128]{1,0:T(8,128)S(1)} %pad_maximum_fusion), channel_id=1, source_target_pairs={{0,2},{1,3},{2,0},{3,1},{4,6},{5,7},{6,4},{7,5},{8,10},{9,11},{10,... | collective-permute-start | bytes 98312 | tf_op jit(solution)/shard_map/ppermute | solution.py:210
  65.3 2.1 %collective-permute-start.23 = (f32[64,128]{1,0:T(8,128)S(1)}, f32[64,128]{1,0:T(8,128)S(1)}, u32[]{:S(2)}, u32[]{:S(2)}) collective-permute-start(f32[64,128]{1,0:T(8,128)S(1)} %pad_maximum_fusion.1), channel_id=1, source_target_pairs={{0,64},{1,65},{2,66},{3,67},{4,68},{5,69},{6,70},{7,71},{8,72},{9,... | collective-permute-start | bytes 98312 | tf_op jit(solution)/shard_map/ppermute | solution.py:210
  68.6 1.9 %collective-permute-done.24 = f32[64,128]{1,0:T(8,128)S(1)} collective-permute-done((f32[64,128]{1,0:T(8,128)S(1)}, f32[64,128]{1,0:T(8,128)S(1)}, u32[]{:S(2)}, u32[]{:S(2)}) %collective-permute-start.24) | collective-permute-done | bytes 32800 | tf_op jit(solution)/shard_map/ppermute | solution.py:210
  71.3 3.5 %collective-permute-start.27 = (f32[64,128]{1,0:T(8,128)S(1)}, f32[64,128]{1,0:T(8,128)S(1)}, u32[]{:S(2)}, u32[]{:S(2)}) collective-permute-start(f32[64,128]{1,0:T(8,128)S(1)} %pad_maximum_fusion.2), channel_id=1, source_target_pairs={{0,30},{1,31},{2,28},{3,29},{4,26},{5,27},{6,24},{7,25},{8,22},{9,... | collective-permute-start | bytes 98312 | tf_op jit(solution)/shard_map/ppermute | solution.py:210
  74.9 1.9 %collective-permute-start.26 = (f32[64,128]{1,0:T(8,128)S(1)}, f32[64,128]{1,0:T(8,128)S(1)}, u32[]{:S(2)}, u32[]{:S(2)}) collective-permute-start(f32[64,128]{1,0:T(8,128)S(1)} %pad_maximum_fusion.2), channel_id=1, source_target_pairs={{0,24},{1,25},{2,26},{3,27},{4,28},{5,29},{6,30},{7,31},{8,16},{9,... | collective-permute-start | bytes 98312 | tf_op jit(solution)/shard_map/ppermute | solution.py:210
  77.3 1.7 %collective-permute-done.27 = f32[64,128]{1,0:T(8,128)S(1)} collective-permute-done((f32[64,128]{1,0:T(8,128)S(1)}, f32[64,128]{1,0:T(8,128)S(1)}, u32[]{:S(2)}, u32[]{:S(2)}) %collective-permute-start.27) | collective-permute-done | bytes 32800 | tf_op jit(solution)/shard_map/ppermute | solution.py:210
  80.0 1.9 %collective-permute-done.25 = f32[64,128]{1,0:T(8,128)S(1)} collective-permute-done((f32[64,128]{1,0:T(8,128)S(1)}, f32[64,128]{1,0:T(8,128)S(1)}, u32[]{:S(2)}, u32[]{:S(2)}) %collective-permute-start.25) | collective-permute-done | bytes 32800 | tf_op jit(solution)/shard_map/ppermute | solution.py:210
  82.0 4.4 %collective-permute-start.28 = (f32[64,128]{1,0:T(8,128)S(1)}, f32[64,128]{1,0:T(8,128)S(1)}, u32[]{:S(2)}, u32[]{:S(2)}) collective-permute-start(f32[64,128]{1,0:T(8,128)S(1)} %pad_maximum_fusion.3), channel_id=1, source_target_pairs={{0,192},{1,193},{2,194},{3,195},{4,196},{5,197},{6,198},{7,199},{8... | collective-permute-start | bytes 98312 | tf_op jit(solution)/shard_map/ppermute | solution.py:210
  86.3 1.9 %collective-permute-done.28 = f32[64,128]{1,0:T(8,128)S(1)} collective-permute-done((f32[64,128]{1,0:T(8,128)S(1)}, f32[64,128]{1,0:T(8,128)S(1)}, u32[]{:S(2)}, u32[]{:S(2)}) %collective-permute-start.28) | collective-permute-done | bytes 32800 | tf_op jit(solution)/shard_map/ppermute | solution.py:210
  88.3 6.1 %rotate.1 = f32[64,8,256]{2,1,0:T(8,128)} custom-call(f32[64,128]{1,0:T(8,128)S(1)} %pad_maximum_fusion.4.p_ref, bf16[8,256,256]{2,1,0:T(8,128)(2,1)S(1)} %get-tuple-element.44.z_ref), custom_call_target="tpu_custom_call" | custom-call | tf_op jit(solution)/shard_map/rotate/pallas_call | solution.py:340
  (59 shorter events, 24.2 us)
Async XLA Ops:
  1.9 8.1 %collective-permute-start = (f32[17,8,256]{2,1,0:T(8,128)S(1)}, f32[17,8,256]{2,1,0:T(8,128)S(1)}, u32[]{:S(2)}, u32[]{:S(2)}) collective-permute-start(f32[17,8,256]{2,1,0:T(8,128)S(1)} %get-tuple-element.26), channel_id=1, source_target_pairs={{0,8},{1,9},{2,10},{3,11},{4,12},{5,13},{6,14},{7,15},{8,0},{9,1},... | collective-permute-start | bytes 417800 | tf_op jit(solution)/shard_map/ppermute | solution.py:41
  5.2 7.0 %collective-permute-start.1 = (f32[17,8,256]{2,1,0:T(8,128)S(1)}, f32[17,8,256]{2,1,0:T(8,128)S(1)}, u32[]{:S(2)}, u32[]{:S(2)}) collective-permute-start(f32[17,8,256]{2,1,0:T(8,128)S(1)} %get-tuple-element.27), channel_id=1, source_target_pairs={{0,16},{1,17},{2,18},{3,19},{4,20},{5,21},{6,22},{7,23},{8,24},{9,... | collective-permute-start | bytes 417800 | tf_op jit(solution)/shard_map/ppermute | solution.py:41
  5.9 6.6 %collective-permute-start.2 = (f32[17,8,256]{2,1,0:T(8,128)S(1)}, f32[17,8,256]{2,1,0:T(8,128)S(1)}, u32[]{:S(2)}, u32[]{:S(2)}) collective-permute-start(f32[17,8,256]{2,1,0:T(8,128)S(1)} %get-tuple-element.28), channel_id=1, source_target_pairs={{0,24},{1,25},{2,26},{3,27},{4,28},{5,29},{6,30},{7,31},{8,16},{9,... | collective-permute-start | bytes 417800 | tf_op jit(solution)/shard_map/ppermute | solution.py:41
  12.6 11.5 %collective-permute-start.4 = (f32[2,16,16,256]{3,2,1,0:T(8,128)S(1)}, f32[2,16,16,256]{3,2,1,0:T(8,128)S(1)}, u32[]{:S(2)}, u32[]{:S(2)}) collective-permute-start(f32[2,16,16,256]{3,2,1,0:T(8,128)S(1)} %get-tuple-element.29.refs_0_.refs_7_), channel_id=1, source_target_pairs={{0,7},{1,0},{2,1},{3,2},{4,3},{5,4},{6,5},{7,6},{8,15},{9,8},{10,9... | collective-permute-start | bytes 1572872 | tf_op jit(solution)/shard_map/ppermute | solution.py:41
  12.6 11.4 %collective-permute-start.3 = (f32[2,16,16,256]{3,2,1,0:T(8,128)S(1)}, f32[2,16,16,256]{3,2,1,0:T(8,128)S(1)}, u32[]{:S(2)}, u32[]{:S(2)}) collective-permute-start(f32[2,16,16,256]{3,2,1,0:T(8,128)S(1)} %get-tuple-element.29.refs_0_.refs_7_), channel_id=1, source_target_pairs={{0,1},{1,2},{2,3},{3,4},{4,5},{5,6},{6,7},{7,0},{8,9},{9,10},{10,1... | collective-permute-start | bytes 1572872 | tf_op jit(solution)/shard_map/ppermute | solution.py:41
  13.1 6.9 %collective-permute-start.5 = (f32[2,4,16,256]{3,2,1,0:T(8,128)S(1)}, f32[2,4,16,256]{3,2,1,0:T(8,128)S(1)}, u32[]{:S(2)}, u32[]{:S(2)}) collective-permute-start(f32[2,4,16,256]{3,2,1,0:T(8,128)S(1)} %get-tuple-element.30), channel_id=1, source_target_pairs={{0,32},{1,33},{2,34},{3,35},{4,36},{5,37},{6,38},{7,39},{8,40},{9,... | collective-permute-start | bytes 393224 | tf_op jit(solution)/shard_map/ppermute | solution.py:41
  15.0 9.0 %collective-permute-start.6 = (f32[2,4,16,256]{3,2,1,0:T(8,128)S(1)}, f32[2,4,16,256]{3,2,1,0:T(8,128)S(1)}, u32[]{:S(2)}, u32[]{:S(2)}) collective-permute-start(f32[2,4,16,256]{3,2,1,0:T(8,128)S(1)} %get-tuple-element.31), channel_id=1, source_target_pairs={{0,224},{1,225},{2,226},{3,227},{4,228},{5,229},{6,230},{7,231},{8... | collective-permute-start | bytes 393224 | tf_op jit(solution)/shard_map/ppermute | solution.py:41
  25.1 7.5 %collective-permute-start.8 = (f32[2,16,16,256]{3,2,1,0:T(8,128)S(1)}, f32[2,16,16,256]{3,2,1,0:T(8,128)S(1)}, u32[]{:S(2)}, u32[]{:S(2)}) collective-permute-start(f32[2,16,16,256]{3,2,1,0:T(8,128)S(1)} %get-tuple-element.33.refs_0_.refs_7_), channel_id=1, source_target_pairs={{0,7},{1,0},{2,1},{3,2},{4,3},{5,4},{6,5},{7,6},{8,15},{9,8},{10,9... | collective-permute-start | bytes 1572872 | tf_op jit(solution)/shard_map/ppermute | solution.py:41
  25.6 8.6 %collective-permute-start.7 = (f32[2,16,16,256]{3,2,1,0:T(8,128)S(1)}, f32[2,16,16,256]{3,2,1,0:T(8,128)S(1)}, u32[]{:S(2)}, u32[]{:S(2)}) collective-permute-start(f32[2,16,16,256]{3,2,1,0:T(8,128)S(1)} %get-tuple-element.33.refs_0_.refs_7_), channel_id=1, source_target_pairs={{0,1},{1,2},{2,3},{3,4},{4,5},{5,6},{6,7},{7,0},{8,9},{9,10},{10,1... | collective-permute-start | bytes 1572872 | tf_op jit(solution)/shard_map/ppermute | solution.py:41
  25.6 5.0 %collective-permute-start.9 = (f32[2,4,16,256]{3,2,1,0:T(8,128)S(1)}, f32[2,4,16,256]{3,2,1,0:T(8,128)S(1)}, u32[]{:S(2)}, u32[]{:S(2)}) collective-permute-start(f32[2,4,16,256]{3,2,1,0:T(8,128)S(1)} %get-tuple-element.34), channel_id=1, source_target_pairs={{0,32},{1,33},{2,34},{3,35},{4,36},{5,37},{6,38},{7,39},{8,40},{9,... | collective-permute-start | bytes 393224 | tf_op jit(solution)/shard_map/ppermute | solution.py:41
  25.6 7.0 %collective-permute-start.10 = (f32[2,4,16,256]{3,2,1,0:T(8,128)S(1)}, f32[2,4,16,256]{3,2,1,0:T(8,128)S(1)}, u32[]{:S(2)}, u32[]{:S(2)}) collective-permute-start(f32[2,4,16,256]{3,2,1,0:T(8,128)S(1)} %get-tuple-element.35), channel_id=1, source_target_pairs={{0,224},{1,225},{2,226},{3,227},{4,228},{5,229},{6,230},{7,231},{8... | collective-permute-start | bytes 393224 | tf_op jit(solution)/shard_map/ppermute | solution.py:41
  35.2 7.8 %collective-permute-start.12 = (f32[2,16,16,256]{3,2,1,0:T(8,128)S(1)}, f32[2,16,16,256]{3,2,1,0:T(8,128)S(1)}, u32[]{:S(2)}, u32[]{:S(2)}) collective-permute-start(f32[2,16,16,256]{3,2,1,0:T(8,128)S(1)} %get-tuple-element.36.refs_0_), channel_id=1, source_target_pairs={{0,7},{1,0},{2,1},{3,2},{4,3},{5,4},{6,5},{7,6},{8,15},{9,8},{10,9... | collective-permute-start | bytes 1572872 | tf_op jit(solution)/shard_map/ppermute | solution.py:41
  35.5 8.6 %collective-permute-start.11 = (f32[2,16,16,256]{3,2,1,0:T(8,128)S(1)}, f32[2,16,16,256]{3,2,1,0:T(8,128)S(1)}, u32[]{:S(2)}, u32[]{:S(2)}) collective-permute-start(f32[2,16,16,256]{3,2,1,0:T(8,128)S(1)} %get-tuple-element.36.refs_0_), channel_id=1, source_target_pairs={{0,1},{1,2},{2,3},{3,4},{4,5},{5,6},{6,7},{7,0},{8,9},{9,10},{10,1... | collective-permute-start | bytes 1572872 | tf_op jit(solution)/shard_map/ppermute | solution.py:41
  36.0 5.0 %collective-permute-start.13 = (f32[2,4,16,256]{3,2,1,0:T(8,128)S(1)}, f32[2,4,16,256]{3,2,1,0:T(8,128)S(1)}, u32[]{:S(2)}, u32[]{:S(2)}) collective-permute-start(f32[2,4,16,256]{3,2,1,0:T(8,128)S(1)} %get-tuple-element.37), channel_id=1, source_target_pairs={{0,32},{1,33},{2,34},{3,35},{4,36},{5,37},{6,38},{7,39},{8,40},{9,... | collective-permute-start | bytes 393224 | tf_op jit(solution)/shard_map/ppermute | solution.py:41
  36.0 6.9 %collective-permute-start.14 = (f32[2,4,16,256]{3,2,1,0:T(8,128)S(1)}, f32[2,4,16,256]{3,2,1,0:T(8,128)S(1)}, u32[]{:S(2)}, u32[]{:S(2)}) collective-permute-start(f32[2,4,16,256]{3,2,1,0:T(8,128)S(1)} %get-tuple-element.38), channel_id=1, source_target_pairs={{0,224},{1,225},{2,226},{3,227},{4,228},{5,229},{6,230},{7,231},{8... | collective-permute-start | bytes 393224 | tf_op jit(solution)/shard_map/ppermute | solution.py:41
  45.2 7.3 %collective-permute-start.15 = (f32[8,16,256]{2,1,0:T(8,128)S(1)}, f32[8,16,256]{2,1,0:T(8,128)S(1)}, u32[]{:S(2)}, u32[]{:S(2)}) collective-permute-start(f32[8,16,256]{2,1,0:T(8,128)S(1)} %get-tuple-element.40), channel_id=1, source_target_pairs={{0,8},{1,9},{2,10},{3,11},{4,12},{5,13},{6,14},{7,15},{8,0},{9,1},... | collective-permute-start | bytes 393224 | tf_op jit(solution)/shard_map/ppermute | solution.py:41
  47.9 7.1 %collective-permute-start.16 = (f32[8,16,256]{2,1,0:T(8,128)S(1)}, f32[8,16,256]{2,1,0:T(8,128)S(1)}, u32[]{:S(2)}, u32[]{:S(2)}) collective-permute-start(f32[8,16,256]{2,1,0:T(8,128)S(1)} %get-tuple-element.41), channel_id=1, source_target_pairs={{0,16},{1,17},{2,18},{3,19},{4,20},{5,21},{6,22},{7,23},{8,24},{9,... | collective-permute-start | bytes 393224 | tf_op jit(solution)/shard_map/ppermute | solution.py:41
  48.6 7.7 %collective-permute-start.17 = (f32[8,16,256]{2,1,0:T(8,128)S(1)}, f32[8,16,256]{2,1,0:T(8,128)S(1)}, u32[]{:S(2)}, u32[]{:S(2)}) collective-permute-start(f32[8,16,256]{2,1,0:T(8,128)S(1)} %get-tuple-element.42), channel_id=1, source_target_pairs={{0,24},{1,25},{2,26},{3,27},{4,28},{5,29},{6,30},{7,31},{8,16},{9,... | collective-permute-start | bytes 393224 | tf_op jit(solution)/shard_map/ppermute | solution.py:41
  64.1 6.4 %collective-permute-start.24 = (f32[64,128]{1,0:T(8,128)S(1)}, f32[64,128]{1,0:T(8,128)S(1)}, u32[]{:S(2)}, u32[]{:S(2)}) collective-permute-start(f32[64,128]{1,0:T(8,128)S(1)} %pad_maximum_fusion.1), channel_id=1, source_target_pairs={{0,80},{1,81},{2,82},{3,83},{4,84},{5,85},{6,86},{7,87},{8,88},{9,... | collective-permute-start | bytes 98312 | tf_op jit(solution)/shard_map/ppermute | solution.py:210
  65.3 5.2 %collective-permute-start.23 = (f32[64,128]{1,0:T(8,128)S(1)}, f32[64,128]{1,0:T(8,128)S(1)}, u32[]{:S(2)}, u32[]{:S(2)}) collective-permute-start(f32[64,128]{1,0:T(8,128)S(1)} %pad_maximum_fusion.1), channel_id=1, source_target_pairs={{0,64},{1,65},{2,66},{3,67},{4,68},{5,69},{6,70},{7,71},{8,72},{9,... | collective-permute-start | bytes 98312 | tf_op jit(solution)/shard_map/ppermute | solution.py:210
  71.3 7.7 %collective-permute-start.27 = (f32[64,128]{1,0:T(8,128)S(1)}, f32[64,128]{1,0:T(8,128)S(1)}, u32[]{:S(2)}, u32[]{:S(2)}) collective-permute-start(f32[64,128]{1,0:T(8,128)S(1)} %pad_maximum_fusion.2), channel_id=1, source_target_pairs={{0,30},{1,31},{2,28},{3,29},{4,26},{5,27},{6,24},{7,25},{8,22},{9,... | collective-permute-start | bytes 98312 | tf_op jit(solution)/shard_map/ppermute | solution.py:210
  74.9 5.1 %collective-permute-start.26 = (f32[64,128]{1,0:T(8,128)S(1)}, f32[64,128]{1,0:T(8,128)S(1)}, u32[]{:S(2)}, u32[]{:S(2)}) collective-permute-start(f32[64,128]{1,0:T(8,128)S(1)} %pad_maximum_fusion.2), channel_id=1, source_target_pairs={{0,24},{1,25},{2,26},{3,27},{4,28},{5,29},{6,30},{7,31},{8,16},{9,... | collective-permute-start | bytes 98312 | tf_op jit(solution)/shard_map/ppermute | solution.py:210
  76.8 5.1 %collective-permute-start.25 = (f32[64,128]{1,0:T(8,128)S(1)}, f32[64,128]{1,0:T(8,128)S(1)}, u32[]{:S(2)}, u32[]{:S(2)}) collective-permute-start(f32[64,128]{1,0:T(8,128)S(1)} %pad_maximum_fusion.2), channel_id=1, source_target_pairs={{0,6},{1,7},{2,4},{3,5},{4,2},{5,3},{6,0},{7,1},{8,14},{9,15},{10,... | collective-permute-start | bytes 98312 | tf_op jit(solution)/shard_map/ppermute | solution.py:210
  82.0 6.3 %collective-permute-start.28 = (f32[64,128]{1,0:T(8,128)S(1)}, f32[64,128]{1,0:T(8,128)S(1)}, u32[]{:S(2)}, u32[]{:S(2)}) collective-permute-start(f32[64,128]{1,0:T(8,128)S(1)} %pad_maximum_fusion.3), channel_id=1, source_target_pairs={{0,192},{1,193},{2,194},{3,195},{4,196},{5,197},{6,198},{7,199},{8... | collective-permute-start | bytes 98312 | tf_op jit(solution)/shard_map/ppermute | solution.py:210
  (7 other events, 42.6 us)

commit v7 on v6

--- a/solution.py
+++ b/solution.py
@@ -62,13 +62,22 @@
     return i // 8 * 8 + (i + 7) % 8
 
 
-def split_kernel(x_ref, v_ref, *o_refs):
+def split_kernel(x_hbm, v_hbm, *refs):
+    o_refs, (x_ref, v_ref, sems) = refs[:4], refs[4:]
     _, y_lo, y_hi, _, _ = place()
-    part = x_ref.shape[0] // 4
+    part = x_ref.shape[1]
+    copies = [pltpu.make_async_copy(v_hbm, v_ref, sems.at[4])]
+    for k in range(4):
+        q = (y_lo ^ (k // 2)) * 2 + (y_hi ^ (k % 2))
+        source = x_hbm.at[pl.ds(q * part, part)]
+        copies.append(pltpu.make_async_copy(source, x_ref.at[k], sems.at[k]))
+    for copy in copies:
+        copy.start()
+    copies[0].wait()
     for k, o_ref in enumerate(o_refs):
-        q = (y_lo ^ (k // 2)) * 2 + (y_hi ^ (k % 2))
+        copies[k + 1].wait()
         for r in range(8):
-            x = x_ref[pl.ds(q * part, part), r, :]
+            x = x_ref[k, :, r, :]
             o_ref[2 * r : 2 * r + 2] = x.reshape(2, 8, x.shape[1])
         o_ref[16] = v_ref[...]
 
@@ -86,7 +95,7 @@
     for k, ref in enumerate(parts):
         start = (y_lo ^ (k // 2)) * 8
         f_ref[k % 2, pl.ds(start, 8)] = ref[0:16].reshape(8, *f_ref.shape[2:])
-        v = ref[16]
+        v = (ref[16] - (CENTER + 1.5 * COEFS[0])) * (2.0 / HALF_WIDTH)
         for r in range(8):
             v_ref[k % 2, start + r] = jnp.broadcast_to(v[r : r + 1, :], v.shape)
     for p in range(2):
@@ -355,8 +364,23 @@
     field = (2, 2 * rows, orbs, lanes)
     face = (2, 4, orbs, lanes)
     matrix = stencil_matrix(lanes // NZ)
-    own = (potential - (CENTER + 1.5 * COEFS[0])) * (2.0 / HALF_WIDTH)
-    parts = call(split_kernel, "split", [(2 * rows + 1, 8, lanes)] * 4, psi, own)
+    longer = jax.ShapeDtypeStruct((2 * rows + 1, 8, lanes), jnp.float32)
+    parts = pl.pallas_call(
+        split_kernel,
+        out_shape=[longer] * 4,
+        in_specs=[pl.BlockSpec(memory_space=pltpu.HBM)] * 2,
+        out_specs=[VMEM] * 4,
+        scratch_shapes=[
+            pltpu.VMEM((4, orbs, rows, lanes), jnp.float32),
+            pltpu.VMEM(potential.shape, jnp.float32),
+            pltpu.SemaphoreType.DMA((5,)),
+        ],
+        compiler_params=pltpu.CompilerParams(vmem_limit_bytes=32 << 20),
+        name="split",
+    )(
+        pltpu.with_memory_space_constraint(psi, pltpu.HBM),
+        pltpu.with_memory_space_constraint(potential, pltpu.HBM),
+    )
     parts = [parts[0]] + [swap(parts[k], Y_MASKS[k]) for k in (1, 2, 3)]
     joined = [field, (2, 2 * rows, 8, lanes), face, face]
     now, v, face1, face2 = call(join_kernel, "join", joined, *parts)

time: 94.5 us -> 93.8 us (level)
  local copies, waits for them, and re-layouts: 1.05 us -> 0.01 us
  Pallas kernels: 10.4 us -> 11.4 us
    pallas_call x0 -> x1, Pallas kernels: none -> 1.2 us  [on_device(): pl.pallas_call(split_kernel, out_shape=[longer] * 4, in_specs=[pl.BlockSp...]
    unnamed x4 -> x2, local copies, waits for them, and re-layouts: 1.05 us -> 0.01 us
    pallas_call x7 -> x6, Pallas kernels: 10.4 us -> 10.2 us  [call(): pl.pallas_call(kernel, out_shape=shapes[0] if single else shapes, in_spec...]
where the time goes in v7:
time: 93.8 us; the launch traced here: 93.6 us
  starting transfers between devices  43.9 us (47%)
  waiting for transfers between devices  38 us (41%)
  Pallas kernels  11.4 us (12%)
    ppermute x18, waiting for transfers between devices, permute(): return lax.ppermute(x, AXES, [(i, target(i)) for i in range(256)])  25.9 us
    ppermute x18, starting transfers between devices, permute(): return lax.ppermute(x, AXES, [(i, target(i)) for i in range(256)])  25.3 us
    ppermute x11, starting transfers between devices, swapped(): return lax.ppermute(x, AXES, [(i, i ^ mask) for i in range(256)])  18.6 us
    ppermute x11, waiting for transfers between devices, swapped(): return lax.ppermute(x, AXES, [(i, i ^ mask) for i in range(256)])  12.1 us
    pallas_call x6, Pallas kernels, call(): pl.pallas_call(kernel, out_shape=shapes[0] if single else shapes, in_spec...  10.2 us
  transfers between devices with their start and end apart: 29, of which 22 were waited for; matrix products, arithmetic and copies ran while one was open for 0% of the time, Pallas kernels for 0%

profile of v7, /device:TPU:6, one launch (start us, length us, event | category | flops | bytes accessed | tf_op | source)
XLA Modules:
  0.0 93.6 jit_solution(15822180224485402904)
XLA Ops:
  1.2 3.3 %collective-permute-start = (f32[17,8,256]{2,1,0:T(8,128)S(1)}, f32[17,8,256]{2,1,0:T(8,128)S(1)}, u32[]{:S(2)}, u32[]{:S(2)}) collective-permute-start(f32[17,8,256]{2,1,0:T(8,128)S(1)} %get-tuple-element.26), channel_id=1, source_target_pairs={{0,8},{1,9},{2,10},{3,11},{4,12},{5,13},{6,14},{7,15},{8,0},{9,1},... | collective-permute-start | bytes 417800 | tf_op jit(solution)/shard_map/ppermute | solution.py:41
  5.6 3.8 %collective-permute-done.refs_1_ = f32[17,8,256]{2,1,0:T(8,128)S(1)} collective-permute-done((f32[17,8,256]{2,1,0:T(8,128)S(1)}, f32[17,8,256]{2,1,0:T(8,128)S(1)}, u32[]{:S(2)}, u32[]{:S(2)}) %collective-permute-start) | collective-permute-done | bytes 139296 | tf_op jit(solution)/shard_map/ppermute | solution.py:41
  9.3 2.2 %collective-permute-done.1.refs_2_ = f32[17,8,256]{2,1,0:T(8,128)S(1)} collective-permute-done((f32[17,8,256]{2,1,0:T(8,128)S(1)}, f32[17,8,256]{2,1,0:T(8,128)S(1)}, u32[]{:S(2)}, u32[]{:S(2)}) %collective-permute-start.1) | collective-permute-done | bytes 139296 | tf_op jit(solution)/shard_map/ppermute | solution.py:41
  12.4 1.9 %collective-permute-start.5 = (f32[2,4,16,256]{3,2,1,0:T(8,128)S(1)}, f32[2,4,16,256]{3,2,1,0:T(8,128)S(1)}, u32[]{:S(2)}, u32[]{:S(2)}) collective-permute-start(f32[2,4,16,256]{3,2,1,0:T(8,128)S(1)} %get-tuple-element.30), channel_id=1, source_target_pairs={{0,32},{1,33},{2,34},{3,35},{4,36},{5,37},{6,38},{7,39},{8,40},{9,... | collective-permute-start | bytes 393224 | tf_op jit(solution)/shard_map/ppermute | solution.py:41
  14.3 4.9 %collective-permute-start.6 = (f32[2,4,16,256]{3,2,1,0:T(8,128)S(1)}, f32[2,4,16,256]{3,2,1,0:T(8,128)S(1)}, u32[]{:S(2)}, u32[]{:S(2)}) collective-permute-start(f32[2,4,16,256]{3,2,1,0:T(8,128)S(1)} %get-tuple-element.31), channel_id=1, source_target_pairs={{0,224},{1,225},{2,226},{3,227},{4,228},{5,229},{6,230},{7,231},{8... | collective-permute-start | bytes 393224 | tf_op jit(solution)/shard_map/ppermute | solution.py:41
  19.3 4.1 %collective-permute-done.6.refs_4_ = f32[2,4,16,256]{3,2,1,0:T(8,128)S(1)} collective-permute-done((f32[2,4,16,256]{3,2,1,0:T(8,128)S(1)}, f32[2,4,16,256]{3,2,1,0:T(8,128)S(1)}, u32[]{:S(2)}, u32[]{:S(2)}) %collective-permute-start.6) | collective-permute-done | bytes 131104 | tf_op jit(solution)/shard_map/ppermute | solution.py:41
  24.9 4.0 %collective-permute-start.10 = (f32[2,4,16,256]{3,2,1,0:T(8,128)S(1)}, f32[2,4,16,256]{3,2,1,0:T(8,128)S(1)}, u32[]{:S(2)}, u32[]{:S(2)}) collective-permute-start(f32[2,4,16,256]{3,2,1,0:T(8,128)S(1)} %get-tuple-element.35), channel_id=1, source_target_pairs={{0,224},{1,225},{2,226},{3,227},{4,228},{5,229},{6,230},{7,231},{8... | collective-permute-start | bytes 393224 | tf_op jit(solution)/shard_map/ppermute | solution.py:41
  29.9 2.0 %collective-permute-done.10.refs_4_ = f32[2,4,16,256]{3,2,1,0:T(8,128)S(1)} collective-permute-done((f32[2,4,16,256]{3,2,1,0:T(8,128)S(1)}, f32[2,4,16,256]{3,2,1,0:T(8,128)S(1)}, u32[]{:S(2)}, u32[]{:S(2)}) %collective-permute-start.10) | collective-permute-done | bytes 131104 | tf_op jit(solution)/shard_map/ppermute | solution.py:41
  31.8 1.6 %collective-permute-done.7.refs_1_ = f32[2,16,16,256]{3,2,1,0:T(8,128)S(1)} collective-permute-done((f32[2,16,16,256]{3,2,1,0:T(8,128)S(1)}, f32[2,16,16,256]{3,2,1,0:T(8,128)S(1)}, u32[]{:S(2)}, u32[]{:S(2)}) %collective-permute-start.7) | collective-permute-done | bytes 524320 | tf_op jit(solution)/shard_map/ppermute | solution.py:41
  35.3 4.0 %collective-permute-start.14 = (f32[2,4,16,256]{3,2,1,0:T(8,128)S(1)}, f32[2,4,16,256]{3,2,1,0:T(8,128)S(1)}, u32[]{:S(2)}, u32[]{:S(2)}) collective-permute-start(f32[2,4,16,256]{3,2,1,0:T(8,128)S(1)} %get-tuple-element.38), channel_id=1, source_target_pairs={{0,224},{1,225},{2,226},{3,227},{4,228},{5,229},{6,230},{7,231},{8... | collective-permute-start | bytes 393224 | tf_op jit(solution)/shard_map/ppermute | solution.py:41
  40.3 2.0 %collective-permute-done.14.refs_4_ = f32[2,4,16,256]{3,2,1,0:T(8,128)S(1)} collective-permute-done((f32[2,4,16,256]{3,2,1,0:T(8,128)S(1)}, f32[2,4,16,256]{3,2,1,0:T(8,128)S(1)}, u32[]{:S(2)}, u32[]{:S(2)}) %collective-permute-start.14) | collective-permute-done | bytes 131104 | tf_op jit(solution)/shard_map/ppermute | solution.py:41
  44.5 2.7 %collective-permute-start.15 = (f32[8,16,256]{2,1,0:T(8,128)S(1)}, f32[8,16,256]{2,1,0:T(8,128)S(1)}, u32[]{:S(2)}, u32[]{:S(2)}) collective-permute-start(f32[8,16,256]{2,1,0:T(8,128)S(1)} %get-tuple-element.40), channel_id=1, source_target_pairs={{0,8},{1,9},{2,10},{3,11},{4,12},{5,13},{6,14},{7,15},{8,0},{9,1},... | collective-permute-start | bytes 393224 | tf_op jit(solution)/shard_map/ppermute | solution.py:41
  48.6 3.1 %collective-permute-done.15.refs_1_ = f32[8,16,256]{2,1,0:T(8,128)S(1)} collective-permute-done((f32[8,16,256]{2,1,0:T(8,128)S(1)}, f32[8,16,256]{2,1,0:T(8,128)S(1)}, u32[]{:S(2)}, u32[]{:S(2)}) %collective-permute-start.15) | collective-permute-done | bytes 131104 | tf_op jit(solution)/shard_map/ppermute | solution.py:41
  51.7 2.5 %collective-permute-done.16.refs_2_ = f32[8,16,256]{2,1,0:T(8,128)S(1)} collective-permute-done((f32[8,16,256]{2,1,0:T(8,128)S(1)}, f32[8,16,256]{2,1,0:T(8,128)S(1)}, u32[]{:S(2)}, u32[]{:S(2)}) %collective-permute-start.16) | collective-permute-done | bytes 131104 | tf_op jit(solution)/shard_map/ppermute | solution.py:41
  58.9 2.6 %collective-permute-start.19 = (f32[64,128]{1,0:T(8,128)S(1)}, f32[64,128]{1,0:T(8,128)S(1)}, u32[]{:S(2)}, u32[]{:S(2)}) collective-permute-start(f32[64,128]{1,0:T(8,128)S(1)} %pad_maximum_fusion), channel_id=1, source_target_pairs={{0,2},{1,3},{2,0},{3,1},{4,6},{5,7},{6,4},{7,5},{8,10},{9,11},{10,... | collective-permute-start | bytes 98312 | tf_op jit(solution)/shard_map/ppermute | solution.py:219
  64.6 2.1 %collective-permute-start.23 = (f32[64,128]{1,0:T(8,128)S(1)}, f32[64,128]{1,0:T(8,128)S(1)}, u32[]{:S(2)}, u32[]{:S(2)}) collective-permute-start(f32[64,128]{1,0:T(8,128)S(1)} %pad_maximum_fusion.1), channel_id=1, source_target_pairs={{0,64},{1,65},{2,66},{3,67},{4,68},{5,69},{6,70},{7,71},{8,72},{9,... | collective-permute-start | bytes 98312 | tf_op jit(solution)/shard_map/ppermute | solution.py:219
  67.9 1.9 %collective-permute-done.24 = f32[64,128]{1,0:T(8,128)S(1)} collective-permute-done((f32[64,128]{1,0:T(8,128)S(1)}, f32[64,128]{1,0:T(8,128)S(1)}, u32[]{:S(2)}, u32[]{:S(2)}) %collective-permute-start.24) | collective-permute-done | bytes 32800 | tf_op jit(solution)/shard_map/ppermute | solution.py:219
  70.6 3.5 %collective-permute-start.27 = (f32[64,128]{1,0:T(8,128)S(1)}, f32[64,128]{1,0:T(8,128)S(1)}, u32[]{:S(2)}, u32[]{:S(2)}) collective-permute-start(f32[64,128]{1,0:T(8,128)S(1)} %pad_maximum_fusion.2), channel_id=1, source_target_pairs={{0,30},{1,31},{2,28},{3,29},{4,26},{5,27},{6,24},{7,25},{8,22},{9,... | collective-permute-start | bytes 98312 | tf_op jit(solution)/shard_map/ppermute | solution.py:219
  74.2 1.9 %collective-permute-start.26 = (f32[64,128]{1,0:T(8,128)S(1)}, f32[64,128]{1,0:T(8,128)S(1)}, u32[]{:S(2)}, u32[]{:S(2)}) collective-permute-start(f32[64,128]{1,0:T(8,128)S(1)} %pad_maximum_fusion.2), channel_id=1, source_target_pairs={{0,24},{1,25},{2,26},{3,27},{4,28},{5,29},{6,30},{7,31},{8,16},{9,... | collective-permute-start | bytes 98312 | tf_op jit(solution)/shard_map/ppermute | solution.py:219
  76.6 1.7 %collective-permute-done.27 = f32[64,128]{1,0:T(8,128)S(1)} collective-permute-done((f32[64,128]{1,0:T(8,128)S(1)}, f32[64,128]{1,0:T(8,128)S(1)}, u32[]{:S(2)}, u32[]{:S(2)}) %collective-permute-start.27) | collective-permute-done | bytes 32800 | tf_op jit(solution)/shard_map/ppermute | solution.py:219
  79.3 1.9 %collective-permute-done.25 = f32[64,128]{1,0:T(8,128)S(1)} collective-permute-done((f32[64,128]{1,0:T(8,128)S(1)}, f32[64,128]{1,0:T(8,128)S(1)}, u32[]{:S(2)}, u32[]{:S(2)}) %collective-permute-start.25) | collective-permute-done | bytes 32800 | tf_op jit(solution)/shard_map/ppermute | solution.py:219
  81.2 4.4 %collective-permute-start.28 = (f32[64,128]{1,0:T(8,128)S(1)}, f32[64,128]{1,0:T(8,128)S(1)}, u32[]{:S(2)}, u32[]{:S(2)}) collective-permute-start(f32[64,128]{1,0:T(8,128)S(1)} %pad_maximum_fusion.3), channel_id=1, source_target_pairs={{0,192},{1,193},{2,194},{3,195},{4,196},{5,197},{6,198},{7,199},{8... | collective-permute-start | bytes 98312 | tf_op jit(solution)/shard_map/ppermute | solution.py:219
  85.6 1.9 %collective-permute-done.28 = f32[64,128]{1,0:T(8,128)S(1)} collective-permute-done((f32[64,128]{1,0:T(8,128)S(1)}, f32[64,128]{1,0:T(8,128)S(1)}, u32[]{:S(2)}, u32[]{:S(2)}) %collective-permute-start.28) | collective-permute-done | bytes 32800 | tf_op jit(solution)/shard_map/ppermute | solution.py:219
  87.5 6.1 %rotate.1 = f32[64,8,256]{2,1,0:T(8,128)} custom-call(f32[64,128]{1,0:T(8,128)S(1)} %pad_maximum_fusion.4.p_ref, bf16[8,256,256]{2,1,0:T(8,128)(2,1)S(1)} %get-tuple-element.44.z_ref), custom_call_target="tpu_custom_call" | custom-call | tf_op jit(solution)/shard_map/rotate/pallas_call | solution.py:349
  (56 shorter events, 23.5 us)
Async XLA Ops:
  1.2 8.1 %collective-permute-start = (f32[17,8,256]{2,1,0:T(8,128)S(1)}, f32[17,8,256]{2,1,0:T(8,128)S(1)}, u32[]{:S(2)}, u32[]{:S(2)}) collective-permute-start(f32[17,8,256]{2,1,0:T(8,128)S(1)} %get-tuple-element.26), channel_id=1, source_target_pairs={{0,8},{1,9},{2,10},{3,11},{4,12},{5,13},{6,14},{7,15},{8,0},{9,1},... | collective-permute-start | bytes 417800 | tf_op jit(solution)/shard_map/ppermute | solution.py:41
  4.5 7.0 %collective-permute-start.1 = (f32[17,8,256]{2,1,0:T(8,128)S(1)}, f32[17,8,256]{2,1,0:T(8,128)S(1)}, u32[]{:S(2)}, u32[]{:S(2)}) collective-permute-start(f32[17,8,256]{2,1,0:T(8,128)S(1)} %get-tuple-element.27), channel_id=1, source_target_pairs={{0,16},{1,17},{2,18},{3,19},{4,20},{5,21},{6,22},{7,23},{8,24},{9,... | collective-permute-start | bytes 417800 | tf_op jit(solution)/shard_map/ppermute | solution.py:41
  5.2 6.6 %collective-permute-start.2 = (f32[17,8,256]{2,1,0:T(8,128)S(1)}, f32[17,8,256]{2,1,0:T(8,128)S(1)}, u32[]{:S(2)}, u32[]{:S(2)}) collective-permute-start(f32[17,8,256]{2,1,0:T(8,128)S(1)} %get-tuple-element.28), channel_id=1, source_target_pairs={{0,24},{1,25},{2,26},{3,27},{4,28},{5,29},{6,30},{7,31},{8,16},{9,... | collective-permute-start | bytes 417800 | tf_op jit(solution)/shard_map/ppermute | solution.py:41
  11.9 11.5 %collective-permute-start.4 = (f32[2,16,16,256]{3,2,1,0:T(8,128)S(1)}, f32[2,16,16,256]{3,2,1,0:T(8,128)S(1)}, u32[]{:S(2)}, u32[]{:S(2)}) collective-permute-start(f32[2,16,16,256]{3,2,1,0:T(8,128)S(1)} %get-tuple-element.29.refs_0_.refs_7_), channel_id=1, source_target_pairs={{0,7},{1,0},{2,1},{3,2},{4,3},{5,4},{6,5},{7,6},{8,15},{9,8},{10,9... | collective-permute-start | bytes 1572872 | tf_op jit(solution)/shard_map/ppermute | solution.py:41
  11.9 11.4 %collective-permute-start.3 = (f32[2,16,16,256]{3,2,1,0:T(8,128)S(1)}, f32[2,16,16,256]{3,2,1,0:T(8,128)S(1)}, u32[]{:S(2)}, u32[]{:S(2)}) collective-permute-start(f32[2,16,16,256]{3,2,1,0:T(8,128)S(1)} %get-tuple-element.29.refs_0_.refs_7_), channel_id=1, source_target_pairs={{0,1},{1,2},{2,3},{3,4},{4,5},{5,6},{6,7},{7,0},{8,9},{9,10},{10,1... | collective-permute-start | bytes 1572872 | tf_op jit(solution)/shard_map/ppermute | solution.py:41
  12.4 6.9 %collective-permute-start.5 = (f32[2,4,16,256]{3,2,1,0:T(8,128)S(1)}, f32[2,4,16,256]{3,2,1,0:T(8,128)S(1)}, u32[]{:S(2)}, u32[]{:S(2)}) collective-permute-start(f32[2,4,16,256]{3,2,1,0:T(8,128)S(1)} %get-tuple-element.30), channel_id=1, source_target_pairs={{0,32},{1,33},{2,34},{3,35},{4,36},{5,37},{6,38},{7,39},{8,40},{9,... | collective-permute-start | bytes 393224 | tf_op jit(solution)/shard_map/ppermute | solution.py:41
  14.3 9.0 %collective-permute-start.6 = (f32[2,4,16,256]{3,2,1,0:T(8,128)S(1)}, f32[2,4,16,256]{3,2,1,0:T(8,128)S(1)}, u32[]{:S(2)}, u32[]{:S(2)}) collective-permute-start(f32[2,4,16,256]{3,2,1,0:T(8,128)S(1)} %get-tuple-element.31), channel_id=1, source_target_pairs={{0,224},{1,225},{2,226},{3,227},{4,228},{5,229},{6,230},{7,231},{8... | collective-permute-start | bytes 393224 | tf_op jit(solution)/shard_map/ppermute | solution.py:41
  24.3 7.5 %collective-permute-start.8 = (f32[2,16,16,256]{3,2,1,0:T(8,128)S(1)}, f32[2,16,16,256]{3,2,1,0:T(8,128)S(1)}, u32[]{:S(2)}, u32[]{:S(2)}) collective-permute-start(f32[2,16,16,256]{3,2,1,0:T(8,128)S(1)} %get-tuple-element.33.refs_0_.refs_7_), channel_id=1, source_target_pairs={{0,7},{1,0},{2,1},{3,2},{4,3},{5,4},{6,5},{7,6},{8,15},{9,8},{10,9... | collective-permute-start | bytes 1572872 | tf_op jit(solution)/shard_map/ppermute | solution.py:41
  24.9 8.6 %collective-permute-start.7 = (f32[2,16,16,256]{3,2,1,0:T(8,128)S(1)}, f32[2,16,16,256]{3,2,1,0:T(8,128)S(1)}, u32[]{:S(2)}, u32[]{:S(2)}) collective-permute-start(f32[2,16,16,256]{3,2,1,0:T(8,128)S(1)} %get-tuple-element.33.refs_0_.refs_7_), channel_id=1, source_target_pairs={{0,1},{1,2},{2,3},{3,4},{4,5},{5,6},{6,7},{7,0},{8,9},{9,10},{10,1... | collective-permute-start | bytes 1572872 | tf_op jit(solution)/shard_map/ppermute | solution.py:41
  24.9 5.0 %collective-permute-start.9 = (f32[2,4,16,256]{3,2,1,0:T(8,128)S(1)}, f32[2,4,16,256]{3,2,1,0:T(8,128)S(1)}, u32[]{:S(2)}, u32[]{:S(2)}) collective-permute-start(f32[2,4,16,256]{3,2,1,0:T(8,128)S(1)} %get-tuple-element.34), channel_id=1, source_target_pairs={{0,32},{1,33},{2,34},{3,35},{4,36},{5,37},{6,38},{7,39},{8,40},{9,... | collective-permute-start | bytes 393224 | tf_op jit(solution)/shard_map/ppermute | solution.py:41
  24.9 7.0 %collective-permute-start.10 = (f32[2,4,16,256]{3,2,1,0:T(8,128)S(1)}, f32[2,4,16,256]{3,2,1,0:T(8,128)S(1)}, u32[]{:S(2)}, u32[]{:S(2)}) collective-permute-start(f32[2,4,16,256]{3,2,1,0:T(8,128)S(1)} %get-tuple-element.35), channel_id=1, source_target_pairs={{0,224},{1,225},{2,226},{3,227},{4,228},{5,229},{6,230},{7,231},{8... | collective-permute-start | bytes 393224 | tf_op jit(solution)/shard_map/ppermute | solution.py:41
  34.5 7.8 %collective-permute-start.12 = (f32[2,16,16,256]{3,2,1,0:T(8,128)S(1)}, f32[2,16,16,256]{3,2,1,0:T(8,128)S(1)}, u32[]{:S(2)}, u32[]{:S(2)}) collective-permute-start(f32[2,16,16,256]{3,2,1,0:T(8,128)S(1)} %get-tuple-element.36.refs_0_), channel_id=1, source_target_pairs={{0,7},{1,0},{2,1},{3,2},{4,3},{5,4},{6,5},{7,6},{8,15},{9,8},{10,9... | collective-permute-start | bytes 1572872 | tf_op jit(solution)/shard_map/ppermute | solution.py:41
  34.8 8.6 %collective-permute-start.11 = (f32[2,16,16,256]{3,2,1,0:T(8,128)S(1)}, f32[2,16,16,256]{3,2,1,0:T(8,128)S(1)}, u32[]{:S(2)}, u32[]{:S(2)}) collective-permute-start(f32[2,16,16,256]{3,2,1,0:T(8,128)S(1)} %get-tuple-element.36.refs_0_), channel_id=1, source_target_pairs={{0,1},{1,2},{2,3},{3,4},{4,5},{5,6},{6,7},{7,0},{8,9},{9,10},{10,1... | collective-permute-start | bytes 1572872 | tf_op jit(solution)/shard_map/ppermute | solution.py:41
  35.3 5.0 %collective-permute-start.13 = (f32[2,4,16,256]{3,2,1,0:T(8,128)S(1)}, f32[2,4,16,256]{3,2,1,0:T(8,128)S(1)}, u32[]{:S(2)}, u32[]{:S(2)}) collective-permute-start(f32[2,4,16,256]{3,2,1,0:T(8,128)S(1)} %get-tuple-element.37), channel_id=1, source_target_pairs={{0,32},{1,33},{2,34},{3,35},{4,36},{5,37},{6,38},{7,39},{8,40},{9,... | collective-permute-start | bytes 393224 | tf_op jit(solution)/shard_map/ppermute | solution.py:41
  35.3 7.0 %collective-permute-start.14 = (f32[2,4,16,256]{3,2,1,0:T(8,128)S(1)}, f32[2,4,16,256]{3,2,1,0:T(8,128)S(1)}, u32[]{:S(2)}, u32[]{:S(2)}) collective-permute-start(f32[2,4,16,256]{3,2,1,0:T(8,128)S(1)} %get-tuple-element.38), channel_id=1, source_target_pairs={{0,224},{1,225},{2,226},{3,227},{4,228},{5,229},{6,230},{7,231},{8... | collective-permute-start | bytes 393224 | tf_op jit(solution)/shard_map/ppermute | solution.py:41
  44.5 7.3 %collective-permute-start.15 = (f32[8,16,256]{2,1,0:T(8,128)S(1)}, f32[8,16,256]{2,1,0:T(8,128)S(1)}, u32[]{:S(2)}, u32[]{:S(2)}) collective-permute-start(f32[8,16,256]{2,1,0:T(8,128)S(1)} %get-tuple-element.40), channel_id=1, source_target_pairs={{0,8},{1,9},{2,10},{3,11},{4,12},{5,13},{6,14},{7,15},{8,0},{9,1},... | collective-permute-start | bytes 393224 | tf_op jit(solution)/shard_map/ppermute | solution.py:41
  47.2 7.1 %collective-permute-start.16 = (f32[8,16,256]{2,1,0:T(8,128)S(1)}, f32[8,16,256]{2,1,0:T(8,128)S(1)}, u32[]{:S(2)}, u32[]{:S(2)}) collective-permute-start(f32[8,16,256]{2,1,0:T(8,128)S(1)} %get-tuple-element.41), channel_id=1, source_target_pairs={{0,16},{1,17},{2,18},{3,19},{4,20},{5,21},{6,22},{7,23},{8,24},{9,... | collective-permute-start | bytes 393224 | tf_op jit(solution)/shard_map/ppermute | solution.py:41
  47.9 7.7 %collective-permute-start.17 = (f32[8,16,256]{2,1,0:T(8,128)S(1)}, f32[8,16,256]{2,1,0:T(8,128)S(1)}, u32[]{:S(2)}, u32[]{:S(2)}) collective-permute-start(f32[8,16,256]{2,1,0:T(8,128)S(1)} %get-tuple-element.42), channel_id=1, source_target_pairs={{0,24},{1,25},{2,26},{3,27},{4,28},{5,29},{6,30},{7,31},{8,16},{9,... | collective-permute-start | bytes 393224 | tf_op jit(solution)/shard_map/ppermute | solution.py:41
  63.4 6.4 %collective-permute-start.24 = (f32[64,128]{1,0:T(8,128)S(1)}, f32[64,128]{1,0:T(8,128)S(1)}, u32[]{:S(2)}, u32[]{:S(2)}) collective-permute-start(f32[64,128]{1,0:T(8,128)S(1)} %pad_maximum_fusion.1), channel_id=1, source_target_pairs={{0,80},{1,81},{2,82},{3,83},{4,84},{5,85},{6,86},{7,87},{8,88},{9,... | collective-permute-start | bytes 98312 | tf_op jit(solution)/shard_map/ppermute | solution.py:219
  64.6 5.2 %collective-permute-start.23 = (f32[64,128]{1,0:T(8,128)S(1)}, f32[64,128]{1,0:T(8,128)S(1)}, u32[]{:S(2)}, u32[]{:S(2)}) collective-permute-start(f32[64,128]{1,0:T(8,128)S(1)} %pad_maximum_fusion.1), channel_id=1, source_target_pairs={{0,64},{1,65},{2,66},{3,67},{4,68},{5,69},{6,70},{7,71},{8,72},{9,... | collective-permute-start | bytes 98312 | tf_op jit(solution)/shard_map/ppermute | solution.py:219
  70.6 7.7 %collective-permute-start.27 = (f32[64,128]{1,0:T(8,128)S(1)}, f32[64,128]{1,0:T(8,128)S(1)}, u32[]{:S(2)}, u32[]{:S(2)}) collective-permute-start(f32[64,128]{1,0:T(8,128)S(1)} %pad_maximum_fusion.2), channel_id=1, source_target_pairs={{0,30},{1,31},{2,28},{3,29},{4,26},{5,27},{6,24},{7,25},{8,22},{9,... | collective-permute-start | bytes 98312 | tf_op jit(solution)/shard_map/ppermute | solution.py:219
  74.2 5.1 %collective-permute-start.26 = (f32[64,128]{1,0:T(8,128)S(1)}, f32[64,128]{1,0:T(8,128)S(1)}, u32[]{:S(2)}, u32[]{:S(2)}) collective-permute-start(f32[64,128]{1,0:T(8,128)S(1)} %pad_maximum_fusion.2), channel_id=1, source_target_pairs={{0,24},{1,25},{2,26},{3,27},{4,28},{5,29},{6,30},{7,31},{8,16},{9,... | collective-permute-start | bytes 98312 | tf_op jit(solution)/shard_map/ppermute | solution.py:219
  76.0 5.1 %collective-permute-start.25 = (f32[64,128]{1,0:T(8,128)S(1)}, f32[64,128]{1,0:T(8,128)S(1)}, u32[]{:S(2)}, u32[]{:S(2)}) collective-permute-start(f32[64,128]{1,0:T(8,128)S(1)} %pad_maximum_fusion.2), channel_id=1, source_target_pairs={{0,6},{1,7},{2,4},{3,5},{4,2},{5,3},{6,0},{7,1},{8,14},{9,15},{10,... | collective-permute-start | bytes 98312 | tf_op jit(solution)/shard_map/ppermute | solution.py:219
  81.2 6.3 %collective-permute-start.28 = (f32[64,128]{1,0:T(8,128)S(1)}, f32[64,128]{1,0:T(8,128)S(1)}, u32[]{:S(2)}, u32[]{:S(2)}) collective-permute-start(f32[64,128]{1,0:T(8,128)S(1)} %pad_maximum_fusion.3), channel_id=1, source_target_pairs={{0,192},{1,193},{2,194},{3,195},{4,196},{5,197},{6,198},{7,199},{8... | collective-permute-start | bytes 98312 | tf_op jit(solution)/shard_map/ppermute | solution.py:219
  (6 other events, 41.5 us)

commit v8 on v7

--- a/solution.py
+++ b/solution.py
@@ -102,7 +102,7 @@
         send_faces(even, f_ref.at[p], p, f1_ref, f2_ref)
 
 
-def level_kernel(level, *refs):
+def level_kernel(level, patches, *refs):
     f_ref, l_ref, r_ref, z1_ref, z2_ref, v_ref, m_ref = refs[:7]
     refs = refs[7:]
     if level > 1:
@@ -115,7 +115,7 @@
     right_flip = jnp.where((x == 3) & (core == 1), 1, 0)
     factor = 2.0 if level > 1 else 1.0
     alpha = -0.5 * factor / (HALF_WIDTH * SCALE)
-    for p in range(2):
+    for p in patches:
         near = []
         for ref, q in ((l_ref, p ^ left_flip), (f_ref, p), (r_ref, p ^ right_flip)):
             rest = ref[q].reshape(flat)
@@ -145,9 +145,9 @@
             refs[0][p] = out
             send_faces(even, out, p, refs[1], refs[2])
         else:
-            refs[4][...] = out
-            for k in (p, p + 2):
-                refs[k][...] = refs[4][pl.ds((y_lo ^ (k // 2)) * 8, 8)]
+            refs[2][...] = out
+            for k in range(2):
+                refs[k][...] = refs[2][pl.ds((y_lo ^ k) * 8, 8)]
 
 
 def two_sum(a, b):
@@ -389,12 +389,22 @@
         left, right = permute(now, y_up), permute(now, y_down)
         face1, face2 = permute(face1, z_even), permute(face2, z_odd)
         args = [now, left, right, face1, face2, v, matrix] + ([] if old is None else [old])
-        kernel = functools.partial(level_kernel, level)
+        kernel = functools.partial(level_kernel, level, (0, 1))
         if level < 3:
             outs = call(kernel, f"level{level}", [field, face, face], *args)
             old, (now, face1, face2) = now, outs
         else:
-            parts = call(kernel, "level3", [part] * 4, *args, scratch=[field[1:]])
+            halves = [
+                call(
+                    functools.partial(level_kernel, level, (p,)),
+                    f"level3_{p}",
+                    [part] * 2,
+                    *args,
+                    scratch=[field[1:]],
+                )
+                for p in (1, 0)
+            ]
+            parts = [halves[1][0], halves[0][0], halves[1][1], halves[0][1]]
     parts = [parts[0]] + [swap(parts[k], Y_MASKS[k]) for k in (1, 2, 3)]
     pieces = ((rows, 4 * m, lanes), jnp.bfloat16)
     whole = [(rows, m, lanes)]

time: 93.8 us -> 93 us (level)
    pallas_call x6 -> x7, Pallas kernels: 10.2 us -> 10.3 us  [call(): pl.pallas_call(kernel, out_shape=shapes[0] if single else shapes, in_spec...]
  transfers between devices with their start and end apart: 29 -> 29, of which waited for: 22 -> 22; matrix products, arithmetic and copies ran while one was open for 0% -> 0% of each run, Pallas kernels for 0% -> 1%
where the time goes in v8:
time: 93 us; the launch traced here: 92.8 us
  starting transfers between devices  43.3 us (47%)
  waiting for transfers between devices  37.7 us (41%)
  Pallas kernels  11.5 us (12%)
    ppermute x18, waiting for transfers between devices, permute(): return lax.ppermute(x, AXES, [(i, target(i)) for i in range(256)])  25.2 us
    ppermute x18, starting transfers between devices, permute(): return lax.ppermute(x, AXES, [(i, target(i)) for i in range(256)])  25.1 us
    ppermute x11, starting transfers between devices, swapped(): return lax.ppermute(x, AXES, [(i, i ^ mask) for i in range(256)])  18.2 us
    ppermute x11, waiting for transfers between devices, swapped(): return lax.ppermute(x, AXES, [(i, i ^ mask) for i in range(256)])  12.5 us
    pallas_call x7, Pallas kernels, call(): pl.pallas_call(kernel, out_shape=shapes[0] if single else shapes, in_spec...  10.3 us
  transfers between devices with their start and end apart: 29, of which 22 were waited for; matrix products, arithmetic and copies ran while one was open for 0% of the time, Pallas kernels for 1%

profile of v8, /device:TPU:6, one launch (start us, length us, event | category | flops | bytes accessed | tf_op | source)
XLA Modules:
  0.0 92.8 jit_solution(1888400387550739766)
XLA Ops:
  1.2 3.3 %collective-permute-start = (f32[17,8,256]{2,1,0:T(8,128)S(1)}, f32[17,8,256]{2,1,0:T(8,128)S(1)}, u32[]{:S(2)}, u32[]{:S(2)}) collective-permute-start(f32[17,8,256]{2,1,0:T(8,128)S(1)} %get-tuple-element.26), channel_id=1, source_target_pairs={{0,8},{1,9},{2,10},{3,11},{4,12},{5,13},{6,14},{7,15},{8,0},{9,1},... | collective-permute-start | bytes 417800 | tf_op jit(solution)/shard_map/ppermute | solution.py:41
  5.6 3.8 %collective-permute-done.refs_1_ = f32[17,8,256]{2,1,0:T(8,128)S(1)} collective-permute-done((f32[17,8,256]{2,1,0:T(8,128)S(1)}, f32[17,8,256]{2,1,0:T(8,128)S(1)}, u32[]{:S(2)}, u32[]{:S(2)}) %collective-permute-start) | collective-permute-done | bytes 139296 | tf_op jit(solution)/shard_map/ppermute | solution.py:41
  9.3 2.2 %collective-permute-done.1.refs_2_ = f32[17,8,256]{2,1,0:T(8,128)S(1)} collective-permute-done((f32[17,8,256]{2,1,0:T(8,128)S(1)}, f32[17,8,256]{2,1,0:T(8,128)S(1)}, u32[]{:S(2)}, u32[]{:S(2)}) %collective-permute-start.1) | collective-permute-done | bytes 139296 | tf_op jit(solution)/shard_map/ppermute | solution.py:41
  12.4 1.9 %collective-permute-start.5 = (f32[2,4,16,256]{3,2,1,0:T(8,128)S(1)}, f32[2,4,16,256]{3,2,1,0:T(8,128)S(1)}, u32[]{:S(2)}, u32[]{:S(2)}) collective-permute-start(f32[2,4,16,256]{3,2,1,0:T(8,128)S(1)} %get-tuple-element.30), channel_id=1, source_target_pairs={{0,32},{1,33},{2,34},{3,35},{4,36},{5,37},{6,38},{7,39},{8,40},{9,... | collective-permute-start | bytes 393224 | tf_op jit(solution)/shard_map/ppermute | solution.py:41
  14.3 4.9 %collective-permute-start.6 = (f32[2,4,16,256]{3,2,1,0:T(8,128)S(1)}, f32[2,4,16,256]{3,2,1,0:T(8,128)S(1)}, u32[]{:S(2)}, u32[]{:S(2)}) collective-permute-start(f32[2,4,16,256]{3,2,1,0:T(8,128)S(1)} %get-tuple-element.31), channel_id=1, source_target_pairs={{0,224},{1,225},{2,226},{3,227},{4,228},{5,229},{6,230},{7,231},{8... | collective-permute-start | bytes 393224 | tf_op jit(solution)/shard_map/ppermute | solution.py:41
  19.3 4.1 %collective-permute-done.6.refs_4_ = f32[2,4,16,256]{3,2,1,0:T(8,128)S(1)} collective-permute-done((f32[2,4,16,256]{3,2,1,0:T(8,128)S(1)}, f32[2,4,16,256]{3,2,1,0:T(8,128)S(1)}, u32[]{:S(2)}, u32[]{:S(2)}) %collective-permute-start.6) | collective-permute-done | bytes 131104 | tf_op jit(solution)/shard_map/ppermute | solution.py:41
  24.9 4.0 %collective-permute-start.10 = (f32[2,4,16,256]{3,2,1,0:T(8,128)S(1)}, f32[2,4,16,256]{3,2,1,0:T(8,128)S(1)}, u32[]{:S(2)}, u32[]{:S(2)}) collective-permute-start(f32[2,4,16,256]{3,2,1,0:T(8,128)S(1)} %get-tuple-element.35), channel_id=1, source_target_pairs={{0,224},{1,225},{2,226},{3,227},{4,228},{5,229},{6,230},{7,231},{8... | collective-permute-start | bytes 393224 | tf_op jit(solution)/shard_map/ppermute | solution.py:41
  29.9 2.0 %collective-permute-done.10.refs_4_ = f32[2,4,16,256]{3,2,1,0:T(8,128)S(1)} collective-permute-done((f32[2,4,16,256]{3,2,1,0:T(8,128)S(1)}, f32[2,4,16,256]{3,2,1,0:T(8,128)S(1)}, u32[]{:S(2)}, u32[]{:S(2)}) %collective-permute-start.10) | collective-permute-done | bytes 131104 | tf_op jit(solution)/shard_map/ppermute | solution.py:41
  31.8 1.6 %collective-permute-done.7.refs_1_ = f32[2,16,16,256]{3,2,1,0:T(8,128)S(1)} collective-permute-done((f32[2,16,16,256]{3,2,1,0:T(8,128)S(1)}, f32[2,16,16,256]{3,2,1,0:T(8,128)S(1)}, u32[]{:S(2)}, u32[]{:S(2)}) %collective-permute-start.7) | collective-permute-done | bytes 524320 | tf_op jit(solution)/shard_map/ppermute | solution.py:41
  35.3 4.0 %collective-permute-start.14 = (f32[2,4,16,256]{3,2,1,0:T(8,128)S(1)}, f32[2,4,16,256]{3,2,1,0:T(8,128)S(1)}, u32[]{:S(2)}, u32[]{:S(2)}) collective-permute-start(f32[2,4,16,256]{3,2,1,0:T(8,128)S(1)} %get-tuple-element.38), channel_id=1, source_target_pairs={{0,224},{1,225},{2,226},{3,227},{4,228},{5,229},{6,230},{7,231},{8... | collective-permute-start | bytes 393224 | tf_op jit(solution)/shard_map/ppermute | solution.py:41
  40.3 2.0 %collective-permute-done.14.refs_4_ = f32[2,4,16,256]{3,2,1,0:T(8,128)S(1)} collective-permute-done((f32[2,4,16,256]{3,2,1,0:T(8,128)S(1)}, f32[2,4,16,256]{3,2,1,0:T(8,128)S(1)}, u32[]{:S(2)}, u32[]{:S(2)}) %collective-permute-start.14) | collective-permute-done | bytes 131104 | tf_op jit(solution)/shard_map/ppermute | solution.py:41
  44.0 2.7 %collective-permute-start.15 = (f32[8,16,256]{2,1,0:T(8,128)S(1)}, f32[8,16,256]{2,1,0:T(8,128)S(1)}, u32[]{:S(2)}, u32[]{:S(2)}) collective-permute-start(f32[8,16,256]{2,1,0:T(8,128)S(1)} %get-tuple-element.40), channel_id=1, source_target_pairs={{0,8},{1,9},{2,10},{3,11},{4,12},{5,13},{6,14},{7,15},{8,0},{9,1},... | collective-permute-start | bytes 393224 | tf_op jit(solution)/shard_map/ppermute | solution.py:41
  48.6 2.7 %collective-permute-done.15.refs_1_ = f32[8,16,256]{2,1,0:T(8,128)S(1)} collective-permute-done((f32[8,16,256]{2,1,0:T(8,128)S(1)}, f32[8,16,256]{2,1,0:T(8,128)S(1)}, u32[]{:S(2)}, u32[]{:S(2)}) %collective-permute-start.15) | collective-permute-done | bytes 131104 | tf_op jit(solution)/shard_map/ppermute | solution.py:41
  51.2 3.5 %collective-permute-done.17.refs_3_ = f32[8,16,256]{2,1,0:T(8,128)S(1)} collective-permute-done((f32[8,16,256]{2,1,0:T(8,128)S(1)}, f32[8,16,256]{2,1,0:T(8,128)S(1)}, u32[]{:S(2)}, u32[]{:S(2)}) %collective-permute-start.17) | collective-permute-done | bytes 131104 | tf_op jit(solution)/shard_map/ppermute | solution.py:41
  58.2 2.5 %collective-permute-start.19 = (f32[64,128]{1,0:T(8,128)S(1)}, f32[64,128]{1,0:T(8,128)S(1)}, u32[]{:S(2)}, u32[]{:S(2)}) collective-permute-start(f32[64,128]{1,0:T(8,128)S(1)} %pad_maximum_fusion), channel_id=1, source_target_pairs={{0,2},{1,3},{2,0},{3,1},{4,6},{5,7},{6,4},{7,5},{8,10},{9,11},{10,... | collective-permute-start | bytes 98312 | tf_op jit(solution)/shard_map/ppermute | solution.py:219
  62.6 1.9 %collective-permute-start.24 = (f32[64,128]{1,0:T(8,128)S(1)}, f32[64,128]{1,0:T(8,128)S(1)}, u32[]{:S(2)}, u32[]{:S(2)}) collective-permute-start(f32[64,128]{1,0:T(8,128)S(1)} %pad_maximum_fusion.1), channel_id=1, source_target_pairs={{0,80},{1,81},{2,82},{3,83},{4,84},{5,85},{6,86},{7,87},{8,88},{9,... | collective-permute-start | bytes 98312 | tf_op jit(solution)/shard_map/ppermute | solution.py:219
  64.5 1.7 %collective-permute-start.23 = (f32[64,128]{1,0:T(8,128)S(1)}, f32[64,128]{1,0:T(8,128)S(1)}, u32[]{:S(2)}, u32[]{:S(2)}) collective-permute-start(f32[64,128]{1,0:T(8,128)S(1)} %pad_maximum_fusion.1), channel_id=1, source_target_pairs={{0,64},{1,65},{2,66},{3,67},{4,68},{5,69},{6,70},{7,71},{8,72},{9,... | collective-permute-start | bytes 98312 | tf_op jit(solution)/shard_map/ppermute | solution.py:219
  67.1 1.3 %collective-permute-done.24 = f32[64,128]{1,0:T(8,128)S(1)} collective-permute-done((f32[64,128]{1,0:T(8,128)S(1)}, f32[64,128]{1,0:T(8,128)S(1)}, u32[]{:S(2)}, u32[]{:S(2)}) %collective-permute-start.24) | collective-permute-done | bytes 32800 | tf_op jit(solution)/shard_map/ppermute | solution.py:219
  70.1 4.2 %collective-permute-start.27 = (f32[64,128]{1,0:T(8,128)S(1)}, f32[64,128]{1,0:T(8,128)S(1)}, u32[]{:S(2)}, u32[]{:S(2)}) collective-permute-start(f32[64,128]{1,0:T(8,128)S(1)} %pad_maximum_fusion.2), channel_id=1, source_target_pairs={{0,30},{1,31},{2,28},{3,29},{4,26},{5,27},{6,24},{7,25},{8,22},{9,... | collective-permute-start | bytes 98312 | tf_op jit(solution)/shard_map/ppermute | solution.py:219
  76.1 1.3 %collective-permute-done.27 = f32[64,128]{1,0:T(8,128)S(1)} collective-permute-done((f32[64,128]{1,0:T(8,128)S(1)}, f32[64,128]{1,0:T(8,128)S(1)}, u32[]{:S(2)}, u32[]{:S(2)}) %collective-permute-start.27) | collective-permute-done | bytes 32800 | tf_op jit(solution)/shard_map/ppermute | solution.py:219
  77.4 2.0 %collective-permute-done.26 = f32[64,128]{1,0:T(8,128)S(1)} collective-permute-done((f32[64,128]{1,0:T(8,128)S(1)}, f32[64,128]{1,0:T(8,128)S(1)}, u32[]{:S(2)}, u32[]{:S(2)}) %collective-permute-start.26) | collective-permute-done | bytes 32800 | tf_op jit(solution)/shard_map/ppermute | solution.py:219
  80.6 4.0 %collective-permute-start.28 = (f32[64,128]{1,0:T(8,128)S(1)}, f32[64,128]{1,0:T(8,128)S(1)}, u32[]{:S(2)}, u32[]{:S(2)}) collective-permute-start(f32[64,128]{1,0:T(8,128)S(1)} %pad_maximum_fusion.3), channel_id=1, source_target_pairs={{0,192},{1,193},{2,194},{3,195},{4,196},{5,197},{6,198},{7,199},{8... | collective-permute-start | bytes 98312 | tf_op jit(solution)/shard_map/ppermute | solution.py:219
  84.6 2.1 %collective-permute-done.28 = f32[64,128]{1,0:T(8,128)S(1)} collective-permute-done((f32[64,128]{1,0:T(8,128)S(1)}, f32[64,128]{1,0:T(8,128)S(1)}, u32[]{:S(2)}, u32[]{:S(2)}) %collective-permute-start.28) | collective-permute-done | bytes 32800 | tf_op jit(solution)/shard_map/ppermute | solution.py:219
  86.7 6.1 %rotate.1 = f32[64,8,256]{2,1,0:T(8,128)} custom-call(f32[64,128]{1,0:T(8,128)S(1)} %pad_maximum_fusion.4.p_ref, bf16[8,256,256]{2,1,0:T(8,128)(2,1)S(1)} %get-tuple-element.44.z_ref), custom_call_target="tpu_custom_call" | custom-call | tf_op jit(solution)/shard_map/rotate/pallas_call | solution.py:349
  (57 shorter events, 22.9 us)
Async XLA Ops:
  1.2 8.1 %collective-permute-start = (f32[17,8,256]{2,1,0:T(8,128)S(1)}, f32[17,8,256]{2,1,0:T(8,128)S(1)}, u32[]{:S(2)}, u32[]{:S(2)}) collective-permute-start(f32[17,8,256]{2,1,0:T(8,128)S(1)} %get-tuple-element.26), channel_id=1, source_target_pairs={{0,8},{1,9},{2,10},{3,11},{4,12},{5,13},{6,14},{7,15},{8,0},{9,1},... | collective-permute-start | bytes 417800 | tf_op jit(solution)/shard_map/ppermute | solution.py:41
  4.5 7.0 %collective-permute-start.1 = (f32[17,8,256]{2,1,0:T(8,128)S(1)}, f32[17,8,256]{2,1,0:T(8,128)S(1)}, u32[]{:S(2)}, u32[]{:S(2)}) collective-permute-start(f32[17,8,256]{2,1,0:T(8,128)S(1)} %get-tuple-element.27), channel_id=1, source_target_pairs={{0,16},{1,17},{2,18},{3,19},{4,20},{5,21},{6,22},{7,23},{8,24},{9,... | collective-permute-start | bytes 417800 | tf_op jit(solution)/shard_map/ppermute | solution.py:41
  5.2 6.6 %collective-permute-start.2 = (f32[17,8,256]{2,1,0:T(8,128)S(1)}, f32[17,8,256]{2,1,0:T(8,128)S(1)}, u32[]{:S(2)}, u32[]{:S(2)}) collective-permute-start(f32[17,8,256]{2,1,0:T(8,128)S(1)} %get-tuple-element.28), channel_id=1, source_target_pairs={{0,24},{1,25},{2,26},{3,27},{4,28},{5,29},{6,30},{7,31},{8,16},{9,... | collective-permute-start | bytes 417800 | tf_op jit(solution)/shard_map/ppermute | solution.py:41
  11.9 11.5 %collective-permute-start.4 = (f32[2,16,16,256]{3,2,1,0:T(8,128)S(1)}, f32[2,16,16,256]{3,2,1,0:T(8,128)S(1)}, u32[]{:S(2)}, u32[]{:S(2)}) collective-permute-start(f32[2,16,16,256]{3,2,1,0:T(8,128)S(1)} %get-tuple-element.29.refs_0_.refs_7_), channel_id=1, source_target_pairs={{0,7},{1,0},{2,1},{3,2},{4,3},{5,4},{6,5},{7,6},{8,15},{9,8},{10,9... | collective-permute-start | bytes 1572872 | tf_op jit(solution)/shard_map/ppermute | solution.py:41
  11.9 11.4 %collective-permute-start.3 = (f32[2,16,16,256]{3,2,1,0:T(8,128)S(1)}, f32[2,16,16,256]{3,2,1,0:T(8,128)S(1)}, u32[]{:S(2)}, u32[]{:S(2)}) collective-permute-start(f32[2,16,16,256]{3,2,1,0:T(8,128)S(1)} %get-tuple-element.29.refs_0_.refs_7_), channel_id=1, source_target_pairs={{0,1},{1,2},{2,3},{3,4},{4,5},{5,6},{6,7},{7,0},{8,9},{9,10},{10,1... | collective-permute-start | bytes 1572872 | tf_op jit(solution)/shard_map/ppermute | solution.py:41
  12.4 6.9 %collective-permute-start.5 = (f32[2,4,16,256]{3,2,1,0:T(8,128)S(1)}, f32[2,4,16,256]{3,2,1,0:T(8,128)S(1)}, u32[]{:S(2)}, u32[]{:S(2)}) collective-permute-start(f32[2,4,16,256]{3,2,1,0:T(8,128)S(1)} %get-tuple-element.30), channel_id=1, source_target_pairs={{0,32},{1,33},{2,34},{3,35},{4,36},{5,37},{6,38},{7,39},{8,40},{9,... | collective-permute-start | bytes 393224 | tf_op jit(solution)/shard_map/ppermute | solution.py:41
  14.3 9.0 %collective-permute-start.6 = (f32[2,4,16,256]{3,2,1,0:T(8,128)S(1)}, f32[2,4,16,256]{3,2,1,0:T(8,128)S(1)}, u32[]{:S(2)}, u32[]{:S(2)}) collective-permute-start(f32[2,4,16,256]{3,2,1,0:T(8,128)S(1)} %get-tuple-element.31), channel_id=1, source_target_pairs={{0,224},{1,225},{2,226},{3,227},{4,228},{5,229},{6,230},{7,231},{8... | collective-permute-start | bytes 393224 | tf_op jit(solution)/shard_map/ppermute | solution.py:41
  24.3 7.5 %collective-permute-start.8 = (f32[2,16,16,256]{3,2,1,0:T(8,128)S(1)}, f32[2,16,16,256]{3,2,1,0:T(8,128)S(1)}, u32[]{:S(2)}, u32[]{:S(2)}) collective-permute-start(f32[2,16,16,256]{3,2,1,0:T(8,128)S(1)} %get-tuple-element.33.refs_0_.refs_7_), channel_id=1, source_target_pairs={{0,7},{1,0},{2,1},{3,2},{4,3},{5,4},{6,5},{7,6},{8,15},{9,8},{10,9... | collective-permute-start | bytes 1572872 | tf_op jit(solution)/shard_map/ppermute | solution.py:41
  24.9 8.6 %collective-permute-start.7 = (f32[2,16,16,256]{3,2,1,0:T(8,128)S(1)}, f32[2,16,16,256]{3,2,1,0:T(8,128)S(1)}, u32[]{:S(2)}, u32[]{:S(2)}) collective-permute-start(f32[2,16,16,256]{3,2,1,0:T(8,128)S(1)} %get-tuple-element.33.refs_0_.refs_7_), channel_id=1, source_target_pairs={{0,1},{1,2},{2,3},{3,4},{4,5},{5,6},{6,7},{7,0},{8,9},{9,10},{10,1... | collective-permute-start | bytes 1572872 | tf_op jit(solution)/shard_map/ppermute | solution.py:41
  24.9 5.0 %collective-permute-start.9 = (f32[2,4,16,256]{3,2,1,0:T(8,128)S(1)}, f32[2,4,16,256]{3,2,1,0:T(8,128)S(1)}, u32[]{:S(2)}, u32[]{:S(2)}) collective-permute-start(f32[2,4,16,256]{3,2,1,0:T(8,128)S(1)} %get-tuple-element.34), channel_id=1, source_target_pairs={{0,32},{1,33},{2,34},{3,35},{4,36},{5,37},{6,38},{7,39},{8,40},{9,... | collective-permute-start | bytes 393224 | tf_op jit(solution)/shard_map/ppermute | solution.py:41
  24.9 7.0 %collective-permute-start.10 = (f32[2,4,16,256]{3,2,1,0:T(8,128)S(1)}, f32[2,4,16,256]{3,2,1,0:T(8,128)S(1)}, u32[]{:S(2)}, u32[]{:S(2)}) collective-permute-start(f32[2,4,16,256]{3,2,1,0:T(8,128)S(1)} %get-tuple-element.35), channel_id=1, source_target_pairs={{0,224},{1,225},{2,226},{3,227},{4,228},{5,229},{6,230},{7,231},{8... | collective-permute-start | bytes 393224 | tf_op jit(solution)/shard_map/ppermute | solution.py:41
  34.5 7.8 %collective-permute-start.12 = (f32[2,16,16,256]{3,2,1,0:T(8,128)S(1)}, f32[2,16,16,256]{3,2,1,0:T(8,128)S(1)}, u32[]{:S(2)}, u32[]{:S(2)}) collective-permute-start(f32[2,16,16,256]{3,2,1,0:T(8,128)S(1)} %get-tuple-element.36.refs_0_), channel_id=1, source_target_pairs={{0,7},{1,0},{2,1},{3,2},{4,3},{5,4},{6,5},{7,6},{8,15},{9,8},{10,9... | collective-permute-start | bytes 1572872 | tf_op jit(solution)/shard_map/ppermute | solution.py:41
  34.8 8.6 %collective-permute-start.11 = (f32[2,16,16,256]{3,2,1,0:T(8,128)S(1)}, f32[2,16,16,256]{3,2,1,0:T(8,128)S(1)}, u32[]{:S(2)}, u32[]{:S(2)}) collective-permute-start(f32[2,16,16,256]{3,2,1,0:T(8,128)S(1)} %get-tuple-element.36.refs_0_), channel_id=1, source_target_pairs={{0,1},{1,2},{2,3},{3,4},{4,5},{5,6},{6,7},{7,0},{8,9},{9,10},{10,1... | collective-permute-start | bytes 1572872 | tf_op jit(solution)/shard_map/ppermute | solution.py:41
  35.3 5.0 %collective-permute-start.13 = (f32[2,4,16,256]{3,2,1,0:T(8,128)S(1)}, f32[2,4,16,256]{3,2,1,0:T(8,128)S(1)}, u32[]{:S(2)}, u32[]{:S(2)}) collective-permute-start(f32[2,4,16,256]{3,2,1,0:T(8,128)S(1)} %get-tuple-element.37), channel_id=1, source_target_pairs={{0,32},{1,33},{2,34},{3,35},{4,36},{5,37},{6,38},{7,39},{8,40},{9,... | collective-permute-start | bytes 393224 | tf_op jit(solution)/shard_map/ppermute | solution.py:41
  35.3 7.0 %collective-permute-start.14 = (f32[2,4,16,256]{3,2,1,0:T(8,128)S(1)}, f32[2,4,16,256]{3,2,1,0:T(8,128)S(1)}, u32[]{:S(2)}, u32[]{:S(2)}) collective-permute-start(f32[2,4,16,256]{3,2,1,0:T(8,128)S(1)} %get-tuple-element.38), channel_id=1, source_target_pairs={{0,224},{1,225},{2,226},{3,227},{4,228},{5,229},{6,230},{7,231},{8... | collective-permute-start | bytes 393224 | tf_op jit(solution)/shard_map/ppermute | solution.py:41
  44.0 7.3 %collective-permute-start.15 = (f32[8,16,256]{2,1,0:T(8,128)S(1)}, f32[8,16,256]{2,1,0:T(8,128)S(1)}, u32[]{:S(2)}, u32[]{:S(2)}) collective-permute-start(f32[8,16,256]{2,1,0:T(8,128)S(1)} %get-tuple-element.40), channel_id=1, source_target_pairs={{0,8},{1,9},{2,10},{3,11},{4,12},{5,13},{6,14},{7,15},{8,0},{9,1},... | collective-permute-start | bytes 393224 | tf_op jit(solution)/shard_map/ppermute | solution.py:41
  46.7 8.0 %collective-permute-start.17 = (f32[8,16,256]{2,1,0:T(8,128)S(1)}, f32[8,16,256]{2,1,0:T(8,128)S(1)}, u32[]{:S(2)}, u32[]{:S(2)}) collective-permute-start(f32[8,16,256]{2,1,0:T(8,128)S(1)} %get-tuple-element.42), channel_id=1, source_target_pairs={{0,24},{1,25},{2,26},{3,27},{4,28},{5,29},{6,30},{7,31},{8,16},{9,... | collective-permute-start | bytes 393224 | tf_op jit(solution)/shard_map/ppermute | solution.py:41
  48.5 6.3 %collective-permute-start.16 = (f32[8,16,256]{2,1,0:T(8,128)S(1)}, f32[8,16,256]{2,1,0:T(8,128)S(1)}, u32[]{:S(2)}, u32[]{:S(2)}) collective-permute-start(f32[8,16,256]{2,1,0:T(8,128)S(1)} %get-tuple-element.41), channel_id=1, source_target_pairs={{0,16},{1,17},{2,18},{3,19},{4,20},{5,21},{6,22},{7,23},{8,24},{9,... | collective-permute-start | bytes 393224 | tf_op jit(solution)/shard_map/ppermute | solution.py:41
  57.1 4.9 %collective-permute-start.21 = (f32[64,128]{1,0:T(8,128)S(1)}, f32[64,128]{1,0:T(8,128)S(1)}, u32[]{:S(2)}, u32[]{:S(2)}) collective-permute-start(f32[64,128]{1,0:T(8,128)S(1)} %pad_maximum_fusion), channel_id=1, source_target_pairs={{0,34},{1,35},{2,32},{3,33},{4,38},{5,39},{6,36},{7,37},{8,42},{9,... | collective-permute-start | bytes 98312 | tf_op jit(solution)/shard_map/ppermute | solution.py:219
  62.6 5.8 %collective-permute-start.24 = (f32[64,128]{1,0:T(8,128)S(1)}, f32[64,128]{1,0:T(8,128)S(1)}, u32[]{:S(2)}, u32[]{:S(2)}) collective-permute-start(f32[64,128]{1,0:T(8,128)S(1)} %pad_maximum_fusion.1), channel_id=1, source_target_pairs={{0,80},{1,81},{2,82},{3,83},{4,84},{5,85},{6,86},{7,87},{8,88},{9,... | collective-permute-start | bytes 98312 | tf_op jit(solution)/shard_map/ppermute | solution.py:219
  70.1 7.3 %collective-permute-start.27 = (f32[64,128]{1,0:T(8,128)S(1)}, f32[64,128]{1,0:T(8,128)S(1)}, u32[]{:S(2)}, u32[]{:S(2)}) collective-permute-start(f32[64,128]{1,0:T(8,128)S(1)} %pad_maximum_fusion.2), channel_id=1, source_target_pairs={{0,30},{1,31},{2,28},{3,29},{4,26},{5,27},{6,24},{7,25},{8,22},{9,... | collective-permute-start | bytes 98312 | tf_op jit(solution)/shard_map/ppermute | solution.py:219
  74.3 5.1 %collective-permute-start.26 = (f32[64,128]{1,0:T(8,128)S(1)}, f32[64,128]{1,0:T(8,128)S(1)}, u32[]{:S(2)}, u32[]{:S(2)}) collective-permute-start(f32[64,128]{1,0:T(8,128)S(1)} %pad_maximum_fusion.2), channel_id=1, source_target_pairs={{0,24},{1,25},{2,26},{3,27},{4,28},{5,29},{6,30},{7,31},{8,16},{9,... | collective-permute-start | bytes 98312 | tf_op jit(solution)/shard_map/ppermute | solution.py:219
  75.4 5.1 %collective-permute-start.25 = (f32[64,128]{1,0:T(8,128)S(1)}, f32[64,128]{1,0:T(8,128)S(1)}, u32[]{:S(2)}, u32[]{:S(2)}) collective-permute-start(f32[64,128]{1,0:T(8,128)S(1)} %pad_maximum_fusion.2), channel_id=1, source_target_pairs={{0,6},{1,7},{2,4},{3,5},{4,2},{5,3},{6,0},{7,1},{8,14},{9,15},{10,... | collective-permute-start | bytes 98312 | tf_op jit(solution)/shard_map/ppermute | solution.py:219
  80.6 6.1 %collective-permute-start.28 = (f32[64,128]{1,0:T(8,128)S(1)}, f32[64,128]{1,0:T(8,128)S(1)}, u32[]{:S(2)}, u32[]{:S(2)}) collective-permute-start(f32[64,128]{1,0:T(8,128)S(1)} %pad_maximum_fusion.3), channel_id=1, source_target_pairs={{0,192},{1,193},{2,194},{3,195},{4,196},{5,197},{6,198},{7,199},{8... | collective-permute-start | bytes 98312 | tf_op jit(solution)/shard_map/ppermute | solution.py:219
  (6 other events, 41.3 us)
